TPU v7x, 32 devices: a whole 2x2x4 slice. The times are simulated.
32 devices in a mesh: base: 8 (over z, x), tm: 4 (over y, core).
Axes of the slice: x: 2, y: 2, z: 4, core: 2. Of those that a mesh axis runs over, the one named last changes fastest.
Arguments:
- visibilities: bfloat16 [4, 1024, 2, 256], P('tm', 'base'), may hold values from -6 to 6
- coords: float32 [4, 1024, 2, 256], P('tm', 'base'), may hold values from -16 to 16
- counts: int32 [4, 1024], P('tm', 'base'), may hold values from 1 to 256, 157286 in all within a row
- stations: int32 [1024, 2], P('base'), may hold values from 0 to 31
- owners: int32 [1024, 1], replicated, may hold values from 0 to 7; in each aligned block of 128 rows (0 to 127, 128 to 255, ...) at most 24 rows name the same one
- offsets: int32 [1024, 2], replicated, may hold values from 0 to 224
- screens: bfloat16 [32, 2, 1024], P('base'), may hold values from -4 to 4
Outputs:
- grid_tiles: float32 [8, 256, 2, 256], P('base', 'tm')
Inputs may be any that keep to these rules, and one draw needn't show every extreme that they name: `counts`: in each time block some subgrid uses all 256 slots. `owners`: among the 128 subgrids of one index of base no tile is named more than 24 times, a bound that some block reaches.
All inputs are finite; a program needn't handle non-finite values.
Results may differ from a plain program's by a relative error of at most 0.023.
Values may be sent and summed in bfloat16 or wider, within the bound.
No kernel may reach another device: no remote copies, remote signals or barrier semaphores. Data moves between devices by JAX's collectives and lax.ppermute only.
A program may use at most 64 MiB of HBM per device.

v0:
```python
import math

import jax
import jax.numpy as jnp
from jax import lax
from jax.sharding import PartitionSpec as P

SUB = 32
TILE = 256


def taper_line(side):
    points = jnp.arange(side, dtype=jnp.float32)
    scaled = (points + 0.5 - side / 2.0) / (side / 2.0)
    return 1.0 - scaled * scaled


def fourier_tables(side):
    index_ids = jnp.arange(side, dtype=jnp.int32)
    turn_ids = index_ids[:, None] * index_ids[None, :] % side
    angles = turn_ids.astype(jnp.float32) * (2.0 * math.pi / side)
    return (jnp.cos(angles), jnp.sin(angles))


def transform(real_part, imag_part, left_cos, left_sin, right_cos, right_sin):
    highest = lax.Precision.HIGHEST
    mid_real = jnp.einsum("sml,jl->smj", real_part, right_cos, precision=highest) + jnp.einsum(
        "sml,jl->smj", imag_part, right_sin, precision=highest
    )
    mid_imag = jnp.einsum("sml,jl->smj", imag_part, right_cos, precision=highest) - jnp.einsum(
        "sml,jl->smj", real_part, right_sin, precision=highest
    )
    out_real = jnp.einsum("km,smj->skj", left_cos, mid_real, precision=highest) + jnp.einsum(
        "km,smj->skj", left_sin, mid_imag, precision=highest
    )
    out_imag = jnp.einsum("km,smj->skj", left_cos, mid_imag, precision=highest) - jnp.einsum(
        "km,smj->skj", left_sin, mid_real, precision=highest
    )
    return (out_real, out_imag)


def block_images(visibilities, coords, counts, side):
    slot_count = visibilities.shape[-1]
    positions = jnp.arange(side, dtype=jnp.float32) - side / 2.0
    phase_step = 2.0 * math.pi / side
    angle_u = coords[:, 0, None, :] * positions[:, None] * phase_step
    table_u = jnp.concatenate([jnp.cos(angle_u), jnp.sin(angle_u)], axis=1).astype(jnp.bfloat16)
    in_count = (jnp.arange(slot_count, dtype=jnp.int32) < counts[:, None]).astype(jnp.float32)
    weight_real = visibilities[:, 0, :].astype(jnp.float32) * in_count
    weight_imag = visibilities[:, 1, :].astype(jnp.float32) * in_count
    angle_v = coords[:, 1, None, :] * positions[:, None] * phase_step
    cosine_v = jnp.cos(angle_v)
    sine_v = jnp.sin(angle_v)
    wave_real = weight_real[:, None, :] * cosine_v - weight_imag[:, None, :] * sine_v
    wave_imag = weight_real[:, None, :] * sine_v + weight_imag[:, None, :] * cosine_v
    table_v = jnp.concatenate([wave_real, wave_imag], axis=1).astype(jnp.bfloat16)
    products = jnp.einsum("smv,slv->sml", table_v, table_u, preferred_element_type=jnp.float32)
    real_part = products[:, :side, :side] - products[:, side:, side:]
    imag_part = products[:, :side, side:] + products[:, side:, :side]
    norm_factor = 1.0 / math.sqrt(slot_count)
    return (jnp.stack([real_part, imag_part], axis=1) * norm_factor).astype(jnp.bfloat16)


def make_lookup(pairs):

    def lookup(picked, shard_rows, first_id):
        row_total = shard_rows.shape[0]
        inside = (pairs >= 0) & (pairs < row_total)
        safe_ids = jnp.clip(pairs, 0, row_total - 1)
        first_new = jnp.where(inside[:, 0, None, None], shard_rows[safe_ids[:, 0]], picked[0])
        second_new = jnp.where(inside[:, 1, None, None], shard_rows[safe_ids[:, 1]], picked[1])
        return (first_new, second_new)

    return lookup


def gain_apply(summed, first_side, second_side, row_total, side):
    local_count = summed.shape[0]
    first_real = first_side[:, 0].astype(jnp.float32)
    first_imag = first_side[:, 1].astype(jnp.float32)
    second_real = second_side[:, 0].astype(jnp.float32)
    second_imag = second_side[:, 1].astype(jnp.float32)
    gain_real = first_real * second_real + first_imag * second_imag
    gain_imag = first_real * second_imag - first_imag * second_real
    taper_full = taper_line(side)
    window = (taper_full[:, None] * taper_full[None, :]).reshape(row_total * side)
    x_real = (summed[:, 0] * gain_real - summed[:, 1] * gain_imag) * window
    x_imag = (summed[:, 0] * gain_imag + summed[:, 1] * gain_real) * window
    return (
        x_real.reshape(local_count, row_total, side),
        x_imag.reshape(local_count, row_total, side),
    )


def per_device(visibilities, coords, counts, stations, owners, offsets, screens):
    local_count = visibilities.shape[1]
    side = SUB
    pixels = side * side
    tm_count = lax.axis_size("tm")
    base_count = lax.axis_size("base")
    tm_index = lax.axis_index("tm")
    base_index = lax.axis_index("base")
    share = pixels // tm_count
    row_share = side // tm_count
    per_map = math.gcd(local_count, 16)

    def one_block(block_id):
        first_row = block_id * per_map
        vis_part = lax.dynamic_slice_in_dim(visibilities[0], first_row, per_map, 0)
        coord_part = lax.dynamic_slice_in_dim(coords[0], first_row, per_map, 0)
        count_part = lax.dynamic_slice_in_dim(counts[0], first_row, per_map, 0)
        return block_images(vis_part, coord_part, count_part, side)

    time_images = lax.map(one_block, jnp.arange(local_count // per_map, dtype=jnp.int32))
    time_images = time_images.reshape(local_count, 2, pixels).astype(jnp.float32)
    cos_table, sin_table = fourier_tables(side)
    lookup = make_lookup(stations)
    summed = lax.psum(time_images.astype(jnp.bfloat16), "tm").astype(jnp.float32)
    empty_side = jnp.zeros((local_count, 2, pixels), jnp.bfloat16)
    first_side, second_side = lookup(
        (empty_side, empty_side), lax.all_gather(screens, "base", axis=0, tiled=True), jnp.int32(0)
    )
    x_real, x_imag = gain_apply(summed, first_side, second_side, side, side)
    left_cos = lax.dynamic_slice_in_dim(cos_table, tm_index * row_share, row_share, 0)
    left_sin = lax.dynamic_slice_in_dim(sin_table, tm_index * row_share, row_share, 0)
    out_real, out_imag = transform(x_real, x_imag, left_cos, left_sin, cos_table, sin_table)
    pieces = (
        (jnp.stack([out_real, out_imag], axis=1) / side)
        .astype(jnp.bfloat16)
        .reshape(local_count, 2, share)
    )
    capacity = max(2, 3 * local_count // (2 * base_count))
    slot_total = base_count * capacity
    tile_ids = jnp.arange(base_count, dtype=jnp.int32)
    my_owners = lax.dynamic_slice_in_dim(owners[:, 0], base_index * local_count, local_count, 0)
    owner_hits = (my_owners[:, None] == tile_ids[None, :]).astype(jnp.int32)
    earlier = jnp.cumsum(owner_hits, axis=0) - owner_hits
    rank_ids = jnp.sum(earlier * owner_hits, axis=1)
    slot_ids = my_owners * capacity + rank_ids
    slot_range = jnp.arange(slot_total, dtype=jnp.int32)
    send_table = (slot_range[:, None] == slot_ids[None, :]).astype(jnp.bfloat16)
    outgoing = jnp.dot(
        send_table, pieces.reshape(local_count, 2 * share), preferred_element_type=jnp.float32
    )
    outgoing = outgoing.astype(jnp.bfloat16).reshape(slot_total, 2, share)
    incoming = lax.all_to_all(outgoing, "base", split_axis=0, concat_axis=0, tiled=True)
    is_mine = (owners[:, 0] == base_index).astype(jnp.int32).reshape(base_count, local_count)
    before = jnp.cumsum(is_mine, axis=1) - is_mine
    rank_range = jnp.arange(capacity, dtype=jnp.int32)
    chosen = (is_mine[:, None, :] > 0) & (before[:, None, :] == rank_range[None, :, None])
    local_range = jnp.arange(local_count, dtype=jnp.int32)
    source_ids = (
        jnp.sum(jnp.where(chosen, local_range[None, None, :], 0), axis=2)
        + tile_ids[:, None] * local_count
    )
    filled = jnp.any(chosen, axis=2).astype(jnp.int32).reshape(slot_total)
    slot_offsets = offsets[source_ids.reshape(slot_total)] * filled[:, None]
    row_starts = slot_offsets[:, 0] + tm_index * row_share
    tile_range = jnp.arange(TILE, dtype=jnp.int32)
    share_range = jnp.arange(row_share, dtype=jnp.int32)
    cell_range = jnp.arange(side, dtype=jnp.int32)
    row_place = (
        tile_range[None, :, None] == row_starts[:, None, None] + share_range[None, None, :]
    ).astype(jnp.bfloat16)
    col_place = (
        tile_range[None, None, :] == slot_offsets[:, 1, None, None] + cell_range[None, :, None]
    ).astype(jnp.bfloat16)
    values = incoming.reshape(slot_total, 2, row_share, side)
    spread = jnp.einsum(
        "scab,sbq->scaq", values, col_place, preferred_element_type=jnp.float32
    ).astype(jnp.bfloat16)
    tile_sum = jnp.einsum("sra,scaq->rcq", row_place, spread, preferred_element_type=jnp.float32)
    own_tile = lax.psum_scatter(
        tile_sum.astype(jnp.bfloat16), "tm", scatter_dimension=0, tiled=True
    ).astype(jnp.float32)
    return own_tile[None]


def solution(mesh):
    return jax.shard_map(
        per_device,
        mesh=mesh,
        in_specs=(
            P("tm", "base", None, None),
            P("tm", "base", None, None),
            P("tm", "base"),
            P("base", None),
            P(),
            P(),
            P("base", None, None),
        ),
        out_specs=P("base", "tm", None, None),
        check_vma=False,
    )
```

profile of v0, /device:TPU:0, one launch (start us, length us, event | category | flops | bytes accessed | tf_op | source)
XLA Modules:
  0.0 169.5 jit_solution(6895000689914638842)
XLA Ops:
  6.5 67.7 %while.12 = (s32[]{:T(128)}, bf16[8,16,2,32,32]{4,3,1,0,2:T(8,128)(2,1)S(1)}, s32[8]{0:T(128)S(1)}, s32[1,128]{1,0:T(1,128)}, bf16[1,128,2,256]{3,2,1,0:T(2,128)...) while((s32[]{:T(128)}, ...), condition=%wide.region_6.7_spmd, body=%wide.region_5.6_spmd.sunk | while | flops 37638180 | bytes 3916407 | solution.py:114
  7.9 0.8 constant_dynamic-slice_fusion.6
  8.7 0.7 constant_dynamic-slice_fusion.7
  9.4 0.7 fusion.121
  10.2 4.2 %cosine_convert_fusion.2 = (bf16[16,32,256]{2,1,0:T(8,128)(2,1)S(1)}, bf16[16,32,256]{2,1,0:T(8,128)(2,1)S(1)}, bf16[16,32,256]{2,1,0:T(8,128)(2,1)S(1)}, bf16[16,32,256]{2,1,0:T(8,128)(2,1)S(1)}) fusion(f32[16,256]{1,0:T(8,128)S(1)} %get-tuple-element.202, f32[32]{0:T(128)S(1)} %iota_add_fusion.4, f32[16,256]{1,0:T(8,128)S(1)} %get-tuple-element.203, ...), kind=kLoop, calls=%fused_computation.13.clone.1 | loop fusion | flops 1835008 | bytes 1114240 | tf_op jit(solution)/shard_map/convert
  16.4 0.8 constant_dynamic-slice_fusion.6
  17.1 0.7 constant_dynamic-slice_fusion.7
  17.9 0.7 fusion.121
  18.7 4.2 %cosine_convert_fusion.2 = (bf16[16,32,256]{2,1,0:T(8,128)(2,1)S(1)}, bf16[16,32,256]{2,1,0:T(8,128)(2,1)S(1)}, bf16[16,32,256]{2,1,0:T(8,128)(2,1)S(1)}, bf16[16,32,256]{2,1,0:T(8,128)(2,1)S(1)}) fusion(f32[16,256]{1,0:T(8,128)S(1)} %get-tuple-element.202, f32[32]{0:T(128)S(1)} %iota_add_fusion.4, f32[16,256]{1,0:T(8,128)S(1)} %get-tuple-element.203, ...), kind=kLoop, calls=%fused_computation.13.clone.1 | loop fusion | flops 1835008 | bytes 1114240 | tf_op jit(solution)/shard_map/convert
  24.8 0.8 constant_dynamic-slice_fusion.6
  25.6 0.7 constant_dynamic-slice_fusion.7
  26.4 0.7 fusion.121
  27.2 4.2 %cosine_convert_fusion.2 = (bf16[16,32,256]{2,1,0:T(8,128)(2,1)S(1)}, bf16[16,32,256]{2,1,0:T(8,128)(2,1)S(1)}, bf16[16,32,256]{2,1,0:T(8,128)(2,1)S(1)}, bf16[16,32,256]{2,1,0:T(8,128)(2,1)S(1)}) fusion(f32[16,256]{1,0:T(8,128)S(1)} %get-tuple-element.202, f32[32]{0:T(128)S(1)} %iota_add_fusion.4, f32[16,256]{1,0:T(8,128)S(1)} %get-tuple-element.203, ...), kind=kLoop, calls=%fused_computation.13.clone.1 | loop fusion | flops 1835008 | bytes 1114240 | tf_op jit(solution)/shard_map/convert
  33.3 0.8 constant_dynamic-slice_fusion.6
  34.1 0.7 constant_dynamic-slice_fusion.7
  34.8 0.7 fusion.121
  35.6 4.2 %cosine_convert_fusion.2 = (bf16[16,32,256]{2,1,0:T(8,128)(2,1)S(1)}, bf16[16,32,256]{2,1,0:T(8,128)(2,1)S(1)}, bf16[16,32,256]{2,1,0:T(8,128)(2,1)S(1)}, bf16[16,32,256]{2,1,0:T(8,128)(2,1)S(1)}) fusion(f32[16,256]{1,0:T(8,128)S(1)} %get-tuple-element.202, f32[32]{0:T(128)S(1)} %iota_add_fusion.4, f32[16,256]{1,0:T(8,128)S(1)} %get-tuple-element.203, ...), kind=kLoop, calls=%fused_computation.13.clone.1 | loop fusion | flops 1835008 | bytes 1114240 | tf_op jit(solution)/shard_map/convert
  41.8 0.8 constant_dynamic-slice_fusion.6
  42.5 0.7 constant_dynamic-slice_fusion.7
  43.3 0.7 fusion.121
  44.1 4.2 %cosine_convert_fusion.2 = (bf16[16,32,256]{2,1,0:T(8,128)(2,1)S(1)}, bf16[16,32,256]{2,1,0:T(8,128)(2,1)S(1)}, bf16[16,32,256]{2,1,0:T(8,128)(2,1)S(1)}, bf16[16,32,256]{2,1,0:T(8,128)(2,1)S(1)}) fusion(f32[16,256]{1,0:T(8,128)S(1)} %get-tuple-element.202, f32[32]{0:T(128)S(1)} %iota_add_fusion.4, f32[16,256]{1,0:T(8,128)S(1)} %get-tuple-element.203, ...), kind=kLoop, calls=%fused_computation.13.clone.1 | loop fusion | flops 1835008 | bytes 1114240 | tf_op jit(solution)/shard_map/convert
  50.2 0.8 constant_dynamic-slice_fusion.6
  51.0 0.7 constant_dynamic-slice_fusion.7
  51.7 0.7 fusion.121
  52.6 4.2 %cosine_convert_fusion.2 = (bf16[16,32,256]{2,1,0:T(8,128)(2,1)S(1)}, bf16[16,32,256]{2,1,0:T(8,128)(2,1)S(1)}, bf16[16,32,256]{2,1,0:T(8,128)(2,1)S(1)}, bf16[16,32,256]{2,1,0:T(8,128)(2,1)S(1)}) fusion(f32[16,256]{1,0:T(8,128)S(1)} %get-tuple-element.202, f32[32]{0:T(128)S(1)} %iota_add_fusion.4, f32[16,256]{1,0:T(8,128)S(1)} %get-tuple-element.203, ...), kind=kLoop, calls=%fused_computation.13.clone.1 | loop fusion | flops 1835008 | bytes 1114240 | tf_op jit(solution)/shard_map/convert
  58.7 0.8 constant_dynamic-slice_fusion.6
  59.5 0.7 constant_dynamic-slice_fusion.7
  60.2 0.7 fusion.121
  61.0 4.2 %cosine_convert_fusion.2 = (bf16[16,32,256]{2,1,0:T(8,128)(2,1)S(1)}, bf16[16,32,256]{2,1,0:T(8,128)(2,1)S(1)}, bf16[16,32,256]{2,1,0:T(8,128)(2,1)S(1)}, bf16[16,32,256]{2,1,0:T(8,128)(2,1)S(1)}) fusion(f32[16,256]{1,0:T(8,128)S(1)} %get-tuple-element.202, f32[32]{0:T(128)S(1)} %iota_add_fusion.4, f32[16,256]{1,0:T(8,128)S(1)} %get-tuple-element.203, ...), kind=kLoop, calls=%fused_computation.13.clone.1 | loop fusion | flops 1835008 | bytes 1114240 | tf_op jit(solution)/shard_map/convert
  67.2 0.8 constant_dynamic-slice_fusion.6
  67.9 0.7 constant_dynamic-slice_fusion.7
  68.7 0.7 fusion.121
  69.5 4.2 %cosine_convert_fusion.2 = (bf16[16,32,256]{2,1,0:T(8,128)(2,1)S(1)}, bf16[16,32,256]{2,1,0:T(8,128)(2,1)S(1)}, bf16[16,32,256]{2,1,0:T(8,128)(2,1)S(1)}, bf16[16,32,256]{2,1,0:T(8,128)(2,1)S(1)}) fusion(f32[16,256]{1,0:T(8,128)S(1)} %get-tuple-element.202, f32[32]{0:T(128)S(1)} %iota_add_fusion.4, f32[16,256]{1,0:T(8,128)S(1)} %get-tuple-element.203, ...), kind=kLoop, calls=%fused_computation.13.clone.1 | loop fusion | flops 1835008 | bytes 1114240 | tf_op jit(solution)/shard_map/convert
  74.3 2.9 %reshape.325 = bf16[128,2,1024]{2,0,1:T(8,128)(2,1)} reshape(bf16[8,16,2,32,32]{4,3,1,0,2:T(8,128)(2,1)S(1)} %get-tuple-element.82) | data formatting | bytes 1048576 | tf_op jit(solution)/shard_map/reshape | solution.py:115
  78.2 32.5 %all_gather.3 = bf16[32,2,1024]{2,1,0:T(2,128)(2,1)S(1)} all-gather(bf16[4,2,1024]{2,1,0:T(2,128)(2,1)S(1)} %copy-done), channel_id=1, replica_groups=mesh['base'=8,'tm'=4] {'base'}, dimensions={0}, use_global_device_ids=true | all-gather | bytes 147456 | tf_op jit(solution)/shard_map/all_gather | solution.py:121
  111.7 1.6 gather_fusion.2
  113.5 0.7 gather_fusion
  114.6 1.6 gather_fusion.1
  116.4 1.1 convert_element_type.135
  118.2 0.7 fusion.48
  124.0 0.7 reshape.326
  124.7 5.5 %all-to-all-start = ((bf16[192,2,256]{2,1,0:T(2,128)(2,1)}), bf16[192,2,256]{2,1,0:T(2,128)(2,1)S(1)}, u32[]{:S(2)}, u32[]{:S(2)}) async-start(bf16[192,2,256]{2,1,0:T(2,128)(2,1)} %reshape.326), calls=%async_computation | async-start | bytes 393216 | tf_op jit(solution)/shard_map/all_to_all | solution.py:146
  130.6 7.4 %all-to-all-done = bf16[192,2,256]{2,1,0:T(2,128)(2,1)S(1)} async-done(((bf16[192,2,256]{2,1,0:T(2,128)(2,1)}), bf16[192,2,256]{2,1,0:T(2,128)(2,1)S(1)}, u32[]{:S(2)}, u32[]{:S(2)}) %all-to-all-start) | async-done | bytes 196640 | tf_op jit(solution)/shard_map/all_to_all | solution.py:146
  138.9 1.8 %fusion.20 = bf16[192,2,8,256]{3,2,1,0:T(8,128)(2,1)S(1)} fusion(bf16[192,2,8,32]{3,2,1,0:T(8,128)(2,1)S(1)} %copy.93, s32[192,32]{1,0:T(8,128)S(1)} %iota_add_fusion.1), kind=kOutput, calls=%fused_computation.43 | convolution fusion | flops 52690944 | bytes 1794048 | tf_op jit(solution)/shard_map/scab,sbq->scaq/dot_general | solution.py:169
  140.6 2.1 %fusion.32 = bf16[256,2,256]{2,0,1:T(8,128)(2,1)} fusion(bf16[192,2,8,256]{3,2,1,0:T(8,128)(2,1)S(1)} %fusion.20, s32[192,8]{0,1:T(8,128)S(1)} %iota_add_fusion.2), kind=kOutput, calls=%fused_computation.51 | convolution fusion | flops 403177472 | bytes 1841152 | tf_op jit(solution)/shard_map/sra,scaq->rcq/dot_general | solution.py:172
  142.8 18.2 %reduce-scatter.2.cloned.1.call-done = bf16[64,2,256]{2,0,1:T(8,128)(2,1)} async-done(((bf16[256,2,256]{2,0,1:T(8,128)(2,1)}), bf16[64,2,256]{2,0,1:T(8,128)(2,1)}) %reduce-scatter.2.cloned.1.call-update) | async-done | bytes 65552 | tf_op jit(solution)/shard_map/reduce_scatter | solution.py:173
  161.0 0.8 bitcast_convert_fusion
  161.9 0.8 copy.95
  (128 shorter events, 20.1 us)
Async XLA Ops:
  6.5 109.8 %all-reduce.2.cloned.1.call-start = ((), (), s32[]{:S(2)}) async-start(), calls=%async_computation.2 | async-start | bytes 1048576 | tf_op jit(solution)/shard_map/psum | solution.py:118
  74.3 3.0 %copy-start.3 = (s32[128,2]{0,1:T(2,128)S(1)}, s32[128,2]{0,1:T(2,128)}, u32[]{:S(2)}) copy-start(s32[128,2]{0,1:T(2,128)} %param.12) | copy-start | bytes 3076
  74.3 3.1 %copy-start.2 = (s32[1024,1]{0,1:T(1,128)S(1)}, s32[1024,1]{0,1:T(1,128)}, u32[]{:S(2)}) copy-start(s32[1024,1]{0,1:T(1,128)} %param.13) | copy-start | bytes 12292
  74.3 3.9 %copy-start = (bf16[4,2,1024]{2,1,0:T(2,128)(2,1)S(1)}, bf16[4,2,1024]{2,1,0:T(2,128)(2,1)}, u32[]{:S(2)}) copy-start(bf16[4,2,1024]{2,1,0:T(2,128)(2,1)} %param.15) | copy-start | bytes 49156
  74.3 36.9 %copy-start.1 = (s32[1024,2]{0,1:T(2,128)S(1)}, s32[1024,2]{0,1:T(2,128)}, u32[]{:S(2)}) copy-start(s32[1024,2]{0,1:T(2,128)} %param.14) | copy-start | bytes 24580
  124.7 13.3 %all-to-all-start = ((bf16[192,2,256]{2,1,0:T(2,128)(2,1)}), bf16[192,2,256]{2,1,0:T(2,128)(2,1)S(1)}, u32[]{:S(2)}, u32[]{:S(2)}) async-start(bf16[192,2,256]{2,1,0:T(2,128)(2,1)} %reshape.326), calls=%async_computation | async-start | bytes 393216 | tf_op jit(solution)/shard_map/all_to_all | solution.py:146
  130.2 30.8 %reduce-scatter.2.cloned.1.call-start = ((), (), s32[]{:S(2)}) async-start(), calls=%async_computation.3 | async-start | bytes 327680 | tf_op jit(solution)/shard_map/reduce_scatter | solution.py:173
Sparse Core Ops, SparseCore 0:
  77.4 35.8 all-reduce.1
  142.9 18.0 reduce-scatter.1
where the time goes:
time: 171 us; the launch traced here: 169 us
  other arithmetic  40.7 us (24%)
  local copies, waits for them, and re-layouts  33.3 us (19%)
  blocking collectives  32.5 us (19%)
  waiting for transfers between devices  25.7 us (15%)
  between operations  13.8 us (8%)
  matrix products  11.8 us (7%)
  loops' own time  5.97 us (3%)
  starting transfers between devices  5.75 us (3%)
    another operation x8, other arithmetic  33.3 us
    all_gather x1, blocking collectives, per_device(): lax.all_gather(screens, 'base', axis=0, tiled=True)  32.5 us
    reduce_scatter x1, waiting for transfers between devices, per_device(): lax.psum_scatter(tile_sum.astype(jnp.bfloat16), 'tm', scatter_dimension=0...  18.2 us
    all_to_all x1, waiting for transfers between devices, per_device(): lax.all_to_all(outgoing, 'base', split_axis=0, concat_axis=0, tiled=True)  7.41 us
    dynamic_slice x16, local copies, waits for them, and re-layouts, one_block(): coord_part = lax.dynamic_slice_in_dim(coords[0], first_row, per_map, 0)  6.17 us
    another operation x1, loops' own time, per_device(): lax.map(one_block, jnp.arange(local_count // per_map, dtype=jnp.int32))  5.97 us
    dynamic_slice x16, local copies, waits for them, and re-layouts, one_block(): vis_part = lax.dynamic_slice_in_dim(visibilities[0], first_row, per_map, 0)  5.88 us
    lt x8, local copies, waits for them, and re-layouts, block_images(): jnp.arange(slot_count, dtype=jnp.int32) < counts[:, None]  5.86 us
  transfers between devices with their start and end apart: 3, of which 2 were waited for; matrix products, arithmetic and copies ran while one was open for 4% of the time, Pallas kernels for 0%

commit v1 on v0

v1 whole, which is shorter than its diff:
```python
import functools
import math

import jax
import jax.numpy as jnp
import numpy as np
from jax import lax
from jax.experimental import pallas as pl
from jax.experimental.pallas import tpu as pltpu
from jax.sharding import PartitionSpec as P

SUB = 32
TILE = 256
LANES = 128
SINE = (4.442883014678955, -7.308245658874512, 3.6063544750213623, -0.8461129069328308, 0.10982698202133179)
COSINE = (1.4142135381698608, -6.978850841522217, 5.7394609451293945, -1.8835626224777222, 0.31069815158843994)
PARAMS = dict(compiler_params=pltpu.CompilerParams(vmem_limit_bytes=48 * 1024 * 1024))


def iota(shape, axis):
    return lax.broadcasted_iota(jnp.int32, shape, axis)


def turn(x):
    t = x - jnp.round(x)
    u = t * t
    s = ((((SINE[4] * u + SINE[3]) * u + SINE[2]) * u + SINE[1]) * u + SINE[0]) * t
    c = (((COSINE[4] * u + COSINE[3]) * u + COSINE[2]) * u + COSINE[1]) * u + COSINE[0]
    return 1.0 - s * s, s * c


def times(xr, xi, yr, yi):
    return xr * yr - xi * yi, xr * yi + xi * yr


def bit_reverse(i, size):
    out = 0
    while size > 1:
        out, i, size = out * 2 + i % 2, i // 2, size // 2
    return out


def column_of(lane):
    half = SUB // 2
    return jnp.where(lane < half, lane + half, SUB - 1 - lane)


def images_kernel(T, L, counts, offsets, coords, vis, keep, send, z1r, z1i, z2r, z2i, vs, cs):
    Q, Q2 = SUB // T, SUB // T // 2
    a, base = lax.axis_index("tm"), lax.axis_index("base")
    first = base * L
    step1, step2 = T // 4, T // 2
    sign1 = 1 - 2 * ((a // step1) % 2)
    sign2 = 1 - 2 * ((a // step2) % 2)
    sign1f, flip = sign1.astype(jnp.float32), (sign1 * sign2).astype(jnp.float32)

    R = 16
    rho, lane = iota((R, LANES), 0), iota((R, LANES), 1)
    owner, block, part = rho // 4, (rho // 2) % 2, rho % 2
    slot = lane + LANES * block
    rate1 = jnp.where(part == 0, 8.0 / SUB, sign1f * (step1 / SUB))
    flips = jnp.where(part == 0, 1.0, flip)
    crossed = jnp.where(part == 0, -1.0, 1.0)

    def pick(values):
        out = values[-1]
        for k in range(len(values) - 2, -1, -1):
            out = jnp.where(owner == k, values[k], out)
        return out

    def prepare(i, carry):
        rows = pl.ds(pl.multiple_of(i * R, R), R)
        subs = [i * 4 + k for k in range(4)]
        row_off = [offsets[0, first + s] for s in subs]
        col_off = [offsets[1, first + s] for s in subs]
        odd = [(r + c) % 2 for r, c in zip(row_off, col_off)]
        signs = [(1 - 2 * o).astype(jnp.float32) for o in odd]
        moved = jnp.where(
            part == 0,
            pick([(c % SUB).astype(jnp.float32) for c in col_off]),
            pick([(r % SUB).astype(jnp.float32) for r in row_off]),
        )
        c = coords[rows, :] + moved
        cs[rows, :] = c
        r1, i1 = turn(c * rate1)
        z1r[rows, :] = r1
        z1i[rows, :] = i1
        z2r[rows, :] = r1 * r1 - i1 * i1
        z2i[rows, :] = 2.0 * r1 * i1 * flips
        along = jnp.where(part == 0, c, pltpu.roll(c, 1, 0))
        hr, hi = turn(along * (-0.5 / SUB))
        x = vis[rows, :].astype(jnp.float32)
        x = jnp.where(slot < pick([counts[0, s] for s in subs]), x * pick(signs), 0.0)
        other = jnp.where(part == 0, pltpu.roll(x, R - 1, 0), pltpu.roll(x, 1, 0))
        vs[rows, :] = x * hr + other * (hi * crossed)
        return carry

    lax.fori_loop(0, 4 * L // R, prepare, 0, unroll=2)

    rho8 = iota((8, LANES), 0)
    rate_u = (rho8.astype(jnp.float32) + 0.5) * (1.0 / SUB)
    delta, q = rho8 // Q, rho8 % Q
    group = max(1, 8 // Q)
    rate_v = (T * q + (a ^ delta) - SUB // 2).astype(jnp.float32) * (1.0 / SUB)
    low = iota((8, LANES), 1) < LANES // 2

    def row(ref, r):
        return jnp.broadcast_to(ref[pl.ds(r, 1), :], (8, LANES))

    def one(s, carry):
        lhs_r, lhs_i, cos_u, sin_u = [], [], [], []
        for b in range(2):
            ru = s * 4 + b * 2
            rv = ru + 1
            c0, s0 = turn(row(cs, ru) * rate_u)
            c1, s1 = times(c0, s0, row(z1r, ru), row(z1i, ru))
            cos_u.append(jnp.concatenate([c0, c1], 0).astype(jnp.bfloat16))
            sin_u.append(jnp.concatenate([s0, s1], 0).astype(jnp.bfloat16))
            tr, ti = turn(row(cs, rv) * rate_v)
            w0 = times(row(vs, ru), row(vs, rv), tr, ti)
            y1, y2 = (row(z1r, rv), row(z1i, rv)), (row(z2r, rv), row(z2i, rv))
            w1, w2 = times(*w0, *y1), times(*w0, *y2)
            w3 = times(*w1, *y2)
            lhs_r.append(jnp.concatenate([w[0] for w in (w0, w1, w2, w3)], 0).astype(jnp.bfloat16))
            lhs_i.append(jnp.concatenate([w[1] for w in (w0, w1, w2, w3)], 0).astype(jnp.bfloat16))
        neg_u = [-x for x in sin_u]
        lhs = jnp.concatenate(lhs_r + lhs_i, 1)
        plus_r, minus_r = jnp.concatenate(cos_u + neg_u, 1), jnp.concatenate(cos_u + sin_u, 1)
        plus_i, minus_i = jnp.concatenate(sin_u + cos_u, 1), jnp.concatenate(neg_u + cos_u, 1)
        rhs = jnp.concatenate([plus_r, minus_r, plus_i, minus_i] * 2, 0)
        out = lax.dot_general(lhs, rhs, (((1,), (1,)), ((), ())), preferred_element_type=jnp.float32)
        for g in range(4):
            v = out[8 * g : 8 * g + 8]
            v = jnp.where(low, v, pltpu.roll(v, 8 - Q2, 0)).astype(jnp.bfloat16)
            for k in range(group):
                d = g * group + k
                place = bit_reverse(d // 2, T // 2)
                ref = send if d % 2 else keep
                ref[place, s] = v[k * Q : k * Q + Q2]
        return carry

    lax.fori_loop(0, L, one, 0, unroll=4)


def images(T, L, counts, offsets, coords, vis):
    Q2 = SUB // T // 2
    half = jax.ShapeDtypeStruct((T // 2, L, Q2, LANES), jnp.bfloat16)
    smem, vmem = pl.BlockSpec(memory_space=pltpu.SMEM), pl.BlockSpec(memory_space=pltpu.VMEM)
    return pl.pallas_call(
        functools.partial(images_kernel, T, L),
        out_shape=(half, half),
        in_specs=[smem, smem, vmem, vmem],
        out_specs=(vmem, vmem),
        scratch_shapes=[pltpu.VMEM((4 * L, LANES), jnp.float32)] * 6,
        name="images",
        **PARAMS,
    )(counts, offsets, coords, vis)


def send_kernel(T, L, B, cap, capx, held, *refs):
    terms, (slots, ids, screens, out, rows, gathered) = refs[:-6], refs[-6:]
    Q2 = SUB // T // 2
    total = terms[0][0].astype(jnp.float32)
    for t in terms[1:]:
        total = total + t[0].astype(jnp.float32)
    rows[...] = total.reshape(L * Q2, LANES)
    hot = (iota((B * capx, L), 0) == slots[...]).astype(jnp.float32).astype(jnp.bfloat16)
    for q in range(Q2):
        x = rows[pl.ds(q, L, stride=Q2), :].astype(jnp.bfloat16)
        moved = jnp.dot(hot, x, preferred_element_type=jnp.float32).astype(jnp.bfloat16)
        gathered[:, LANES * q : LANES * (q + 1)] = moved
    names = ids[...].astype(jnp.bfloat16)
    tail = capx - cap
    F = Q2 * LANES
    mine = screens[...].astype(jnp.float32)
    fill = jnp.zeros((tail - 8, F), jnp.float32) if tail > 8 else None

    def one(o, carry):
        start = pl.multiple_of(o * capx, 8)
        wanted = iota((LANES, L), 0) + o * capx
        own = (wanted == slots[...]).astype(jnp.float32).astype(jnp.bfloat16)
        listed = lax.dot_general(names, own, (((1,), (1,)), ((), ())), preferred_element_type=jnp.float32)
        listed = jnp.concatenate([listed] + [jnp.zeros((8, F - LANES), jnp.float32)], 1)
        extra = jnp.where(iota((8, F), 0) < held, mine, listed)
        if fill is not None:
            extra = jnp.concatenate([extra, fill], 0)
        block = jnp.concatenate([gathered[pl.ds(start, capx), :][:cap].astype(jnp.float32), extra], 0)
        out[o] = block.astype(jnp.bfloat16)
        return carry

    lax.fori_loop(0, B, one, 0)


def send_blocks(T, L, B, cap, capx, held, terms, slots, ids, screens):
    Q2 = SUB // T // 2
    F = Q2 * LANES
    first = pl.BlockSpec((1, L, Q2, LANES), lambda i: (0, 0, 0, 0))
    whole2 = lambda x: pl.BlockSpec(x.shape, lambda i: (0, 0))
    return pl.pallas_call(
        functools.partial(send_kernel, T, L, B, cap, capx, held),
        grid=(1,),
        out_shape=jax.ShapeDtypeStruct((B, capx, F), jnp.bfloat16),
        in_specs=[first] * len(terms) + [whole2(slots), whole2(ids), whole2(screens)],
        out_specs=pl.BlockSpec((B, capx, F), lambda i: (0, 0, 0)),
        scratch_shapes=[pltpu.VMEM((L * Q2, LANES), jnp.float32), pltpu.VMEM((B * capx, F), jnp.bfloat16)],
        name="send",
        **PARAMS,
    )(*terms, slots, ids, screens)


def place_kernel(T, B, cap, capx, held, blocks, col_off, row_off, weights, keep, send, data, gains, hot, spread, rows):
    Q, Q2 = SUB // T, SUB // T // 2
    F = Q2 * LANES
    S = B * cap
    NX = B * 8
    a = lax.axis_index("tm")
    lane_f = iota((8, F), 1)
    part_f = (lane_f // SUB) % 2

    def gather(b, carry):
        data[pl.ds(b * cap, cap), :] = blocks[b, 0:cap, :].astype(jnp.float32)
        x = blocks[b, cap : cap + 8, :].astype(jnp.float32)
        at = pl.ds(pl.multiple_of(b * 8, 8), 8)
        gains[at, 0:F] = jnp.where(part_f == 0, x, pltpu.roll(x, SUB, 1))
        gains[at, F : 2 * F] = jnp.where(part_f == 1, x, pltpu.roll(x, F - SUB, 1))
        same = iota((cap, LANES), 0) == iota((cap, LANES), 1)
        for k in range(2):
            number = x[held + 2 * k : held + 2 * k + 1, 0:LANES] * 8.0 + x[held + 2 * k + 1 : held + 2 * k + 2, 0:LANES]
            number = jnp.sum(jnp.where(same, jnp.broadcast_to(number, (cap, LANES)), 0.0), axis=1, keepdims=True)
            hit = number.astype(jnp.int32) == iota((cap, NX), 1)
            hot[k, pl.ds(b * cap, cap), :] = hit.astype(jnp.float32)
        return carry

    lax.fori_loop(0, B, gather, 0, unroll=min(B, 8))

    hot_p, hot_q = hot[0].astype(jnp.bfloat16), hot[1].astype(jnp.bfloat16)
    lane = iota((1, LANES), 1)
    low, l = lane // (LANES // 2), column_of(lane % SUB)
    away = [(iota((S, LANES), 1) + LANES * v) - col_off[...] for v in range(2)]
    inside = [(w >= 0) & (w < SUB) for w in away]

    def taper(n):
        scaled = (n.astype(jnp.float32) + 0.5 - SUB / 2.0) / (SUB / 2.0)
        return 1.0 - scaled * scaled

    for q in range(Q2):
        at = slice(LANES * q, LANES * (q + 1))
        at_i = slice(F + LANES * q, F + LANES * (q + 1))
        m = T * (low * Q2 + q) + a
        window = taper(m) * taper(l) * (1.0 / (SUB * 16.0))
        tables = [gains[:, at].astype(jnp.bfloat16), gains[:, at_i].astype(jnp.bfloat16)]
        pr, pi = [jnp.dot(hot_p, t, preferred_element_type=jnp.float32) for t in tables]
        qr, qi = [jnp.dot(hot_q, t, preferred_element_type=jnp.float32) for t in tables]
        d = data[:, at] * window
        x = jnp.concatenate([d * (pr * qr + pi * qi), d * (pr * qi - pi * qr)], 1).astype(jnp.bfloat16)
        y = jnp.dot(x, weights[...], preferred_element_type=jnp.float32)
        for h in range(2):
            for c in range(2):
                v = y[:, (h * 2 + c) * LANES : (h * 2 + c + 1) * LANES]
                for half in range(2):
                    spread[pl.ds((q * 2 + h) * S, S), (c * 2 + half) * LANES : (c * 2 + half + 1) * LANES] = jnp.where(
                        inside[half], v, 0.0
                    ).astype(jnp.bfloat16)

    K = 2 * Q2 * S
    chunk = TILE // T
    index = iota((1, K), 1) // S
    m = (T * ((index % 2) * Q2 + index // 2) + a).astype(jnp.float32) * (1.0 / SUB)
    er, ei = turn(iota((SUB, K), 0).astype(jnp.float32) * m)
    for d in range(T):
        for e in range(chunk // SUB):
            r = (a ^ d) * chunk + e * SUB + iota((SUB, K), 0) - row_off[...]
            mask = (r >= 0) & (r < SUB)
            place = (d % 2) * (T // 2) + bit_reverse(d // 2, T // 2)
            at = place * chunk + e * SUB
            rows[at : at + SUB, :] = jnp.where(mask, er, 0.0).astype(jnp.bfloat16)
            rows[TILE + at : TILE + at + SUB, :] = jnp.where(mask, ei, 0.0).astype(jnp.bfloat16)
    both = jnp.dot(rows[...], spread[...], preferred_element_type=jnp.float32)
    u, v = both[:TILE], both[TILE:]
    tile = jnp.concatenate([u[:, :TILE] + v[:, TILE:], u[:, TILE:] - v[:, :TILE]], 1)
    for i in range(T // 2):
        keep[i] = tile[i * chunk : (i + 1) * chunk]
        j = T // 2 + i
        send[i] = tile[j * chunk : (j + 1) * chunk].astype(jnp.bfloat16)


def place_blocks(T, B, cap, capx, held, blocks, col_off, row_off, weights):
    Q2 = SUB // T // 2
    F, S, K = Q2 * LANES, B * cap, 2 * Q2 * B * cap
    vmem = pl.BlockSpec(memory_space=pltpu.VMEM)
    chunk = TILE // T
    return pl.pallas_call(
        functools.partial(place_kernel, T, B, cap, capx, held),
        out_shape=(
            jax.ShapeDtypeStruct((T // 2, chunk, 2 * TILE), jnp.float32),
            jax.ShapeDtypeStruct((T // 2, chunk, 2 * TILE), jnp.bfloat16),
        ),
        in_specs=[vmem] * 4,
        out_specs=(vmem, vmem),
        scratch_shapes=[
            pltpu.VMEM((S, F), jnp.float32),
            pltpu.VMEM((B * 8, 2 * F), jnp.float32),
            pltpu.VMEM((2, S, B * 8), jnp.float32),
            pltpu.VMEM((K, 2 * TILE), jnp.bfloat16),
            pltpu.VMEM((2 * TILE, K), jnp.bfloat16),
        ],
        name="place",
        **PARAMS,
    )(blocks, col_off, row_off, weights)


def transform_weights():
    lam = np.arange(SUB)
    l = np.where(lam < SUB // 2, lam + SUB // 2, SUB - 1 - lam)
    angle = 2.0 * math.pi * (l[:, None] * (np.arange(LANES)[None, :] % SUB) % SUB) / SUB
    cos, sin = np.cos(angle), np.sin(angle)
    out = np.zeros((2, 2, 2, SUB, 2, 2, LANES))
    for h in range(2):
        out[0, h, 0, :, h, 0], out[0, h, 0, :, h, 1] = cos, -sin
        out[0, h, 1, :, h, 0], out[0, h, 1, :, h, 1] = sin, cos
        out[1, h, 1, :, h, 0], out[1, h, 1, :, h, 1] = -cos, sin
        out[1, h, 0, :, h, 0], out[1, h, 0, :, h, 1] = sin, cos
    return jnp.asarray(out.reshape(2 * LANES, 4 * LANES), jnp.float32).astype(jnp.bfloat16)


def halve(T, keep, send):
    swap = lambda x, d: lax.ppermute(x, "tm", [(i, i ^ d) for i in range(T)])
    terms, d = [keep, swap(send, 1)], 2
    while d < T:
        half = T // d // 2
        moving = sum(t[half : 2 * half].astype(jnp.float32) for t in terms).astype(jnp.bfloat16)
        terms.append(swap(moving, d))
        d *= 2
    return terms


def per_device(visibilities, coords, counts, stations, owners, offsets, screens):
    T, B = lax.axis_size("tm"), lax.axis_size("base")
    L, slots = visibilities.shape[1], visibilities.shape[3]
    a, base = lax.axis_index("tm"), lax.axis_index("base")
    Q, Q2 = SUB // T, SUB // T // 2
    F = Q2 * LANES
    held = screens.shape[0]
    cap = -(-max(2, 3 * L // (2 * B)) // 8) * 8
    capx = cap + 8

    def flat(x):
        return x.reshape(L, 2, slots // LANES, LANES).transpose(0, 2, 1, 3).reshape(4 * L, LANES)

    keep, send = images(T, L, counts, offsets.T, flat(coords[0]), flat(visibilities[0]))

    owner = owners[:, 0].reshape(B, L)
    mine = lax.dynamic_slice_in_dim(owner, base, 1, 0)[0]
    order = jnp.arange(L, dtype=jnp.int32)
    earlier = order[:, None] < order[None, :]
    rank = jnp.sum(((mine[:, None] == mine[None, :]) & earlier).astype(jnp.int32), axis=0)
    slot_ids = (mine * capx + rank)[None, :]
    names = jnp.stack([stations[:, 0] // held, stations[:, 0] % held, stations[:, 1] // held, stations[:, 1] % held])
    names = jnp.concatenate([jnp.zeros((8 - 4, L), jnp.float32), names.astype(jnp.float32)], 0)

    pixels = screens.reshape(held, 2, Q, T, SUB)
    pixels = lax.dynamic_slice_in_dim(pixels, a, 1, 3)[:, :, :, 0]
    pixels = jnp.concatenate([pixels[..., SUB // 2 :], pixels[..., : SUB // 2][..., ::-1]], -1)
    pixels = pixels.reshape(held, 2, 2, Q2, SUB).transpose(0, 3, 2, 1, 4).reshape(held, F)
    pixels = jnp.concatenate([pixels, jnp.zeros((8 - held, F), pixels.dtype)], 0)

    to_me = (owner == base)
    before = jnp.sum((to_me[:, :, None] & earlier[None]).astype(jnp.int32), axis=1)
    chosen = to_me[:, None, :] & (before[:, None, :] == jnp.arange(cap, dtype=jnp.int32)[None, :, None])
    offs = offsets.T.reshape(2, B, 1, L)
    slot_offs = jnp.sum(jnp.where(chosen[None], offs, 0), axis=3).reshape(2, B * cap)
    col_off = slot_offs[1][:, None]
    row_off = jnp.tile(slot_offs[0], 2 * Q2)[None, :]

    terms = halve(T, keep, send)
    outgoing = send_blocks(T, L, B, cap, capx, held, terms, slot_ids, names, pixels)
    incoming = lax.all_to_all(outgoing, "base", split_axis=0, concat_axis=0, tiled=True)
    keep, send = place_blocks(T, B, cap, capx, held, incoming, col_off, row_off, transform_weights())
    tile = sum(t[0].astype(jnp.float32) for t in halve(T, keep, send))
    return tile.reshape(1, TILE // T, 2, TILE)


def solution(mesh):
    return jax.shard_map(
        per_device,
        mesh=mesh,
        in_specs=(
            P("tm", "base", None, None),
            P("tm", "base", None, None),
            P("tm", "base"),
            P("base", None),
            P(),
            P(),
            P("base", None, None),
        ),
        out_specs=P("base", "tm", None, None),
        check_vma=False,
    )
```

time: 171 us -> 51.2 us (0.30)
  other arithmetic: 40.7 us -> 0.93 us
  blocking collectives: 32.5 us -> 0 us
  local copies, waits for them, and re-layouts: 33.3 us -> 6.49 us
  Pallas kernels: 0 us -> 16.8 us
  between operations: 13.8 us -> 0.18 us
  matrix products: 11.8 us -> 0 us
  waiting for transfers between devices: 25.7 us -> 15.4 us
  loops' own time: 5.97 us -> 0 us
  starting transfers between devices: 5.75 us -> 10.9 us
    another operation x18 -> x0, other arithmetic: 35.4 us -> none
    all_gather x1 -> x0, blocking collectives: 32.5 us -> none  [per_device(): lax.all_gather(screens, 'base', axis=0, tiled=True)]
    reduce_scatter x1 -> x0, waiting for transfers between devices: 18.2 us -> none  [per_device(): lax.psum_scatter(tile_sum.astype(jnp.bfloat16), 'tm', scatter_dimension=0...]
    dynamic_slice x41 -> x1, local copies, waits for them, and re-layouts: 17.4 us -> 0.04 us  [per_device(): pixels = lax.dynamic_slice_in_dim(pixels, a, 1, 3)[:, :, :, 0]]
    pallas_call x0 -> x3, Pallas kernels: none -> 16.8 us  [the longest x1 12.5 us: images(): pl.pallas_call(functools.partial(images_kernel, T, L), out_shape=(half, h...]
    dot_general x19 -> x0, matrix products: 11.8 us -> none  [the longest x8 2.22 us: block_images(): jnp.einsum('smv,slv->sml', table_v, table_u, preferred_element_type=jnp.f...]
    ppermute x0 -> x4, waiting for transfers between devices: none -> 7.26 us  [halve(): swap = lambda x, d: lax.ppermute(x, 'tm', [(i, i ^ d) for i in range(T)])]
    another operation x1 -> x0, loops' own time: 5.97 us -> none  [per_device(): lax.map(one_block, jnp.arange(local_count // per_map, dtype=jnp.int32))]
  transfers between devices with their start and end apart: 3 -> 5, of which waited for: 2 -> 4; matrix products, arithmetic and copies ran while one was open for 4% -> 3% of each run, Pallas kernels for 0% -> 0%
where the time goes in v1:
time: 51.2 us; the launch traced here: 50.7 us
  Pallas kernels  16.8 us (33%)
  waiting for transfers between devices  15.4 us (30%)
  starting transfers between devices  10.9 us (21%)
  local copies, waits for them, and re-layouts  6.49 us (13%)
  other arithmetic  0.93 us (2%)
    pallas_call x1, Pallas kernels, images(): pl.pallas_call(functools.partial(images_kernel, T, L), out_shape=(half, h...  12.5 us
    all_to_all x1, waiting for transfers between devices, per_device(): lax.all_to_all(outgoing, 'base', split_axis=0, concat_axis=0, tiled=True)  8.13 us
    ppermute x4, waiting for transfers between devices, halve(): swap = lambda x, d: lax.ppermute(x, 'tm', [(i, i ^ d) for i in range(T)])  7.26 us
    all_to_all x1, starting transfers between devices, per_device(): lax.all_to_all(outgoing, 'base', split_axis=0, concat_axis=0, tiled=True)  6.16 us
    unnamed x20, local copies, waits for them, and re-layouts  5.07 us
    ppermute x4, starting transfers between devices, halve(): swap = lambda x, d: lax.ppermute(x, 'tm', [(i, i ^ d) for i in range(T)])  4.78 us
    pallas_call x1, Pallas kernels, send_blocks(): pl.pallas_call(functools.partial(send_kernel, T, L, B, cap, capx, held),...  2.23 us
    pallas_call x1, Pallas kernels, place_blocks(): pl.pallas_call(functools.partial(place_kernel, T, B, cap, capx, held), ou...  2.1 us
  transfers between devices with their start and end apart: 5, of which 4 were waited for; matrix products, arithmetic and copies ran while one was open for 3% of the time, Pallas kernels for 0%

profile of v1, /device:TPU:0, one launch (start us, length us, event | category | flops | bytes accessed | tf_op | source)
XLA Modules:
  0.0 50.7 jit_solution(18116412550190295210)
XLA Ops:
  0.0 0.0 copy-start.5
  0.0 0.7 %copy-done.5 = s32[1,128]{1,0:T(1,128)S(1)} copy-done((s32[1,128]{1,0:T(1,128)S(1)}, s32[1,128]{1,0:T(1,128)}, u32[]{:S(2)}) %copy-start.5) | copy-done | bytes 536
  0.7 0.0 copy-start
  0.7 0.9 %copy-done = f32[1,128,2,256]{3,2,1,0:T(2,128)S(1)} copy-done((f32[1,128,2,256]{3,2,1,0:T(2,128)S(1)}, f32[1,128,2,256]{3,2,1,0:T(2,128)}, u32[]{:S(2)}) %copy-start) | copy-done | bytes 262168
  1.6 0.0 copy-start.2
  1.6 0.9 %copy-done.2 = bf16[1,128,2,256]{3,2,1,0:T(2,128)(2,1)S(1)} copy-done((bf16[1,128,2,256]{3,2,1,0:T(2,128)(2,1)S(1)}, bf16[1,128,2,256]{3,2,1,0:T(2,128)(2,1)}, u32[]{:S(2)}) %copy-start.2) | copy-done | bytes 131096
  2.5 0.0 copy-start.3
  2.5 0.7 %copy-done.3 = s32[1024,2]{0,1:T(2,128)S(1)} copy-done((s32[1024,2]{0,1:T(2,128)S(1)}, s32[1024,2]{0,1:T(2,128)}, u32[]{:S(2)}) %copy-start.3) | copy-done | bytes 8216
  3.2 12.5 %images.1 = (bf16[2,128,4,128]{3,2,1,0:T(4,128)(2,1)S(1)}, bf16[2,128,4,128]{3,2,1,0:T(4,128)(2,1)S(1)}) custom-call(s32[1,128]{1,0:T(1,128)S(1)} %copy-done.5, s32[2,1024]{1,0:T(2,128)S(1)} %bitcast.52, f32[512,128]{1,0:T(8,128)S(1)} %bitcast.50, bf16[512,128]{1,0:T(8,128)(2,1)S(1)} %bitcast.51), custom_call_target="tpu_custom_call" | custom-call | tf_op jit(solution)/shard_map/images/pallas_call | solution.py:149
  15.7 0.5 %collective-permute-start = (bf16[2,128,4,128]{3,2,1,0:T(4,128)(2,1)S(1)}, bf16[2,128,4,128]{3,2,1,0:T(4,128)(2,1)S(1)}, u32[]{:S(2)}, u32[]{:S(2)}) collective-permute-start(bf16[2,128,4,128]{3,2,1,0:T(4,128)(2,1)S(1)} %get-tuple-element.10), channel_id=1, source_target_pairs={{0,1},{1,0},{2,3},{3,2},{4,5},{5,4},{6,7},{7,6},{8,9},{9,8},{10,11... | collective-permute-start | bytes 786440 | tf_op jit(solution)/shard_map/ppermute | solution.py:327
  16.2 0.0 copy-start.7
  16.2 0.0 copy-start.6
  16.2 0.6 %copy-done.7 = s32[1024,1]{0,1:T(1,128)S(1)} copy-done((s32[1024,1]{0,1:T(1,128)S(1)}, s32[1024,1]{0,1:T(1,128)}, u32[]{:S(2)}) %copy-start.7) | copy-done | bytes 4120
  16.9 0.1 convert_reduce_fusion.1
  17.0 0.0 copy-done.6
  17.0 0.1 reshape.295
  17.2 0.1 fusion.2
  17.3 0.0 copy-start.8
  17.3 0.1 rev.3
  17.4 0.6 %copy-done.8 = s32[128,2]{0,1:T(2,128)S(1)} copy-done((s32[128,2]{0,1:T(2,128)S(1)}, s32[128,2]{0,1:T(2,128)}, u32[]{:S(2)}) %copy-start.8) | copy-done | bytes 1048
  18.0 0.1 pad_maximum_fusion
  18.1 0.0 collective-permute-done.refs_1_
  18.1 0.1 add_convert_fusion
  18.2 2.6 %collective-permute-start.1 = (bf16[1,128,4,128]{3,2,1,0:T(4,128)(2,1)S(1)}, bf16[1,128,4,128]{3,2,1,0:T(4,128)(2,1)S(1)}, u32[]{:S(2)}, u32[]{:S(2)}) collective-permute-start(bf16[1,128,4,128]{3,2,1,0:T(4,128)(2,1)S(1)} %add_convert_fusion), channel_id=1, source_target_pairs={{0,2},{1,3},{2,0},{3,1},{4,6},{5,7},{6,4},{7,5},{8,10},{9,11},{10,... | collective-permute-start | bytes 393224 | tf_op jit(solution)/shard_map/ppermute | solution.py:327
  20.8 0.0 copy-start.4
  20.8 0.1 reshape.297
  20.9 0.6 %copy-done.4 = s32[1024,2]{0,1:T(2,128)S(1)} copy-done((s32[1024,2]{0,1:T(2,128)S(1)}, s32[1024,2]{0,1:T(2,128)}, u32[]{:S(2)}) %copy-start.4) | copy-done | bytes 8216
  21.5 0.2 convert_reduce_fusion
  21.7 3.2 %collective-permute-done.1.refs_2_ = bf16[1,128,4,128]{3,2,1,0:T(4,128)(2,1)S(1)} collective-permute-done((bf16[1,128,4,128]{3,2,1,0:T(4,128)(2,1)S(1)}, bf16[1,128,4,128]{3,2,1,0:T(4,128)(2,1)S(1)}, u32[]{:S(2)}, u32[]{:S(2)}) %collective-permute-start.1) | collective-permute-done | bytes 131104 | tf_op jit(solution)/shard_map/ppermute | solution.py:327
  24.9 2.2 %send.1 = bf16[8,32,512]{2,1,0:T(8,128)(2,1)} custom-call(bf16[2,128,4,128]{3,2,1,0:T(4,128)(2,1)S(1)} %get-tuple-element.9.refs_0_, bf16[2,128,4,128]{3,2,1,0:T(4,128)(2,1)S(1)} %collective-permute-done.refs_1_, bf16[1,128,4,128]{3,2,1,0:T(4,128)(2,1)S(1)} %collective-permute-done.1.refs_2_, s32[1,128]{1,0:T(1,128)S(1)} %bitcast_add_fusion.refs_3_, ...), custom_call_target="tpu_custom_call" | custom-call | tf_op jit(solution)/shard_map/send/pallas_call | solution.py:199
  27.1 0.0 copy-start.1
  27.1 6.2 %all-to-all-start = ((bf16[8,32,512]{2,1,0:T(8,128)(2,1)}), bf16[8,32,512]{2,1,0:T(8,128)(2,1)S(1)}, u32[]{:S(2)}, u32[]{:S(2)}) async-start(bf16[8,32,512]{2,1,0:T(8,128)(2,1)} %send.1), calls=%async_computation | async-start | bytes 524288 | tf_op jit(solution)/shard_map/all_to_all | solution.py:377
  33.3 0.3 select_reduce_fusion
  33.7 0.1 broadcast_in_dim_squeeze.5.col_off
  33.8 0.1 tile.7
  33.9 0.1 broadcast_in_dim_tile.3.row_off
  34.0 8.1 %all-to-all-done.blocks = bf16[8,32,512]{2,1,0:T(8,128)(2,1)S(1)} async-done(((bf16[8,32,512]{2,1,0:T(8,128)(2,1)}), bf16[8,32,512]{2,1,0:T(8,128)(2,1)S(1)}, u32[]{:S(2)}, u32[]{:S(2)}) %all-to-all-start) | async-done | bytes 262176 | tf_op jit(solution)/shard_map/all_to_all | solution.py:377
  42.1 0.0 copy-done.1
  42.1 2.1 %place.1 = (f32[2,64,512]{2,1,0:T(8,128)S(1)}, bf16[2,64,512]{2,1,0:T(8,128)(2,1)S(1)}) custom-call(bf16[8,32,512]{2,1,0:T(8,128)(2,1)S(1)} %all-to-all-done.blocks, s32[192,1]{1,0:T(8,128)S(1)} %broadcast_in_dim_squeeze.5.col_off, s32[1,1536]{1,0:T(1,128)S(1)} %broadcast_in_dim_tile.3.row_off, bf16[256,512]{1,0:T(8,128)(2,1)S(1)} %copy-done.1), custom_call_target="tpu_custom_call" | custom-call | tf_op jit(solution)/shard_map/place/pallas_call | solution.py:292
  44.2 0.1 collective-permute-start.2
  44.3 1.3 %collective-permute-done.2 = bf16[2,64,512]{2,1,0:T(8,128)(2,1)S(1)} collective-permute-done((bf16[2,64,512]{2,1,0:T(8,128)(2,1)S(1)}, bf16[2,64,512]{2,1,0:T(8,128)(2,1)S(1)}, u32[]{:S(2)}, u32[]{:S(2)}) %collective-permute-start.2) | collective-permute-done | bytes 131104 | tf_op jit(solution)/shard_map/ppermute | solution.py:327
  45.6 1.6 %collective-permute-start.3 = (bf16[1,64,512]{2,1,0:T(8,128)(2,1)S(1)}, bf16[1,64,512]{2,1,0:T(8,128)(2,1)S(1)}, u32[]{:S(2)}, u32[]{:S(2)}) collective-permute-start(bf16[1,64,512]{2,1,0:T(8,128)(2,1)S(1)} %add_convert_fusion.1), channel_id=1, source_target_pairs={{0,2},{1,3},{2,0},{3,1},{4,6},{5,7},{6,4},{7,5},{8,10},{9,11},{10,... | collective-permute-start | bytes 196616 | tf_op jit(solution)/shard_map/ppermute | solution.py:327
  47.2 2.7 %collective-permute-done.3 = bf16[1,64,512]{2,1,0:T(8,128)(2,1)S(1)} collective-permute-done((bf16[1,64,512]{2,1,0:T(8,128)(2,1)S(1)}, bf16[1,64,512]{2,1,0:T(8,128)(2,1)S(1)}, u32[]{:S(2)}, u32[]{:S(2)}) %collective-permute-start.3) | collective-permute-done | bytes 65568 | tf_op jit(solution)/shard_map/ppermute | solution.py:327
  50.0 0.7 %add.93 = f32[1,64,2,256]{3,2,1,0:T(2,128)} reshape(f32[1,64,512]{2,1,0:T(8,128)S(1)} %convert_add_fusion) | data formatting | bytes 262144 | tf_op jit(solution)/shard_map/add | solution.py:379
  (18 shorter events, 0.2 us)
Async XLA Ops:
  0.0 0.7 %copy-start.5 = (s32[1,128]{1,0:T(1,128)S(1)}, s32[1,128]{1,0:T(1,128)}, u32[]{:S(2)}) copy-start(s32[1,128]{1,0:T(1,128)} %counts.1) | copy-start | bytes 1540
  0.7 0.9 %copy-start = (f32[1,128,2,256]{3,2,1,0:T(2,128)S(1)}, f32[1,128,2,256]{3,2,1,0:T(2,128)}, u32[]{:S(2)}) copy-start(f32[1,128,2,256]{3,2,1,0:T(2,128)} %param.9) | copy-start | bytes 786436
  1.6 0.9 %copy-start.2 = (bf16[1,128,2,256]{3,2,1,0:T(2,128)(2,1)S(1)}, bf16[1,128,2,256]{3,2,1,0:T(2,128)(2,1)}, u32[]{:S(2)}) copy-start(bf16[1,128,2,256]{3,2,1,0:T(2,128)(2,1)} %param.8) | copy-start | bytes 393220
  2.5 0.7 %copy-start.3 = (s32[1024,2]{0,1:T(2,128)S(1)}, s32[1024,2]{0,1:T(2,128)}, u32[]{:S(2)}) copy-start(s32[1024,2]{0,1:T(2,128)} %param.13) | copy-start | bytes 24580
  15.7 2.4 %collective-permute-start = (bf16[2,128,4,128]{3,2,1,0:T(4,128)(2,1)S(1)}, bf16[2,128,4,128]{3,2,1,0:T(4,128)(2,1)S(1)}, u32[]{:S(2)}, u32[]{:S(2)}) collective-permute-start(bf16[2,128,4,128]{3,2,1,0:T(4,128)(2,1)S(1)} %get-tuple-element.10), channel_id=1, source_target_pairs={{0,1},{1,0},{2,3},{3,2},{4,5},{5,4},{6,7},{7,6},{8,9},{9,8},{10,11... | collective-permute-start | bytes 786440 | tf_op jit(solution)/shard_map/ppermute | solution.py:327
  16.2 0.7 %copy-start.7 = (s32[1024,1]{0,1:T(1,128)S(1)}, s32[1024,1]{0,1:T(1,128)}, u32[]{:S(2)}) copy-start(s32[1024,1]{0,1:T(1,128)} %param.12) | copy-start | bytes 12292
  16.2 0.8 %copy-start.6 = (bf16[4,2,1024]{2,1,0:T(2,128)(2,1)S(1)}, bf16[4,2,1024]{2,1,0:T(2,128)(2,1)}, u32[]{:S(2)}) copy-start(bf16[4,2,1024]{2,1,0:T(2,128)(2,1)} %param.14) | copy-start | bytes 49156
  17.3 0.7 %copy-start.8 = (s32[128,2]{0,1:T(2,128)S(1)}, s32[128,2]{0,1:T(2,128)}, u32[]{:S(2)}) copy-start(s32[128,2]{0,1:T(2,128)} %param.11) | copy-start | bytes 3076
  18.2 6.8 %collective-permute-start.1 = (bf16[1,128,4,128]{3,2,1,0:T(4,128)(2,1)S(1)}, bf16[1,128,4,128]{3,2,1,0:T(4,128)(2,1)S(1)}, u32[]{:S(2)}, u32[]{:S(2)}) collective-permute-start(bf16[1,128,4,128]{3,2,1,0:T(4,128)(2,1)S(1)} %add_convert_fusion), channel_id=1, source_target_pairs={{0,2},{1,3},{2,0},{3,1},{4,6},{5,7},{6,4},{7,5},{8,10},{9,11},{10,... | collective-permute-start | bytes 393224 | tf_op jit(solution)/shard_map/ppermute | solution.py:327
  20.8 0.7 %copy-start.4 = (s32[1024,2]{0,1:T(2,128)S(1)}, s32[1024,2]{0,1:T(2,128)}, u32[]{:S(2)}) copy-start(s32[1024,2]{0,1:T(2,128)} %param.13) | copy-start | bytes 24580
  27.1 15.0 %copy-start.1 = (bf16[256,512]{1,0:T(8,128)(2,1)S(1)}, bf16[256,512]{1,0:T(8,128)(2,1)}, u32[]{:S(2)}) copy-start(bf16[256,512]{1,0:T(8,128)(2,1)} %constant.69.weights) | copy-start | bytes 786436
  27.1 14.9 %all-to-all-start = ((bf16[8,32,512]{2,1,0:T(8,128)(2,1)}), bf16[8,32,512]{2,1,0:T(8,128)(2,1)S(1)}, u32[]{:S(2)}, u32[]{:S(2)}) async-start(bf16[8,32,512]{2,1,0:T(8,128)(2,1)} %send.1), calls=%async_computation | async-start | bytes 524288 | tf_op jit(solution)/shard_map/all_to_all | solution.py:377
  44.2 1.4 %collective-permute-start.2 = (bf16[2,64,512]{2,1,0:T(8,128)(2,1)S(1)}, bf16[2,64,512]{2,1,0:T(8,128)(2,1)S(1)}, u32[]{:S(2)}, u32[]{:S(2)}) collective-permute-start(bf16[2,64,512]{2,1,0:T(8,128)(2,1)S(1)} %get-tuple-element.12), channel_id=1, source_target_pairs={{0,1},{1,0},{2,3},{3,2},{4,5},{5,4},{6,7},{7,6},{8,9},{9,8},{10,11... | collective-permute-start | bytes 393224 | tf_op jit(solution)/shard_map/ppermute | solution.py:327
  45.6 4.3 %collective-permute-start.3 = (bf16[1,64,512]{2,1,0:T(8,128)(2,1)S(1)}, bf16[1,64,512]{2,1,0:T(8,128)(2,1)S(1)}, u32[]{:S(2)}, u32[]{:S(2)}) collective-permute-start(bf16[1,64,512]{2,1,0:T(8,128)(2,1)S(1)} %add_convert_fusion.1), channel_id=1, source_target_pairs={{0,2},{1,3},{2,0},{3,1},{4,6},{5,7},{6,4},{7,5},{8,10},{9,11},{10,... | collective-permute-start | bytes 196616 | tf_op jit(solution)/shard_map/ppermute | solution.py:327

commit v2 on v1

--- a/solution.py
+++ b/solution.py
@@ -45,10 +45,22 @@
     return jnp.where(lane < half, lane + half, SUB - 1 - lane)
 
 
-def images_kernel(T, L, counts, offsets, coords, vis, keep, send, z1r, z1i, z2r, z2i, vs, cs):
+def images_kernel(T, L, in_counts, in_offsets, in_coords, in_vis, keep, send, z1r, z1i, z2r, z2i, vs, cs, vis, counts, offsets, sems):
     Q, Q2 = SUB // T, SUB // T // 2
     a, base = lax.axis_index("tm"), lax.axis_index("base")
-    first = base * L
+    parts = 2
+    span = 4 * L // parts
+    numbers = [
+        pltpu.make_async_copy(in_counts, counts, sems.at[0]),
+        pltpu.make_async_copy(in_offsets.at[:, pl.ds(pl.multiple_of(base * L, LANES), L)], offsets, sems.at[1]),
+    ]
+    loads = []
+    for k in range(parts):
+        at = pl.ds(k * span, span)
+        loads.append(pltpu.make_async_copy(in_coords.at[at, :], cs.at[at, :], sems.at[2 + 2 * k]))
+        loads.append(pltpu.make_async_copy(in_vis.at[at, :], vis.at[at, :], sems.at[3 + 2 * k]))
+    for copy in numbers + loads:
+        copy.start()
     step1, step2 = T // 4, T // 2
     sign1 = 1 - 2 * ((a // step1) % 2)
     sign2 = 1 - 2 * ((a // step2) % 2)
@@ -71,16 +83,16 @@
     def prepare(i, carry):
         rows = pl.ds(pl.multiple_of(i * R, R), R)
         subs = [i * 4 + k for k in range(4)]
-        row_off = [offsets[0, first + s] for s in subs]
-        col_off = [offsets[1, first + s] for s in subs]
-        odd = [(r + c) % 2 for r, c in zip(row_off, col_off)]
+        row_off = [offsets[0, s] for s in subs]
+        col_off = [offsets[1, s] for s in subs]
+        odd = [(r + c) & 1 for r, c in zip(row_off, col_off)]
         signs = [(1 - 2 * o).astype(jnp.float32) for o in odd]
         moved = jnp.where(
             part == 0,
-            pick([(c % SUB).astype(jnp.float32) for c in col_off]),
-            pick([(r % SUB).astype(jnp.float32) for r in row_off]),
+            pick([(c & (SUB - 1)).astype(jnp.float32) for c in col_off]),
+            pick([(r & (SUB - 1)).astype(jnp.float32) for r in row_off]),
         )
-        c = coords[rows, :] + moved
+        c = cs[rows, :] + moved
         cs[rows, :] = c
         r1, i1 = turn(c * rate1)
         z1r[rows, :] = r1
@@ -95,7 +107,12 @@
         vs[rows, :] = x * hr + other * (hi * crossed)
         return carry
 
-    lax.fori_loop(0, 4 * L // R, prepare, 0, unroll=2)
+    for copy in numbers:
+        copy.wait()
+    for k in range(parts):
+        loads[2 * k].wait()
+        loads[2 * k + 1].wait()
+        lax.fori_loop(k * (span // R), (k + 1) * (span // R), prepare, 0, unroll=2)
 
     rho8 = iota((8, LANES), 0)
     rate_u = (rho8.astype(jnp.float32) + 0.5) * (1.0 / SUB)
@@ -107,7 +124,7 @@
     def row(ref, r):
         return jnp.broadcast_to(ref[pl.ds(r, 1), :], (8, LANES))
 
-    def one(s, carry):
+    def tables(s):
         lhs_r, lhs_i, cos_u, sin_u = [], [], [], []
         for b in range(2):
             ru = s * 4 + b * 2
@@ -127,85 +144,134 @@
         lhs = jnp.concatenate(lhs_r + lhs_i, 1)
         plus_r, minus_r = jnp.concatenate(cos_u + neg_u, 1), jnp.concatenate(cos_u + sin_u, 1)
         plus_i, minus_i = jnp.concatenate(sin_u + cos_u, 1), jnp.concatenate(neg_u + cos_u, 1)
-        rhs = jnp.concatenate([plus_r, minus_r, plus_i, minus_i] * 2, 0)
-        out = lax.dot_general(lhs, rhs, (((1,), (1,)), ((), ())), preferred_element_type=jnp.float32)
+        return lhs, [plus_r, minus_r, plus_i, minus_i]
+
+    def two(p, carry):
+        s = 2 * p
+        l0, r0 = tables(s)
+        l1, r1 = tables(s + 1)
+        out = lax.dot_general(
+            jnp.concatenate([l0, l1], 0),
+            jnp.concatenate(r0 + r1, 0),
+            (((1,), (1,)), ((), ())),
+            preferred_element_type=jnp.float32,
+        )
         for g in range(4):
-            v = out[8 * g : 8 * g + 8]
-            v = jnp.where(low, v, pltpu.roll(v, 8 - Q2, 0)).astype(jnp.bfloat16)
+            x, y = out[8 * g : 8 * g + 8], out[SUB + 8 * g : SUB + 8 * g + 8]
+            x = jnp.where(low, x, pltpu.roll(pltpu.roll(x, 8 - Q2, 0), LANES // 2, 1)).astype(jnp.bfloat16)
+            y = jnp.where(low, pltpu.roll(y, LANES // 2, 1), pltpu.roll(y, 8 - Q2, 0)).astype(jnp.bfloat16)
             for k in range(group):
                 d = g * group + k
                 place = bit_reverse(d // 2, T // 2)
                 ref = send if d % 2 else keep
-                ref[place, s] = v[k * Q : k * Q + Q2]
+                ref[place, s] = x[k * Q : k * Q + Q2]
+                ref[place, s + 1] = y[k * Q : k * Q + Q2]
         return carry
 
-    lax.fori_loop(0, L, one, 0, unroll=4)
+    lax.fori_loop(0, L // 2, two, 0, unroll=16)
 
 
 def images(T, L, counts, offsets, coords, vis):
     Q2 = SUB // T // 2
     half = jax.ShapeDtypeStruct((T // 2, L, Q2, LANES), jnp.bfloat16)
-    smem, vmem = pl.BlockSpec(memory_space=pltpu.SMEM), pl.BlockSpec(memory_space=pltpu.VMEM)
+    hbm, vmem = pl.BlockSpec(memory_space=pltpu.HBM), pl.BlockSpec(memory_space=pltpu.VMEM)
     return pl.pallas_call(
         functools.partial(images_kernel, T, L),
         out_shape=(half, half),
-        in_specs=[smem, smem, vmem, vmem],
+        in_specs=[hbm] * 4,
         out_specs=(vmem, vmem),
-        scratch_shapes=[pltpu.VMEM((4 * L, LANES), jnp.float32)] * 6,
+        scratch_shapes=[pltpu.VMEM((4 * L, LANES), jnp.float32)] * 6
+        + [
+            pltpu.VMEM((4 * L, LANES), jnp.bfloat16),
+            pltpu.SMEM((1, L), jnp.int32),
+            pltpu.SMEM((2, L), jnp.int32),
+            pltpu.SemaphoreType.DMA((6,)),
+        ],
         name="images",
         **PARAMS,
     )(counts, offsets, coords, vis)
 
 
-def send_kernel(T, L, B, cap, capx, held, *refs):
-    terms, (slots, ids, screens, out, rows, gathered) = refs[:-6], refs[-6:]
-    Q2 = SUB // T // 2
+def index_kernel(T, L, B, cap, capx, held, owners, stations, screens, hot, extras):
+    Q2 = SUB // T // 2
+    F = Q2 * LANES
+    a, base = lax.axis_index("tm"), lax.axis_index("base")
+    mine = jnp.broadcast_to(owners[pl.ds(base, 1), :], (L, L))
+    same = (mine == mine.T) & (iota((L, L), 0) < iota((L, L), 1))
+    rank = jnp.sum(same.astype(jnp.float32), axis=0, keepdims=True).astype(jnp.int32)
+    slots = mine[0:1] * capx + rank
+    hot[...] = (iota((B * capx, L), 0) == slots).astype(jnp.float32).astype(jnp.bfloat16)
+
+    lane = iota((1, F), 1)
+    m = T * (((lane // (2 * SUB)) % 2) * Q2 + lane // LANES) + a
+    pixel = m * SUB + column_of(lane % SUB)
+    select = (iota((SUB * SUB, F), 0) == pixel).astype(jnp.float32).astype(jnp.bfloat16)
+    x = jnp.concatenate([screens[:, 0, :].astype(jnp.float32), screens[:, 1, :].astype(jnp.float32)], 0)
+    x = jnp.dot(x.astype(jnp.bfloat16), select, preferred_element_type=jnp.float32)
+    mine_x = jnp.where((lane // SUB) % 2 == 0, x[:held], x[held:])
+    mine_x = jnp.concatenate([mine_x, jnp.zeros((8 - held, F), jnp.float32)], 0)
+
+    p, q = stations[0:1, :], stations[1:2, :]
+    names = jnp.concatenate([jnp.zeros((4, L), jnp.int32), p // held, p % held, q // held, q % held], 0)
+    names = names.astype(jnp.float32).astype(jnp.bfloat16)
+
+    def one(o, carry):
+        own = (iota((LANES, L), 0) + o * capx == slots).astype(jnp.float32).astype(jnp.bfloat16)
+        listed = lax.dot_general(names, own, (((1,), (1,)), ((), ())), preferred_element_type=jnp.float32)
+        listed = jnp.concatenate([listed] + [jnp.zeros((8, F - LANES), jnp.float32)], 1)
+        extras[o] = jnp.where(iota((8, F), 0) < 4, mine_x, listed).astype(jnp.bfloat16)
+        return carry
+
+    lax.fori_loop(0, B, one, 0, unroll=min(B, 8))
+
+
+def index_tables(T, L, B, cap, capx, held, owners, stations, screens):
+    F = SUB // T // 2 * LANES
+    vmem = pl.BlockSpec(memory_space=pltpu.VMEM)
+    return pl.pallas_call(
+        functools.partial(index_kernel, T, L, B, cap, capx, held),
+        out_shape=(
+            jax.ShapeDtypeStruct((B * capx, L), jnp.bfloat16),
+            jax.ShapeDtypeStruct((B, 8, F), jnp.bfloat16),
+        ),
+        in_specs=[vmem] * 3,
+        out_specs=(vmem, vmem),
+        name="index",
+        cost_estimate=pl.CostEstimate(flops=10**7, bytes_accessed=10**6, transcendentals=0),
+        **PARAMS,
+    )(owners, stations, screens)
+
+
+def send_kernel(T, L, B, cap, capx, *refs):
+    terms, (hot, extras, out, rows) = refs[:-4], refs[-4:]
+    Q2 = SUB // T // 2
+    F = Q2 * LANES
     total = terms[0][0].astype(jnp.float32)
     for t in terms[1:]:
         total = total + t[0].astype(jnp.float32)
     rows[...] = total.reshape(L * Q2, LANES)
-    hot = (iota((B * capx, L), 0) == slots[...]).astype(jnp.float32).astype(jnp.bfloat16)
     for q in range(Q2):
         x = rows[pl.ds(q, L, stride=Q2), :].astype(jnp.bfloat16)
-        moved = jnp.dot(hot, x, preferred_element_type=jnp.float32).astype(jnp.bfloat16)
-        gathered[:, LANES * q : LANES * (q + 1)] = moved
-    names = ids[...].astype(jnp.bfloat16)
-    tail = capx - cap
-    F = Q2 * LANES
-    mine = screens[...].astype(jnp.float32)
-    fill = jnp.zeros((tail - 8, F), jnp.float32) if tail > 8 else None
-
-    def one(o, carry):
-        start = pl.multiple_of(o * capx, 8)
-        wanted = iota((LANES, L), 0) + o * capx
-        own = (wanted == slots[...]).astype(jnp.float32).astype(jnp.bfloat16)
-        listed = lax.dot_general(names, own, (((1,), (1,)), ((), ())), preferred_element_type=jnp.float32)
-        listed = jnp.concatenate([listed] + [jnp.zeros((8, F - LANES), jnp.float32)], 1)
-        extra = jnp.where(iota((8, F), 0) < held, mine, listed)
-        if fill is not None:
-            extra = jnp.concatenate([extra, fill], 0)
-        block = jnp.concatenate([gathered[pl.ds(start, capx), :][:cap].astype(jnp.float32), extra], 0)
-        out[o] = block.astype(jnp.bfloat16)
-        return carry
-
-    lax.fori_loop(0, B, one, 0)
-
-
-def send_blocks(T, L, B, cap, capx, held, terms, slots, ids, screens):
+        moved = jnp.dot(hot[...], x, preferred_element_type=jnp.float32).astype(jnp.bfloat16)
+        out[:, :, LANES * q : LANES * (q + 1)] = moved.reshape(B, capx, LANES)
+    out[:, cap : cap + 8, :] = extras[...]
+
+
+def send_blocks(T, L, B, cap, capx, terms, hot, extras):
     Q2 = SUB // T // 2
     F = Q2 * LANES
     first = pl.BlockSpec((1, L, Q2, LANES), lambda i: (0, 0, 0, 0))
-    whole2 = lambda x: pl.BlockSpec(x.shape, lambda i: (0, 0))
     return pl.pallas_call(
-        functools.partial(send_kernel, T, L, B, cap, capx, held),
+        functools.partial(send_kernel, T, L, B, cap, capx),
         grid=(1,),
         out_shape=jax.ShapeDtypeStruct((B, capx, F), jnp.bfloat16),
-        in_specs=[first] * len(terms) + [whole2(slots), whole2(ids), whole2(screens)],
+        in_specs=[first] * len(terms)
+        + [pl.BlockSpec((B * capx, L), lambda i: (0, 0)), pl.BlockSpec((B, 8, F), lambda i: (0, 0, 0))],
         out_specs=pl.BlockSpec((B, capx, F), lambda i: (0, 0, 0)),
-        scratch_shapes=[pltpu.VMEM((L * Q2, LANES), jnp.float32), pltpu.VMEM((B * capx, F), jnp.bfloat16)],
+        scratch_shapes=[pltpu.VMEM((L * Q2, LANES), jnp.float32)],
         name="send",
         **PARAMS,
-    )(*terms, slots, ids, screens)
+    )(*terms, hot, extras)
 
 
 def place_kernel(T, B, cap, capx, held, blocks, col_off, row_off, weights, keep, send, data, gains, hot, spread, rows):
@@ -225,7 +291,7 @@
         gains[at, F : 2 * F] = jnp.where(part_f == 1, x, pltpu.roll(x, F - SUB, 1))
         same = iota((cap, LANES), 0) == iota((cap, LANES), 1)
         for k in range(2):
-            number = x[held + 2 * k : held + 2 * k + 1, 0:LANES] * 8.0 + x[held + 2 * k + 1 : held + 2 * k + 2, 0:LANES]
+            number = x[4 + 2 * k : 5 + 2 * k, 0:LANES] * 8.0 + x[5 + 2 * k : 6 + 2 * k, 0:LANES]
             number = jnp.sum(jnp.where(same, jnp.broadcast_to(number, (cap, LANES)), 0.0), axis=1, keepdims=True)
             hit = number.astype(jnp.int32) == iota((cap, NX), 1)
             hot[k, pl.ds(b * cap, cap), :] = hit.astype(jnp.float32)
@@ -323,23 +389,24 @@
     return jnp.asarray(out.reshape(2 * LANES, 4 * LANES), jnp.float32).astype(jnp.bfloat16)
 
 
-def halve(T, keep, send):
+def halve(T, keep, send, late=()):
     swap = lambda x, d: lax.ppermute(x, "tm", [(i, i ^ d) for i in range(T)])
     terms, d = [keep, swap(send, 1)], 2
     while d < T:
         half = T // d // 2
         moving = sum(t[half : 2 * half].astype(jnp.float32) for t in terms).astype(jnp.bfloat16)
+        if late and d == 2:
+            moving, *late = lax.optimization_barrier((moving, *late))
         terms.append(swap(moving, d))
         d *= 2
-    return terms
+    return terms, late
 
 
 def per_device(visibilities, coords, counts, stations, owners, offsets, screens):
     T, B = lax.axis_size("tm"), lax.axis_size("base")
     L, slots = visibilities.shape[1], visibilities.shape[3]
-    a, base = lax.axis_index("tm"), lax.axis_index("base")
-    Q, Q2 = SUB // T, SUB // T // 2
-    F = Q2 * LANES
+    base = lax.axis_index("base")
+    Q2 = SUB // T // 2
     held = screens.shape[0]
     cap = -(-max(2, 3 * L // (2 * B)) // 8) * 8
     capx = cap + 8
@@ -348,23 +415,15 @@
         return x.reshape(L, 2, slots // LANES, LANES).transpose(0, 2, 1, 3).reshape(4 * L, LANES)
 
     keep, send = images(T, L, counts, offsets.T, flat(coords[0]), flat(visibilities[0]))
-
-    owner = owners[:, 0].reshape(B, L)
-    mine = lax.dynamic_slice_in_dim(owner, base, 1, 0)[0]
+    terms, late = halve(T, keep, send, (owners, stations, screens))
+    owner = late[0][:, 0].reshape(B, L)
+    hot, extras = index_tables(T, L, B, cap, capx, held, owner, late[1].T, late[2])
+    outgoing = send_blocks(T, L, B, cap, capx, terms, hot, extras)
+    outgoing, owners, offsets = lax.optimization_barrier((outgoing, owners, offsets))
+
+    to_me = owners[:, 0].reshape(B, L) == base
     order = jnp.arange(L, dtype=jnp.int32)
     earlier = order[:, None] < order[None, :]
-    rank = jnp.sum(((mine[:, None] == mine[None, :]) & earlier).astype(jnp.int32), axis=0)
-    slot_ids = (mine * capx + rank)[None, :]
-    names = jnp.stack([stations[:, 0] // held, stations[:, 0] % held, stations[:, 1] // held, stations[:, 1] % held])
-    names = jnp.concatenate([jnp.zeros((8 - 4, L), jnp.float32), names.astype(jnp.float32)], 0)
-
-    pixels = screens.reshape(held, 2, Q, T, SUB)
-    pixels = lax.dynamic_slice_in_dim(pixels, a, 1, 3)[:, :, :, 0]
-    pixels = jnp.concatenate([pixels[..., SUB // 2 :], pixels[..., : SUB // 2][..., ::-1]], -1)
-    pixels = pixels.reshape(held, 2, 2, Q2, SUB).transpose(0, 3, 2, 1, 4).reshape(held, F)
-    pixels = jnp.concatenate([pixels, jnp.zeros((8 - held, F), pixels.dtype)], 0)
-
-    to_me = (owner == base)
     before = jnp.sum((to_me[:, :, None] & earlier[None]).astype(jnp.int32), axis=1)
     chosen = to_me[:, None, :] & (before[:, None, :] == jnp.arange(cap, dtype=jnp.int32)[None, :, None])
     offs = offsets.T.reshape(2, B, 1, L)
@@ -372,11 +431,10 @@
     col_off = slot_offs[1][:, None]
     row_off = jnp.tile(slot_offs[0], 2 * Q2)[None, :]
 
-    terms = halve(T, keep, send)
-    outgoing = send_blocks(T, L, B, cap, capx, held, terms, slot_ids, names, pixels)
     incoming = lax.all_to_all(outgoing, "base", split_axis=0, concat_axis=0, tiled=True)
     keep, send = place_blocks(T, B, cap, capx, held, incoming, col_off, row_off, transform_weights())
-    tile = sum(t[0].astype(jnp.float32) for t in halve(T, keep, send))
+    terms, _ = halve(T, keep, send)
+    tile = sum(t[0].astype(jnp.float32) for t in terms)
     return tile.reshape(1, TILE // T, 2, TILE)
 
 

time: 51.2 us -> 43 us (0.84)
  Pallas kernels: 16.8 us -> 10.2 us
  local copies, waits for them, and re-layouts: 6.49 us -> 4.88 us
    pallas_call x1, Pallas kernels: 12.5 us -> 6.58 us  [images(): pl.pallas_call(functools.partial(images_kernel, T, L), out_shape=(half, h...]
    unnamed x20 -> x19, local copies, waits for them, and re-layouts: 5.07 us -> 3.88 us
    pallas_call x1 -> x2, Pallas kernels: 2.23 us -> 1.51 us  [the longest x1 1.03 us: send_blocks(): pl.pallas_call(functools.partial(send_kernel, T, L, B, cap, capx), grid=(...]
    ppermute x4, waiting for transfers between devices: 7.26 us -> 7.85 us  [halve(): swap = lambda x, d: lax.ppermute(x, 'tm', [(i, i ^ d) for i in range(T)])]
    all_to_all x1, waiting for transfers between devices: 8.13 us -> 7.62 us  [per_device(): lax.all_to_all(outgoing, 'base', split_axis=0, concat_axis=0, tiled=True)]
  transfers between devices with their start and end apart: 5 -> 5, of which waited for: 4 -> 5; matrix products, arithmetic and copies ran while one was open for 3% -> 2% of each run, Pallas kernels for 0% -> 1%
where the time goes in v2:
time: 43 us; the launch traced here: 42.7 us
  waiting for transfers between devices  15.5 us (36%)
  starting transfers between devices  11.3 us (26%)
  Pallas kernels  10.2 us (24%)
  local copies, waits for them, and re-layouts  4.88 us (11%)
  other arithmetic  0.74 us (2%)
    ppermute x4, waiting for transfers between devices, halve(): swap = lambda x, d: lax.ppermute(x, 'tm', [(i, i ^ d) for i in range(T)])  7.85 us
    all_to_all x1, waiting for transfers between devices, per_device(): lax.all_to_all(outgoing, 'base', split_axis=0, concat_axis=0, tiled=True)  7.62 us
    pallas_call x1, Pallas kernels, images(): pl.pallas_call(functools.partial(images_kernel, T, L), out_shape=(half, h...  6.58 us
    all_to_all x1, starting transfers between devices, per_device(): lax.all_to_all(outgoing, 'base', split_axis=0, concat_axis=0, tiled=True)  6.15 us
    ppermute x4, starting transfers between devices, halve(): swap = lambda x, d: lax.ppermute(x, 'tm', [(i, i ^ d) for i in range(T)])  5.14 us
    unnamed x19, local copies, waits for them, and re-layouts  3.88 us
    pallas_call x1, Pallas kernels, place_blocks(): pl.pallas_call(functools.partial(place_kernel, T, B, cap, capx, held), ou...  2.1 us
    pallas_call x1, Pallas kernels, send_blocks(): pl.pallas_call(functools.partial(send_kernel, T, L, B, cap, capx), grid=(...  1.03 us
  transfers between devices with their start and end apart: 5, of which 5 were waited for; matrix products, arithmetic and copies ran while one was open for 2% of the time, Pallas kernels for 1%

profile of v2, /device:TPU:0, one launch (start us, length us, event | category | flops | bytes accessed | tf_op | source)
XLA Modules:
  0.0 42.7 jit_solution(15852108524014631187)
XLA Ops:
  0.0 0.0 copy-start.6
  0.0 0.7 %copy-done.6 = s32[1,128]{1,0:T(1,128)S(1)} copy-done((s32[1,128]{1,0:T(1,128)S(1)}, s32[1,128]{1,0:T(1,128)}, u32[]{:S(2)}) %copy-start.6) | copy-done | bytes 536
  0.7 0.0 copy-start
  0.7 0.9 %copy-done = f32[1,128,2,256]{3,2,1,0:T(2,128)S(1)} copy-done((f32[1,128,2,256]{3,2,1,0:T(2,128)S(1)}, f32[1,128,2,256]{3,2,1,0:T(2,128)}, u32[]{:S(2)}) %copy-start) | copy-done | bytes 262168
  1.6 0.0 copy-start.2
  1.6 0.9 %copy-done.2 = bf16[1,128,2,256]{3,2,1,0:T(2,128)(2,1)S(1)} copy-done((bf16[1,128,2,256]{3,2,1,0:T(2,128)(2,1)S(1)}, bf16[1,128,2,256]{3,2,1,0:T(2,128)(2,1)}, u32[]{:S(2)}) %copy-start.2) | copy-done | bytes 131096
  2.5 0.0 copy-start.3
  2.5 0.7 %copy-done.3 = s32[1024,2]{0,1:T(2,128)S(1)} copy-done((s32[1024,2]{0,1:T(2,128)S(1)}, s32[1024,2]{0,1:T(2,128)}, u32[]{:S(2)}) %copy-start.3) | copy-done | bytes 8216
  3.2 6.6 %images.1 = (bf16[2,128,4,128]{3,2,1,0:T(4,128)(2,1)S(1)}, bf16[2,128,4,128]{3,2,1,0:T(4,128)(2,1)S(1)}) custom-call(s32[1,128]{1,0:T(1,128)S(1)} %copy-done.6, s32[2,1024]{1,0:T(2,128)S(1)} %bitcast.21, f32[512,128]{1,0:T(8,128)S(1)} %bitcast.19, bf16[512,128]{1,0:T(8,128)(2,1)S(1)} %bitcast.20), custom_call_target="tpu_custom_call" | custom-call | tf_op jit(solution)/shard_map/images/pallas_call | solution.py:178
  9.8 0.5 %collective-permute-start = (bf16[2,128,4,128]{3,2,1,0:T(4,128)(2,1)S(1)}, bf16[2,128,4,128]{3,2,1,0:T(4,128)(2,1)S(1)}, u32[]{:S(2)}, u32[]{:S(2)}) collective-permute-start(bf16[2,128,4,128]{3,2,1,0:T(4,128)(2,1)S(1)} %get-tuple-element.19), channel_id=1, source_target_pairs={{0,1},{1,0},{2,3},{3,2},{4,5},{5,4},{6,7},{7,6},{8,9},{9,8},{10,11... | collective-permute-start | bytes 786440 | tf_op jit(solution)/shard_map/ppermute | solution.py:393
  10.3 1.2 %collective-permute-done.refs_1_ = bf16[2,128,4,128]{3,2,1,0:T(4,128)(2,1)S(1)} collective-permute-done((bf16[2,128,4,128]{3,2,1,0:T(4,128)(2,1)S(1)}, bf16[2,128,4,128]{3,2,1,0:T(4,128)(2,1)S(1)}, u32[]{:S(2)}, u32[]{:S(2)}) %collective-permute-start) | collective-permute-done | bytes 262176 | tf_op jit(solution)/shard_map/ppermute | solution.py:393
  11.5 0.1 add_convert_fusion
  11.6 0.0 copy-start.7
  11.6 3.0 %collective-permute-start.1 = (bf16[1,128,4,128]{3,2,1,0:T(4,128)(2,1)S(1)}, bf16[1,128,4,128]{3,2,1,0:T(4,128)(2,1)S(1)}, u32[]{:S(2)}, u32[]{:S(2)}) collective-permute-start(bf16[1,128,4,128]{3,2,1,0:T(4,128)(2,1)S(1)} %add_convert_fusion), channel_id=1, source_target_pairs={{0,2},{1,3},{2,0},{3,1},{4,6},{5,7},{6,4},{7,5},{8,10},{9,11},{10,... | collective-permute-start | bytes 393224 | tf_op jit(solution)/shard_map/ppermute | solution.py:393
  14.5 0.0 copy-start.5
  14.5 0.0 copy-start.8
  14.6 0.0 copy-done.7
  14.6 0.6 %copy-done.5 = s32[1024,1]{0,1:T(1,128)S(1)} copy-done((s32[1024,1]{0,1:T(1,128)S(1)}, s32[1024,1]{0,1:T(1,128)}, u32[]{:S(2)}) %copy-start.5) | copy-done | bytes 4120
  15.2 0.0 copy-done.8
  15.2 0.5 %index.1 = (bf16[256,128]{1,0:T(8,128)(2,1)S(1)}, bf16[8,8,512]{2,1,0:T(8,128)(2,1)S(1)}) custom-call(s32[8,128]{1,0:T(8,128)S(1)} %bitcast.23, s32[2,128]{1,0:T(2,128)S(1)} %bitcast.24, bf16[4,2,1024]{2,1,0:T(2,128)(2,1)S(1)} %copy-done.7), custom_call_target="tpu_custom_call" | custom-call | flops 10000000 | bytes 1000000 | tf_op jit(solution)/shard_map/index/pallas_call | solution.py:231
  15.7 2.6 %collective-permute-done.1.refs_2_ = bf16[1,128,4,128]{3,2,1,0:T(4,128)(2,1)S(1)} collective-permute-done((bf16[1,128,4,128]{3,2,1,0:T(4,128)(2,1)S(1)}, bf16[1,128,4,128]{3,2,1,0:T(4,128)(2,1)S(1)}, u32[]{:S(2)}, u32[]{:S(2)}) %collective-permute-start.1) | collective-permute-done | bytes 131104 | tf_op jit(solution)/shard_map/ppermute | solution.py:393
  18.3 0.0 copy-start.4
  18.3 1.0 %send.1 = bf16[8,32,512]{2,1,0:T(8,128)(2,1)} custom-call(bf16[2,128,4,128]{3,2,1,0:T(4,128)(2,1)S(1)} %get-tuple-element.18.refs_0_, bf16[2,128,4,128]{3,2,1,0:T(4,128)(2,1)S(1)} %collective-permute-done.refs_1_, bf16[1,128,4,128]{3,2,1,0:T(4,128)(2,1)S(1)} %collective-permute-done.1.refs_2_, bf16[256,128]{1,0:T(8,128)(2,1)S(1)} %get-tuple-element.24.refs_3_, ...), custom_call_target="tpu_custom_call" | custom-call | tf_op jit(solution)/shard_map/send/pallas_call | solution.py:264
  19.4 0.0 copy-done.4
  19.4 0.0 copy-start.1
  19.4 6.2 %all-to-all-start = ((bf16[8,32,512]{2,1,0:T(8,128)(2,1)}), bf16[8,32,512]{2,1,0:T(8,128)(2,1)S(1)}, u32[]{:S(2)}, u32[]{:S(2)}) async-start(bf16[8,32,512]{2,1,0:T(8,128)(2,1)} %send.1), calls=%async_computation | async-start | bytes 524288 | tf_op jit(solution)/shard_map/all_to_all | solution.py:434
  25.5 0.2 convert_reduce_fusion
  25.8 0.3 select_reduce_fusion
  26.2 0.1 broadcast_in_dim_squeeze.4.col_off
  26.3 0.1 tile.7
  26.3 0.1 broadcast_in_dim_tile.3.row_off
  26.4 7.6 %all-to-all-done.blocks = bf16[8,32,512]{2,1,0:T(8,128)(2,1)S(1)} async-done(((bf16[8,32,512]{2,1,0:T(8,128)(2,1)}), bf16[8,32,512]{2,1,0:T(8,128)(2,1)S(1)}, u32[]{:S(2)}, u32[]{:S(2)}) %all-to-all-start) | async-done | bytes 262176 | tf_op jit(solution)/shard_map/all_to_all | solution.py:434
  34.0 0.0 copy-done.1
  34.0 2.1 %place.1 = (f32[2,64,512]{2,1,0:T(8,128)S(1)}, bf16[2,64,512]{2,1,0:T(8,128)(2,1)S(1)}) custom-call(bf16[8,32,512]{2,1,0:T(8,128)(2,1)S(1)} %all-to-all-done.blocks, s32[192,1]{1,0:T(8,128)S(1)} %broadcast_in_dim_squeeze.4.col_off, s32[1,1536]{1,0:T(1,128)S(1)} %broadcast_in_dim_tile.3.row_off, bf16[256,512]{1,0:T(8,128)(2,1)S(1)} %copy-done.1), custom_call_target="tpu_custom_call" | custom-call | tf_op jit(solution)/shard_map/place/pallas_call | solution.py:358
  36.2 0.1 collective-permute-start.2
  36.2 1.3 %collective-permute-done.2 = bf16[2,64,512]{2,1,0:T(8,128)(2,1)S(1)} collective-permute-done((bf16[2,64,512]{2,1,0:T(8,128)(2,1)S(1)}, bf16[2,64,512]{2,1,0:T(8,128)(2,1)S(1)}, u32[]{:S(2)}, u32[]{:S(2)}) %collective-permute-start.2) | collective-permute-done | bytes 131104 | tf_op jit(solution)/shard_map/ppermute | solution.py:393
  37.6 1.6 %collective-permute-start.3 = (bf16[1,64,512]{2,1,0:T(8,128)(2,1)S(1)}, bf16[1,64,512]{2,1,0:T(8,128)(2,1)S(1)}, u32[]{:S(2)}, u32[]{:S(2)}) collective-permute-start(bf16[1,64,512]{2,1,0:T(8,128)(2,1)S(1)} %add_convert_fusion.1), channel_id=1, source_target_pairs={{0,2},{1,3},{2,0},{3,1},{4,6},{5,7},{6,4},{7,5},{8,10},{9,11},{10,... | collective-permute-start | bytes 196616 | tf_op jit(solution)/shard_map/ppermute | solution.py:393
  39.2 2.7 %collective-permute-done.3 = bf16[1,64,512]{2,1,0:T(8,128)(2,1)S(1)} collective-permute-done((bf16[1,64,512]{2,1,0:T(8,128)(2,1)S(1)}, bf16[1,64,512]{2,1,0:T(8,128)(2,1)S(1)}, u32[]{:S(2)}, u32[]{:S(2)}) %collective-permute-start.3) | collective-permute-done | bytes 65568 | tf_op jit(solution)/shard_map/ppermute | solution.py:393
  41.9 0.7 %add.34 = f32[1,64,2,256]{3,2,1,0:T(2,128)} reshape(f32[1,64,512]{2,1,0:T(8,128)S(1)} %convert_add_fusion) | data formatting | bytes 262144 | tf_op jit(solution)/shard_map/add | solution.py:437
  (8 shorter events, 0.1 us)
Async XLA Ops:
  0.0 0.7 %copy-start.6 = (s32[1,128]{1,0:T(1,128)S(1)}, s32[1,128]{1,0:T(1,128)}, u32[]{:S(2)}) copy-start(s32[1,128]{1,0:T(1,128)} %in_counts.1) | copy-start | bytes 1540
  0.7 0.9 %copy-start = (f32[1,128,2,256]{3,2,1,0:T(2,128)S(1)}, f32[1,128,2,256]{3,2,1,0:T(2,128)}, u32[]{:S(2)}) copy-start(f32[1,128,2,256]{3,2,1,0:T(2,128)} %param.9) | copy-start | bytes 786436
  1.6 0.9 %copy-start.2 = (bf16[1,128,2,256]{3,2,1,0:T(2,128)(2,1)S(1)}, bf16[1,128,2,256]{3,2,1,0:T(2,128)(2,1)}, u32[]{:S(2)}) copy-start(bf16[1,128,2,256]{3,2,1,0:T(2,128)(2,1)} %param.8) | copy-start | bytes 393220
  2.5 0.7 %copy-start.3 = (s32[1024,2]{0,1:T(2,128)S(1)}, s32[1024,2]{0,1:T(2,128)}, u32[]{:S(2)}) copy-start(s32[1024,2]{0,1:T(2,128)} %param.13) | copy-start | bytes 24580
  9.8 1.7 %collective-permute-start = (bf16[2,128,4,128]{3,2,1,0:T(4,128)(2,1)S(1)}, bf16[2,128,4,128]{3,2,1,0:T(4,128)(2,1)S(1)}, u32[]{:S(2)}, u32[]{:S(2)}) collective-permute-start(bf16[2,128,4,128]{3,2,1,0:T(4,128)(2,1)S(1)} %get-tuple-element.19), channel_id=1, source_target_pairs={{0,1},{1,0},{2,3},{3,2},{4,5},{5,4},{6,7},{7,6},{8,9},{9,8},{10,11... | collective-permute-start | bytes 786440 | tf_op jit(solution)/shard_map/ppermute | solution.py:393
  11.6 3.0 %copy-start.7 = (bf16[4,2,1024]{2,1,0:T(2,128)(2,1)S(1)}, bf16[4,2,1024]{2,1,0:T(2,128)(2,1)}, u32[]{:S(2)}) copy-start(bf16[4,2,1024]{2,1,0:T(2,128)(2,1)} %screens) | copy-start | bytes 49156
  11.6 6.7 %collective-permute-start.1 = (bf16[1,128,4,128]{3,2,1,0:T(4,128)(2,1)S(1)}, bf16[1,128,4,128]{3,2,1,0:T(4,128)(2,1)S(1)}, u32[]{:S(2)}, u32[]{:S(2)}) collective-permute-start(bf16[1,128,4,128]{3,2,1,0:T(4,128)(2,1)S(1)} %add_convert_fusion), channel_id=1, source_target_pairs={{0,2},{1,3},{2,0},{3,1},{4,6},{5,7},{6,4},{7,5},{8,10},{9,11},{10,... | collective-permute-start | bytes 393224 | tf_op jit(solution)/shard_map/ppermute | solution.py:393
  14.5 0.7 %copy-start.5 = (s32[1024,1]{0,1:T(1,128)S(1)}, s32[1024,1]{0,1:T(1,128)}, u32[]{:S(2)}) copy-start(s32[1024,1]{0,1:T(1,128)} %param.12) | copy-start | bytes 12292
  14.5 0.7 %copy-start.8 = (s32[128,2]{0,1:T(2,128)S(1)}, s32[128,2]{0,1:T(2,128)}, u32[]{:S(2)}) copy-start(s32[128,2]{0,1:T(2,128)} %param.11) | copy-start | bytes 3076
  18.3 1.0 %copy-start.4 = (s32[1024,2]{0,1:T(2,128)S(1)}, s32[1024,2]{0,1:T(2,128)}, u32[]{:S(2)}) copy-start(s32[1024,2]{0,1:T(2,128)} %param.13) | copy-start | bytes 24580
  19.4 14.7 %copy-start.1 = (bf16[256,512]{1,0:T(8,128)(2,1)S(1)}, bf16[256,512]{1,0:T(8,128)(2,1)}, u32[]{:S(2)}) copy-start(bf16[256,512]{1,0:T(8,128)(2,1)} %constant.15.weights) | copy-start | bytes 786436
  19.4 14.7 %all-to-all-start = ((bf16[8,32,512]{2,1,0:T(8,128)(2,1)}), bf16[8,32,512]{2,1,0:T(8,128)(2,1)S(1)}, u32[]{:S(2)}, u32[]{:S(2)}) async-start(bf16[8,32,512]{2,1,0:T(8,128)(2,1)} %send.1), calls=%async_computation | async-start | bytes 524288 | tf_op jit(solution)/shard_map/all_to_all | solution.py:434
  36.2 1.4 %collective-permute-start.2 = (bf16[2,64,512]{2,1,0:T(8,128)(2,1)S(1)}, bf16[2,64,512]{2,1,0:T(8,128)(2,1)S(1)}, u32[]{:S(2)}, u32[]{:S(2)}) collective-permute-start(bf16[2,64,512]{2,1,0:T(8,128)(2,1)S(1)} %get-tuple-element.30), channel_id=1, source_target_pairs={{0,1},{1,0},{2,3},{3,2},{4,5},{5,4},{6,7},{7,6},{8,9},{9,8},{10,11... | collective-permute-start | bytes 393224 | tf_op jit(solution)/shard_map/ppermute | solution.py:393
  37.6 4.3 %collective-permute-start.3 = (bf16[1,64,512]{2,1,0:T(8,128)(2,1)S(1)}, bf16[1,64,512]{2,1,0:T(8,128)(2,1)S(1)}, u32[]{:S(2)}, u32[]{:S(2)}) collective-permute-start(bf16[1,64,512]{2,1,0:T(8,128)(2,1)S(1)} %add_convert_fusion.1), channel_id=1, source_target_pairs={{0,2},{1,3},{2,0},{3,1},{4,6},{5,7},{6,4},{7,5},{8,10},{9,11},{10,... | collective-permute-start | bytes 196616 | tf_op jit(solution)/shard_map/ppermute | solution.py:393

commit v3 on v2

--- a/solution.py
+++ b/solution.py
@@ -168,7 +168,7 @@
                 ref[place, s + 1] = y[k * Q : k * Q + Q2]
         return carry
 
-    lax.fori_loop(0, L // 2, two, 0, unroll=16)
+    lax.fori_loop(0, L // 2, two, 0, unroll=32)
 
 
 def images(T, L, counts, offsets, coords, vis):
@@ -189,7 +189,7 @@
         ],
         name="images",
         **PARAMS,
-    )(counts, offsets, coords, vis)
+    )(*[pltpu.with_memory_space_constraint(x, pltpu.HBM) for x in (counts, offsets, coords, vis)])
 
 
 def index_kernel(T, L, B, cap, capx, held, owners, stations, screens, hot, extras):
@@ -260,21 +260,57 @@
 def send_blocks(T, L, B, cap, capx, terms, hot, extras):
     Q2 = SUB // T // 2
     F = Q2 * LANES
-    first = pl.BlockSpec((1, L, Q2, LANES), lambda i: (0, 0, 0, 0))
+    vmem = pl.BlockSpec(memory_space=pltpu.VMEM)
     return pl.pallas_call(
         functools.partial(send_kernel, T, L, B, cap, capx),
-        grid=(1,),
         out_shape=jax.ShapeDtypeStruct((B, capx, F), jnp.bfloat16),
-        in_specs=[first] * len(terms)
-        + [pl.BlockSpec((B * capx, L), lambda i: (0, 0)), pl.BlockSpec((B, 8, F), lambda i: (0, 0, 0))],
-        out_specs=pl.BlockSpec((B, capx, F), lambda i: (0, 0, 0)),
+        in_specs=[vmem] * (len(terms) + 2),
+        out_specs=vmem,
         scratch_shapes=[pltpu.VMEM((L * Q2, LANES), jnp.float32)],
         name="send",
         **PARAMS,
     )(*terms, hot, extras)
 
 
-def place_kernel(T, B, cap, capx, held, blocks, col_off, row_off, weights, keep, send, data, gains, hot, spread, rows):
+def rows_kernel(T, S, row_off, rows):
+    Q2 = SUB // T // 2
+    K = 2 * Q2 * S
+    chunk, half = TILE // T, TILE // 2
+    a = lax.axis_index("tm")
+    index = iota((1, K), 1) // S
+    m = (T * ((index % 2) * Q2 + index // 2) + a).astype(jnp.float32) * (1.0 / SUB)
+    er, ei = turn(iota((SUB, K), 0).astype(jnp.float32) * m)
+    for d in range(T):
+        for e in range(chunk // SUB):
+            r = (a ^ d) * chunk + e * SUB + iota((SUB, K), 0) - row_off[...]
+            mask = (r >= 0) & (r < SUB)
+            at = bit_reverse(d // 2, T // 2) * chunk + e * SUB
+            rows[d % 2, at : at + SUB, :] = jnp.where(mask, er, 0.0).astype(jnp.bfloat16)
+            rows[d % 2, half + at : half + at + SUB, :] = jnp.where(mask, ei, 0.0).astype(jnp.bfloat16)
+
+
+def row_tables(T, S, row_off):
+    K = SUB // T * S
+    vmem = pl.BlockSpec(memory_space=pltpu.VMEM)
+    return pl.pallas_call(
+        functools.partial(rows_kernel, T, S),
+        out_shape=jax.ShapeDtypeStruct((2, TILE, K), jnp.bfloat16),
+        in_specs=[vmem],
+        out_specs=vmem,
+        name="rows",
+        cost_estimate=pl.CostEstimate(flops=10**7, bytes_accessed=10**6, transcendentals=0),
+        **PARAMS,
+    )(row_off)
+
+
+def tile_part(T, rows, spread):
+    both = jnp.dot(rows, spread, preferred_element_type=jnp.float32)
+    u, v = both[: TILE // 2], both[TILE // 2 :]
+    tile = jnp.concatenate([u[:, :TILE] + v[:, TILE:], u[:, TILE:] - v[:, :TILE]], 1)
+    return tile.reshape(T // 2, TILE // T, 2 * TILE)
+
+
+def place_kernel(T, B, cap, capx, held, blocks, col_off, rows, weights, spread, send, data, gains, hot):
     Q, Q2 = SUB // T, SUB // T // 2
     F = Q2 * LANES
     S = B * cap
@@ -328,38 +364,18 @@
                         inside[half], v, 0.0
                     ).astype(jnp.bfloat16)
 
-    K = 2 * Q2 * S
-    chunk = TILE // T
-    index = iota((1, K), 1) // S
-    m = (T * ((index % 2) * Q2 + index // 2) + a).astype(jnp.float32) * (1.0 / SUB)
-    er, ei = turn(iota((SUB, K), 0).astype(jnp.float32) * m)
-    for d in range(T):
-        for e in range(chunk // SUB):
-            r = (a ^ d) * chunk + e * SUB + iota((SUB, K), 0) - row_off[...]
-            mask = (r >= 0) & (r < SUB)
-            place = (d % 2) * (T // 2) + bit_reverse(d // 2, T // 2)
-            at = place * chunk + e * SUB
-            rows[at : at + SUB, :] = jnp.where(mask, er, 0.0).astype(jnp.bfloat16)
-            rows[TILE + at : TILE + at + SUB, :] = jnp.where(mask, ei, 0.0).astype(jnp.bfloat16)
-    both = jnp.dot(rows[...], spread[...], preferred_element_type=jnp.float32)
-    u, v = both[:TILE], both[TILE:]
-    tile = jnp.concatenate([u[:, :TILE] + v[:, TILE:], u[:, TILE:] - v[:, :TILE]], 1)
-    for i in range(T // 2):
-        keep[i] = tile[i * chunk : (i + 1) * chunk]
-        j = T // 2 + i
-        send[i] = tile[j * chunk : (j + 1) * chunk].astype(jnp.bfloat16)
-
-
-def place_blocks(T, B, cap, capx, held, blocks, col_off, row_off, weights):
+    send[...] = tile_part(T, rows[1], spread[...]).astype(jnp.bfloat16)
+
+
+def place_blocks(T, B, cap, capx, held, blocks, col_off, rows, weights):
     Q2 = SUB // T // 2
     F, S, K = Q2 * LANES, B * cap, 2 * Q2 * B * cap
     vmem = pl.BlockSpec(memory_space=pltpu.VMEM)
-    chunk = TILE // T
     return pl.pallas_call(
         functools.partial(place_kernel, T, B, cap, capx, held),
         out_shape=(
-            jax.ShapeDtypeStruct((T // 2, chunk, 2 * TILE), jnp.float32),
-            jax.ShapeDtypeStruct((T // 2, chunk, 2 * TILE), jnp.bfloat16),
+            jax.ShapeDtypeStruct((K, 2 * TILE), jnp.bfloat16),
+            jax.ShapeDtypeStruct((T // 2, TILE // T, 2 * TILE), jnp.bfloat16),
         ),
         in_specs=[vmem] * 4,
         out_specs=(vmem, vmem),
@@ -367,12 +383,27 @@
             pltpu.VMEM((S, F), jnp.float32),
             pltpu.VMEM((B * 8, 2 * F), jnp.float32),
             pltpu.VMEM((2, S, B * 8), jnp.float32),
-            pltpu.VMEM((K, 2 * TILE), jnp.bfloat16),
-            pltpu.VMEM((2 * TILE, K), jnp.bfloat16),
         ],
         name="place",
         **PARAMS,
-    )(blocks, col_off, row_off, weights)
+    )(blocks, col_off, rows, weights)
+
+
+def keep_kernel(T, rows, spread, keep):
+    keep[...] = tile_part(T, rows[0], spread[...])
+
+
+def kept_rows(T, rows, spread):
+    vmem = pl.BlockSpec(memory_space=pltpu.VMEM)
+    return pl.pallas_call(
+        functools.partial(keep_kernel, T),
+        out_shape=jax.ShapeDtypeStruct((T // 2, TILE // T, 2 * TILE), jnp.float32),
+        in_specs=[vmem] * 2,
+        out_specs=vmem,
+        name="keep",
+        cost_estimate=pl.CostEstimate(flops=10**8, bytes_accessed=10**6, transcendentals=0),
+        **PARAMS,
+    )(rows, spread)
 
 
 def transform_weights():
@@ -432,8 +463,9 @@
     row_off = jnp.tile(slot_offs[0], 2 * Q2)[None, :]
 
     incoming = lax.all_to_all(outgoing, "base", split_axis=0, concat_axis=0, tiled=True)
-    keep, send = place_blocks(T, B, cap, capx, held, incoming, col_off, row_off, transform_weights())
-    terms, _ = halve(T, keep, send)
+    rows = row_tables(T, B * cap, row_off)
+    spread, send = place_blocks(T, B, cap, capx, held, incoming, col_off, rows, transform_weights())
+    terms, _ = halve(T, kept_rows(T, rows, spread), send)
     tile = sum(t[0].astype(jnp.float32) for t in terms)
     return tile.reshape(1, TILE // T, 2, TILE)
 

time: 43 us -> 39.3 us (0.914)
  waiting for transfers between devices: 15.5 us -> 12.8 us
  local copies, waits for them, and re-layouts: 4.88 us -> 3.09 us
  Pallas kernels: 10.2 us -> 11 us
    ppermute x4, waiting for transfers between devices: 7.85 us -> 5.87 us  [halve(): swap = lambda x, d: lax.ppermute(x, 'tm', [(i, i ^ d) for i in range(T)])]
    unnamed x19 -> x13, local copies, waits for them, and re-layouts: 3.88 us -> 2.09 us
    pallas_call x1 -> x3, Pallas kernels: 1.03 us -> 2.22 us  [the longest x1 1.01 us: send_blocks(): pl.pallas_call(functools.partial(send_kernel, T, L, B, cap, capx), out_sh...]
    all_to_all x1, waiting for transfers between devices: 7.62 us -> 6.96 us  [per_device(): lax.all_to_all(outgoing, 'base', split_axis=0, concat_axis=0, tiled=True)]
  transfers between devices with their start and end apart: 5 -> 5, of which waited for: 5 -> 5; matrix products, arithmetic and copies ran while one was open for 2% -> 2% of each run, Pallas kernels for 1% -> 4%
where the time goes in v3:
time: 39.3 us; the launch traced here: 38.9 us
  waiting for transfers between devices  12.8 us (33%)
  starting transfers between devices  11.2 us (28%)
  Pallas kernels  11 us (28%)
  local copies, waits for them, and re-layouts  3.09 us (8%)
  other arithmetic  0.73 us (2%)
    all_to_all x1, waiting for transfers between devices, per_device(): lax.all_to_all(outgoing, 'base', split_axis=0, concat_axis=0, tiled=True)  6.96 us
    pallas_call x1, Pallas kernels, images(): pl.pallas_call(functools.partial(images_kernel, T, L), out_shape=(half, h...  6.63 us
    all_to_all x1, starting transfers between devices, per_device(): lax.all_to_all(outgoing, 'base', split_axis=0, concat_axis=0, tiled=True)  6.02 us
    ppermute x4, waiting for transfers between devices, halve(): swap = lambda x, d: lax.ppermute(x, 'tm', [(i, i ^ d) for i in range(T)])  5.87 us
    ppermute x4, starting transfers between devices, halve(): swap = lambda x, d: lax.ppermute(x, 'tm', [(i, i ^ d) for i in range(T)])  5.13 us
    unnamed x13, local copies, waits for them, and re-layouts  2.09 us
    pallas_call x1, Pallas kernels, place_blocks(): pl.pallas_call(functools.partial(place_kernel, T, B, cap, capx, held), ou...  1.68 us
    pallas_call x1, Pallas kernels, send_blocks(): pl.pallas_call(functools.partial(send_kernel, T, L, B, cap, capx), out_sh...  1.01 us
  transfers between devices with their start and end apart: 5, of which 5 were waited for; matrix products, arithmetic and copies ran while one was open for 2% of the time, Pallas kernels for 4%

profile of v3, /device:TPU:0, one launch (start us, length us, event | category | flops | bytes accessed | tf_op | source)
XLA Modules:
  0.0 38.9 jit_solution(8009553107740263324)
XLA Ops:
  0.0 0.0 copy-start.5
  0.0 0.0 copy-start.2
  0.0 6.6 %images.1 = (bf16[2,128,4,128]{3,2,1,0:T(4,128)(2,1)S(1)}, bf16[2,128,4,128]{3,2,1,0:T(4,128)(2,1)S(1)}) custom-call(s32[1,128]{1,0:T(1,128)} %in_counts.1, s32[2,1024]{1,0:T(2,128)} %bitcast.23, f32[512,128]{1,0:T(8,128)} %bitcast.21, bf16[512,128]{1,0:T(8,128)(2,1)} %bitcast.22), custom_call_target="tpu_custom_call" | custom-call | tf_op jit(solution)/shard_map/images/pallas_call | solution.py:178
  6.6 0.5 %collective-permute-start = (bf16[2,128,4,128]{3,2,1,0:T(4,128)(2,1)S(1)}, bf16[2,128,4,128]{3,2,1,0:T(4,128)(2,1)S(1)}, u32[]{:S(2)}, u32[]{:S(2)}) collective-permute-start(bf16[2,128,4,128]{3,2,1,0:T(4,128)(2,1)S(1)} %get-tuple-element.19), channel_id=1, source_target_pairs={{0,1},{1,0},{2,3},{3,2},{4,5},{5,4},{6,7},{7,6},{8,9},{9,8},{10,11... | collective-permute-start | bytes 786440 | tf_op jit(solution)/shard_map/ppermute | solution.py:424
  7.2 1.2 %collective-permute-done.refs_1_ = bf16[2,128,4,128]{3,2,1,0:T(4,128)(2,1)S(1)} collective-permute-done((bf16[2,128,4,128]{3,2,1,0:T(4,128)(2,1)S(1)}, bf16[2,128,4,128]{3,2,1,0:T(4,128)(2,1)S(1)}, u32[]{:S(2)}, u32[]{:S(2)}) %collective-permute-start) | collective-permute-done | bytes 262176 | tf_op jit(solution)/shard_map/ppermute | solution.py:424
  8.3 0.1 add_convert_fusion
  8.4 3.0 %collective-permute-start.1 = (bf16[1,128,4,128]{3,2,1,0:T(4,128)(2,1)S(1)}, bf16[1,128,4,128]{3,2,1,0:T(4,128)(2,1)S(1)}, u32[]{:S(2)}, u32[]{:S(2)}) collective-permute-start(bf16[1,128,4,128]{3,2,1,0:T(4,128)(2,1)S(1)} %add_convert_fusion), channel_id=1, source_target_pairs={{0,2},{1,3},{2,0},{3,1},{4,6},{5,7},{6,4},{7,5},{8,10},{9,11},{10,... | collective-permute-start | bytes 393224 | tf_op jit(solution)/shard_map/ppermute | solution.py:424
  11.4 0.0 copy-start.1
  11.4 0.7 %copy-done.1 = s32[1024,1]{0,1:T(1,128)S(1)} copy-done((s32[1024,1]{0,1:T(1,128)S(1)}, s32[1024,1]{0,1:T(1,128)}, u32[]{:S(2)}) %copy-start.1) | copy-done | bytes 4120
  12.1 0.0 copy-start.3
  12.1 0.7 %copy-done.3 = bf16[4,2,1024]{2,1,0:T(2,128)(2,1)S(1)} copy-done((bf16[4,2,1024]{2,1,0:T(2,128)(2,1)S(1)}, bf16[4,2,1024]{2,1,0:T(2,128)(2,1)}, u32[]{:S(2)}) %copy-start.3) | copy-done | bytes 16408
  12.8 0.0 copy-start.4
  12.8 0.7 %copy-done.4 = s32[128,2]{0,1:T(2,128)S(1)} copy-done((s32[128,2]{0,1:T(2,128)S(1)}, s32[128,2]{0,1:T(2,128)}, u32[]{:S(2)}) %copy-start.4) | copy-done | bytes 1048
  13.5 0.5 %index.1 = (bf16[256,128]{1,0:T(8,128)(2,1)S(1)}, bf16[8,8,512]{2,1,0:T(8,128)(2,1)S(1)}) custom-call(s32[8,128]{1,0:T(8,128)S(1)} %bitcast.19, s32[2,128]{1,0:T(2,128)S(1)} %bitcast.20, bf16[4,2,1024]{2,1,0:T(2,128)(2,1)S(1)} %copy-done.3), custom_call_target="tpu_custom_call" | custom-call | flops 10000000 | bytes 1000000 | tf_op jit(solution)/shard_map/index/pallas_call | solution.py:231
  13.9 1.2 %collective-permute-done.1.refs_2_ = bf16[1,128,4,128]{3,2,1,0:T(4,128)(2,1)S(1)} collective-permute-done((bf16[1,128,4,128]{3,2,1,0:T(4,128)(2,1)S(1)}, bf16[1,128,4,128]{3,2,1,0:T(4,128)(2,1)S(1)}, u32[]{:S(2)}, u32[]{:S(2)}) %collective-permute-start.1) | collective-permute-done | bytes 131104 | tf_op jit(solution)/shard_map/ppermute | solution.py:424
  15.2 0.0 copy-start
  15.2 1.0 %send.1 = bf16[8,32,512]{2,1,0:T(8,128)(2,1)} custom-call(bf16[2,128,4,128]{3,2,1,0:T(4,128)(2,1)S(1)} %get-tuple-element.18.refs_0_, bf16[2,128,4,128]{3,2,1,0:T(4,128)(2,1)S(1)} %collective-permute-done.refs_1_, bf16[1,128,4,128]{3,2,1,0:T(4,128)(2,1)S(1)} %collective-permute-done.1.refs_2_, bf16[256,128]{1,0:T(8,128)(2,1)S(1)} %get-tuple-element.24.refs_3_, ...), custom_call_target="tpu_custom_call" | custom-call | tf_op jit(solution)/shard_map/send/pallas_call | solution.py:264
  16.2 0.0 copy-done.5
  16.2 6.0 %all-to-all-start = ((bf16[8,32,512]{2,1,0:T(8,128)(2,1)}), bf16[8,32,512]{2,1,0:T(8,128)(2,1)S(1)}, u32[]{:S(2)}, u32[]{:S(2)}) async-start(bf16[8,32,512]{2,1,0:T(8,128)(2,1)} %send.1), calls=%async_computation | async-start | bytes 524288 | tf_op jit(solution)/shard_map/all_to_all | solution.py:465
  22.2 0.0 copy-done.2
  22.2 0.2 convert_reduce_fusion
  22.5 0.3 select_reduce_fusion
  22.8 0.1 tile.7
  22.9 0.1 broadcast_in_dim_tile.3.row_off
  23.0 0.1 broadcast_in_dim_squeeze.4.col_off
  23.1 0.6 %rows.1 = bf16[2,256,1536]{2,1,0:T(8,128)(2,1)S(1)} custom-call(s32[1,1536]{1,0:T(1,128)S(1)} %broadcast_in_dim_tile.3.row_off), custom_call_target="tpu_custom_call" | custom-call | flops 10000000 | bytes 1000000 | tf_op jit(solution)/shard_map/rows/pallas_call | solution.py:295
  23.8 7.0 %all-to-all-done.blocks = bf16[8,32,512]{2,1,0:T(8,128)(2,1)S(1)} async-done(((bf16[8,32,512]{2,1,0:T(8,128)(2,1)}), bf16[8,32,512]{2,1,0:T(8,128)(2,1)S(1)}, u32[]{:S(2)}, u32[]{:S(2)}) %all-to-all-start) | async-done | bytes 262176 | tf_op jit(solution)/shard_map/all_to_all | solution.py:465
  30.7 0.0 copy-done
  30.7 1.7 %place.1 = (bf16[1536,512]{1,0:T(8,128)(2,1)S(1)}, bf16[2,64,512]{2,1,0:T(8,128)(2,1)S(1)}) custom-call(bf16[8,32,512]{2,1,0:T(8,128)(2,1)S(1)} %all-to-all-done.blocks, s32[192,1]{1,0:T(8,128)S(1)} %broadcast_in_dim_squeeze.4.col_off, bf16[2,256,1536]{2,1,0:T(8,128)(2,1)S(1)} %rows.1, bf16[256,512]{1,0:T(8,128)(2,1)S(1)} %copy-done), custom_call_target="tpu_custom_call" | custom-call | tf_op jit(solution)/shard_map/place/pallas_call | solution.py:374
  32.4 0.1 collective-permute-start.2
  32.5 0.6 %keep.1 = f32[2,64,512]{2,1,0:T(8,128)S(1)} custom-call(bf16[2,256,1536]{2,1,0:T(8,128)(2,1)S(1)} %rows.1, bf16[1536,512]{1,0:T(8,128)(2,1)S(1)} %get-tuple-element.29.spread), custom_call_target="tpu_custom_call" | custom-call | flops 100000000 | bytes 1000000 | tf_op jit(solution)/shard_map/keep/pallas_call | solution.py:398
  33.1 0.8 %collective-permute-done.2 = bf16[2,64,512]{2,1,0:T(8,128)(2,1)S(1)} collective-permute-done((bf16[2,64,512]{2,1,0:T(8,128)(2,1)S(1)}, bf16[2,64,512]{2,1,0:T(8,128)(2,1)S(1)}, u32[]{:S(2)}, u32[]{:S(2)}) %collective-permute-start.2) | collective-permute-done | bytes 131104 | tf_op jit(solution)/shard_map/ppermute | solution.py:424
  33.8 1.6 %collective-permute-start.3 = (bf16[1,64,512]{2,1,0:T(8,128)(2,1)S(1)}, bf16[1,64,512]{2,1,0:T(8,128)(2,1)S(1)}, u32[]{:S(2)}, u32[]{:S(2)}) collective-permute-start(bf16[1,64,512]{2,1,0:T(8,128)(2,1)S(1)} %fusion), channel_id=1, source_target_pairs={{0,2},{1,3},{2,0},{3,1},{4,6},{5,7},{6,4},{7,5},{8,10},{9,11},{10,... | collective-permute-start | bytes 196616 | tf_op jit(solution)/shard_map/ppermute | solution.py:424
  35.4 2.7 %collective-permute-done.3 = bf16[1,64,512]{2,1,0:T(8,128)(2,1)S(1)} collective-permute-done((bf16[1,64,512]{2,1,0:T(8,128)(2,1)S(1)}, bf16[1,64,512]{2,1,0:T(8,128)(2,1)S(1)}, u32[]{:S(2)}, u32[]{:S(2)}) %collective-permute-start.3) | collective-permute-done | bytes 65568 | tf_op jit(solution)/shard_map/ppermute | solution.py:424
  38.2 0.7 %add.34 = f32[1,64,2,256]{3,2,1,0:T(2,128)} reshape(f32[1,64,512]{2,1,0:T(8,128)S(1)} %fusion.1) | data formatting | bytes 262144 | tf_op jit(solution)/shard_map/add | solution.py:469
  (8 shorter events, 0.1 us)
Async XLA Ops:
  0.0 16.2 %copy-start.5 = (s32[1024,2]{0,1:T(2,128)S(1)}, s32[1024,2]{0,1:T(2,128)}, u32[]{:S(2)}) copy-start(s32[1024,2]{0,1:T(2,128)} %param.13) | copy-start | bytes 24580
  0.0 22.2 %copy-start.2 = (s32[1024,1]{0,1:T(1,128)S(1)}, s32[1024,1]{0,1:T(1,128)}, u32[]{:S(2)}) copy-start(s32[1024,1]{0,1:T(1,128)} %param.12) | copy-start | bytes 12292
  6.6 1.7 %collective-permute-start = (bf16[2,128,4,128]{3,2,1,0:T(4,128)(2,1)S(1)}, bf16[2,128,4,128]{3,2,1,0:T(4,128)(2,1)S(1)}, u32[]{:S(2)}, u32[]{:S(2)}) collective-permute-start(bf16[2,128,4,128]{3,2,1,0:T(4,128)(2,1)S(1)} %get-tuple-element.19), channel_id=1, source_target_pairs={{0,1},{1,0},{2,3},{3,2},{4,5},{5,4},{6,7},{7,6},{8,9},{9,8},{10,11... | collective-permute-start | bytes 786440 | tf_op jit(solution)/shard_map/ppermute | solution.py:424
  8.4 6.8 %collective-permute-start.1 = (bf16[1,128,4,128]{3,2,1,0:T(4,128)(2,1)S(1)}, bf16[1,128,4,128]{3,2,1,0:T(4,128)(2,1)S(1)}, u32[]{:S(2)}, u32[]{:S(2)}) collective-permute-start(bf16[1,128,4,128]{3,2,1,0:T(4,128)(2,1)S(1)} %add_convert_fusion), channel_id=1, source_target_pairs={{0,2},{1,3},{2,0},{3,1},{4,6},{5,7},{6,4},{7,5},{8,10},{9,11},{10,... | collective-permute-start | bytes 393224 | tf_op jit(solution)/shard_map/ppermute | solution.py:424
  11.4 0.7 %copy-start.1 = (s32[1024,1]{0,1:T(1,128)S(1)}, s32[1024,1]{0,1:T(1,128)}, u32[]{:S(2)}) copy-start(s32[1024,1]{0,1:T(1,128)} %param.12) | copy-start | bytes 12292
  12.1 0.7 %copy-start.3 = (bf16[4,2,1024]{2,1,0:T(2,128)(2,1)S(1)}, bf16[4,2,1024]{2,1,0:T(2,128)(2,1)}, u32[]{:S(2)}) copy-start(bf16[4,2,1024]{2,1,0:T(2,128)(2,1)} %screens) | copy-start | bytes 49156
  12.8 0.7 %copy-start.4 = (s32[128,2]{0,1:T(2,128)S(1)}, s32[128,2]{0,1:T(2,128)}, u32[]{:S(2)}) copy-start(s32[128,2]{0,1:T(2,128)} %param.11) | copy-start | bytes 3076
  15.2 15.6 %copy-start = (bf16[256,512]{1,0:T(8,128)(2,1)S(1)}, bf16[256,512]{1,0:T(8,128)(2,1)}, u32[]{:S(2)}) copy-start(bf16[256,512]{1,0:T(8,128)(2,1)} %constant.15.weights) | copy-start | bytes 786436
  16.2 14.6 %all-to-all-start = ((bf16[8,32,512]{2,1,0:T(8,128)(2,1)}), bf16[8,32,512]{2,1,0:T(8,128)(2,1)S(1)}, u32[]{:S(2)}, u32[]{:S(2)}) async-start(bf16[8,32,512]{2,1,0:T(8,128)(2,1)} %send.1), calls=%async_computation | async-start | bytes 524288 | tf_op jit(solution)/shard_map/all_to_all | solution.py:465
  32.4 1.4 %collective-permute-start.2 = (bf16[2,64,512]{2,1,0:T(8,128)(2,1)S(1)}, bf16[2,64,512]{2,1,0:T(8,128)(2,1)S(1)}, u32[]{:S(2)}, u32[]{:S(2)}) collective-permute-start(bf16[2,64,512]{2,1,0:T(8,128)(2,1)S(1)} %get-tuple-element.30), channel_id=1, source_target_pairs={{0,1},{1,0},{2,3},{3,2},{4,5},{5,4},{6,7},{7,6},{8,9},{9,8},{10,11... | collective-permute-start | bytes 393224 | tf_op jit(solution)/shard_map/ppermute | solution.py:424
  33.8 4.3 %collective-permute-start.3 = (bf16[1,64,512]{2,1,0:T(8,128)(2,1)S(1)}, bf16[1,64,512]{2,1,0:T(8,128)(2,1)S(1)}, u32[]{:S(2)}, u32[]{:S(2)}) collective-permute-start(bf16[1,64,512]{2,1,0:T(8,128)(2,1)S(1)} %fusion), channel_id=1, source_target_pairs={{0,2},{1,3},{2,0},{3,1},{4,6},{5,7},{6,4},{7,5},{8,10},{9,11},{10,... | collective-permute-start | bytes 196616 | tf_op jit(solution)/shard_map/ppermute | solution.py:424

commit v4 on v3

--- a/solution.py
+++ b/solution.py
@@ -12,6 +12,7 @@
 SUB = 32
 TILE = 256
 LANES = 128
+GROUP = 32
 SINE = (4.442883014678955, -7.308245658874512, 3.6063544750213623, -0.8461129069328308, 0.10982698202133179)
 COSINE = (1.4142135381698608, -6.978850841522217, 5.7394609451293945, -1.8835626224777222, 0.31069815158843994)
 PARAMS = dict(compiler_params=pltpu.CompilerParams(vmem_limit_bytes=48 * 1024 * 1024))
@@ -45,8 +46,9 @@
     return jnp.where(lane < half, lane + half, SUB - 1 - lane)
 
 
-def images_kernel(T, L, in_counts, in_offsets, in_coords, in_vis, keep, send, z1r, z1i, z2r, z2i, vs, cs, vis, counts, offsets, sems):
+def images_kernel(T, L, G, in_counts, in_offsets, in_coords, in_vis, keep, send, cs, vs, vis, counts, offsets, sems, *tables):
     Q, Q2 = SUB // T, SUB // T // 2
+    half_u = SUB // 2
     a, base = lax.axis_index("tm"), lax.axis_index("base")
     parts = 2
     span = 4 * L // parts
@@ -61,18 +63,10 @@
         loads.append(pltpu.make_async_copy(in_vis.at[at, :], vis.at[at, :], sems.at[3 + 2 * k]))
     for copy in numbers + loads:
         copy.start()
-    step1, step2 = T // 4, T // 2
-    sign1 = 1 - 2 * ((a // step1) % 2)
-    sign2 = 1 - 2 * ((a // step2) % 2)
-    sign1f, flip = sign1.astype(jnp.float32), (sign1 * sign2).astype(jnp.float32)
-
-    R = 16
-    rho, lane = iota((R, LANES), 0), iota((R, LANES), 1)
-    owner, block, part = rho // 4, (rho // 2) % 2, rho % 2
-    slot = lane + LANES * block
-    rate1 = jnp.where(part == 0, 8.0 / SUB, sign1f * (step1 / SUB))
-    flips = jnp.where(part == 0, 1.0, flip)
-    crossed = jnp.where(part == 0, -1.0, 1.0)
+
+    row8, lane8 = iota((8, LANES), 0), iota((8, LANES), 1)
+    owner, slot = row8 // 2, lane8 + LANES * (row8 % 2)
+    low = lane8 < LANES // 2
 
     def pick(values):
         out = values[-1]
@@ -80,82 +74,60 @@
             out = jnp.where(owner == k, values[k], out)
         return out
 
-    def prepare(i, carry):
-        rows = pl.ds(pl.multiple_of(i * R, R), R)
-        subs = [i * 4 + k for k in range(4)]
-        row_off = [offsets[0, s] for s in subs]
-        col_off = [offsets[1, s] for s in subs]
-        odd = [(r + c) & 1 for r, c in zip(row_off, col_off)]
-        signs = [(1 - 2 * o).astype(jnp.float32) for o in odd]
-        moved = jnp.where(
-            part == 0,
-            pick([(c & (SUB - 1)).astype(jnp.float32) for c in col_off]),
-            pick([(r & (SUB - 1)).astype(jnp.float32) for r in row_off]),
-        )
-        c = cs[rows, :] + moved
-        cs[rows, :] = c
-        r1, i1 = turn(c * rate1)
-        z1r[rows, :] = r1
-        z1i[rows, :] = i1
-        z2r[rows, :] = r1 * r1 - i1 * i1
-        z2i[rows, :] = 2.0 * r1 * i1 * flips
-        along = jnp.where(part == 0, c, pltpu.roll(c, 1, 0))
-        hr, hi = turn(along * (-0.5 / SUB))
-        x = vis[rows, :].astype(jnp.float32)
-        x = jnp.where(slot < pick([counts[0, s] for s in subs]), x * pick(signs), 0.0)
-        other = jnp.where(part == 0, pltpu.roll(x, R - 1, 0), pltpu.roll(x, 1, 0))
-        vs[rows, :] = x * hr + other * (hi * crossed)
-        return carry
-
-    for copy in numbers:
-        copy.wait()
-    for k in range(parts):
-        loads[2 * k].wait()
-        loads[2 * k + 1].wait()
-        lax.fori_loop(k * (span // R), (k + 1) * (span // R), prepare, 0, unroll=2)
-
-    rho8 = iota((8, LANES), 0)
-    rate_u = (rho8.astype(jnp.float32) + 0.5) * (1.0 / SUB)
-    delta, q = rho8 // Q, rho8 % Q
-    group = max(1, 8 // Q)
-    rate_v = (T * q + (a ^ delta) - SUB // 2).astype(jnp.float32) * (1.0 / SUB)
-    low = iota((8, LANES), 1) < LANES // 2
-
-    def row(ref, r):
-        return jnp.broadcast_to(ref[pl.ds(r, 1), :], (8, LANES))
-
-    def tables(s):
-        lhs_r, lhs_i, cos_u, sin_u = [], [], [], []
+    def powers(first, n, place_c, place_v, lr, li, uc, us):
+        subs = [first + 4 * n + k for k in range(4)]
+        even, odd = pl.ds(16 * n, 8, stride=2), pl.ds(16 * n + 1, 8, stride=2)
+        row_off, col_off = [offsets[0, k] for k in subs], [offsets[1, k] for k in subs]
+        signs = [(1 - 2 * ((r + c) & 1)).astype(jnp.float32) for r, c in zip(row_off, col_off)]
+        cu = place_c[even, :] + pick([(c & (SUB - 1)).astype(jnp.float32) for c in col_off])
+        cv = place_c[odd, :] + pick([(r & (SUB - 1)).astype(jnp.float32) for r in row_off])
+        scale = jnp.where(slot < pick([counts[0, k] for k in subs]), pick(signs), 0.0)
+        vr, vi = place_v[even, :] * scale, place_v[odd, :] * scale
+
+        half = turn(cu * (0.5 / SUB))
+        step = times(*half, *half)
+        e = half
+        for k in range(half_u):
+            uc[(n * half_u + k) * 8 : (n * half_u + k) * 8 + 8, :] = e[0]
+            us[(n * half_u + k) * 8 : (n * half_u + k) * 8 + 8, :] = e[1]
+            if k + 1 < half_u:
+                e = times(*e, *step)
+        y1 = turn(cv * (1.0 / SUB))
+        y2 = times(*y1, *y1)
+        y4 = times(*y2, *y2)
+        w0 = times(vr, vi, *turn(cv * -0.5 - cu * (0.5 / SUB)))
+        w1 = times(*w0, *y1)
+        chain = [w0, w1, times(*w0, *y2), times(*w1, *y2)]
+        for m in range(SUB):
+            w = chain[m % 4]
+            at = pl.multiple_of((n * SUB + ((m % T) ^ a) * Q + m // T) * 8, 8)
+            lr[pl.ds(at, 8), :] = w[0]
+            li[pl.ds(at, 8), :] = w[1]
+            if m + 4 < SUB:
+                chain[m % 4] = times(*w, *y4)
+
+    def sides(n, lr, li, uc, us):
+        lhs, cos_u, sin_u = [], [], []
+        for ref in (lr, li):
+            lhs += [ref[pl.ds((n // 4) * SUB * 8 + (2 * n + b) % 8, SUB, stride=8), :].astype(jnp.bfloat16) for b in range(2)]
         for b in range(2):
-            ru = s * 4 + b * 2
-            rv = ru + 1
-            c0, s0 = turn(row(cs, ru) * rate_u)
-            c1, s1 = times(c0, s0, row(z1r, ru), row(z1i, ru))
-            cos_u.append(jnp.concatenate([c0, c1], 0).astype(jnp.bfloat16))
-            sin_u.append(jnp.concatenate([s0, s1], 0).astype(jnp.bfloat16))
-            tr, ti = turn(row(cs, rv) * rate_v)
-            w0 = times(row(vs, ru), row(vs, rv), tr, ti)
-            y1, y2 = (row(z1r, rv), row(z1i, rv)), (row(z2r, rv), row(z2i, rv))
-            w1, w2 = times(*w0, *y1), times(*w0, *y2)
-            w3 = times(*w1, *y2)
-            lhs_r.append(jnp.concatenate([w[0] for w in (w0, w1, w2, w3)], 0).astype(jnp.bfloat16))
-            lhs_i.append(jnp.concatenate([w[1] for w in (w0, w1, w2, w3)], 0).astype(jnp.bfloat16))
+            at = pl.ds((n // 4) * half_u * 8 + (2 * n + b) % 8, half_u, stride=8)
+            cos_u.append(uc[at, :].astype(jnp.bfloat16))
+            sin_u.append(us[at, :].astype(jnp.bfloat16))
         neg_u = [-x for x in sin_u]
-        lhs = jnp.concatenate(lhs_r + lhs_i, 1)
-        plus_r, minus_r = jnp.concatenate(cos_u + neg_u, 1), jnp.concatenate(cos_u + sin_u, 1)
-        plus_i, minus_i = jnp.concatenate(sin_u + cos_u, 1), jnp.concatenate(neg_u + cos_u, 1)
-        return lhs, [plus_r, minus_r, plus_i, minus_i]
-
-    def two(p, carry):
-        s = 2 * p
-        l0, r0 = tables(s)
-        l1, r1 = tables(s + 1)
+        rhs = [cos_u + neg_u, cos_u + sin_u, sin_u + cos_u, neg_u + cos_u]
+        return jnp.concatenate(lhs, 1), [jnp.concatenate(r, 1) for r in rhs]
+
+    def products(keep, send, n, *refs):
+        s = 2 * n
+        (l0, r0), (l1, r1) = sides(2 * n, *refs), sides(2 * n + 1, *refs)
         out = lax.dot_general(
             jnp.concatenate([l0, l1], 0),
             jnp.concatenate(r0 + r1, 0),
             (((1,), (1,)), ((), ())),
             preferred_element_type=jnp.float32,
         )
+        group = max(1, 8 // Q)
         for g in range(4):
             x, y = out[8 * g : 8 * g + 8], out[SUB + 8 * g : SUB + 8 * g + 8]
             x = jnp.where(low, x, pltpu.roll(pltpu.roll(x, 8 - Q2, 0), LANES // 2, 1)).astype(jnp.bfloat16)
@@ -166,27 +138,62 @@
                 ref = send if d % 2 else keep
                 ref[place, s] = x[k * Q : k * Q + Q2]
                 ref[place, s + 1] = y[k * Q : k * Q + Q2]
+
+    for copy in numbers:
+        copy.wait()
+    sides_of = [tables[0:4], tables[4:8]]
+    total = L // G
+
+    def arrive(k):
+        loads[2 * k].wait()
+        loads[2 * k + 1].wait()
+        vs[k * span : (k + 1) * span, :] = vis[k * span : (k + 1) * span, :].astype(jnp.float32)
+
+    def make(i, side):
+        at = pl.ds(pl.multiple_of(i * G * 4, 8), G * 4)
+        for n in range(G // 4):
+            powers(i * G, n, cs.at[at, :], vs.at[at, :], *sides_of[side])
+
+    def use(i, side):
+        at = pl.ds(i * G, G)
+        for n in range(G // 2):
+            products(keep.at[:, at], send.at[:, at], n, *sides_of[side])
+
+    def step(j, carry):
+        make(2 * j + 1, 1)
+        use(2 * j, 0)
+        make(2 * j + 2, 0)
+        use(2 * j + 1, 1)
         return carry
 
-    lax.fori_loop(0, L // 2, two, 0, unroll=32)
+    arrive(0)
+    make(0, 0)
+    for k in range(1, parts):
+        arrive(k)
+    lax.fori_loop(0, total // 2 - 1, step, 0)
+    make(total - 1, 1)
+    use(total - 2, 0)
+    use(total - 1, 1)
 
 
 def images(T, L, counts, offsets, coords, vis):
-    Q2 = SUB // T // 2
+    Q2, G = SUB // T // 2, GROUP
     half = jax.ShapeDtypeStruct((T // 2, L, Q2, LANES), jnp.bfloat16)
     hbm, vmem = pl.BlockSpec(memory_space=pltpu.HBM), pl.BlockSpec(memory_space=pltpu.VMEM)
-    return pl.pallas_call(
-        functools.partial(images_kernel, T, L),
+    table = lambda n: pltpu.VMEM((2 * G * n, LANES), jnp.float32)
+    return pl.pallas_call(
+        functools.partial(images_kernel, T, L, G),
         out_shape=(half, half),
         in_specs=[hbm] * 4,
         out_specs=(vmem, vmem),
-        scratch_shapes=[pltpu.VMEM((4 * L, LANES), jnp.float32)] * 6
+        scratch_shapes=[pltpu.VMEM((4 * L, LANES), jnp.float32)] * 2
         + [
             pltpu.VMEM((4 * L, LANES), jnp.bfloat16),
             pltpu.SMEM((1, L), jnp.int32),
             pltpu.SMEM((2, L), jnp.int32),
             pltpu.SemaphoreType.DMA((6,)),
-        ],
+        ]
+        + [table(SUB), table(SUB), table(SUB // 2), table(SUB // 2)] * 2,
         name="images",
         **PARAMS,
     )(*[pltpu.with_memory_space_constraint(x, pltpu.HBM) for x in (counts, offsets, coords, vis)])

time: 39.3 us -> 38.6 us (0.982)
  Pallas kernels: 11 us -> 10.4 us
    pallas_call x1, Pallas kernels: 6.63 us -> 6.01 us  [images(): pl.pallas_call(functools.partial(images_kernel, T, L, G), out_shape=(half...]
where the time goes in v4:
time: 38.6 us; the launch traced here: 38.3 us
  waiting for transfers between devices  12.8 us (33%)
  starting transfers between devices  11.1 us (29%)
  Pallas kernels  10.4 us (27%)
  local copies, waits for them, and re-layouts  3.09 us (8%)
  other arithmetic  0.73 us (2%)
    all_to_all x1, waiting for transfers between devices, per_device(): lax.all_to_all(outgoing, 'base', split_axis=0, concat_axis=0, tiled=True)  6.96 us
    all_to_all x1, starting transfers between devices, per_device(): lax.all_to_all(outgoing, 'base', split_axis=0, concat_axis=0, tiled=True)  6.02 us
    pallas_call x1, Pallas kernels, images(): pl.pallas_call(functools.partial(images_kernel, T, L, G), out_shape=(half...  6.01 us
    ppermute x4, waiting for transfers between devices, halve(): swap = lambda x, d: lax.ppermute(x, 'tm', [(i, i ^ d) for i in range(T)])  5.88 us
    ppermute x4, starting transfers between devices, halve(): swap = lambda x, d: lax.ppermute(x, 'tm', [(i, i ^ d) for i in range(T)])  5.13 us
    unnamed x13, local copies, waits for them, and re-layouts  2.09 us
    pallas_call x1, Pallas kernels, place_blocks(): pl.pallas_call(functools.partial(place_kernel, T, B, cap, capx, held), ou...  1.68 us
    pallas_call x1, Pallas kernels, send_blocks(): pl.pallas_call(functools.partial(send_kernel, T, L, B, cap, capx), out_sh...  1.01 us
  transfers between devices with their start and end apart: 5, of which 5 were waited for; matrix products, arithmetic and copies ran while one was open for 2% of the time, Pallas kernels for 4%

profile of v4, /device:TPU:0, one launch (start us, length us, event | category | flops | bytes accessed | tf_op | source)
XLA Modules:
  0.0 38.3 jit_solution(13100034708787575467)
XLA Ops:
  0.0 0.0 copy-start.5
  0.0 0.0 copy-start.2
  0.0 6.0 %images.1 = (bf16[2,128,4,128]{3,2,1,0:T(4,128)(2,1)S(1)}, bf16[2,128,4,128]{3,2,1,0:T(4,128)(2,1)S(1)}) custom-call(s32[1,128]{1,0:T(1,128)} %in_counts.1, s32[2,1024]{1,0:T(2,128)} %bitcast.23, f32[512,128]{1,0:T(8,128)} %bitcast.21, bf16[512,128]{1,0:T(8,128)(2,1)} %bitcast.22), custom_call_target="tpu_custom_call" | custom-call | tf_op jit(solution)/shard_map/images/pallas_call | solution.py:184
  6.0 0.5 %collective-permute-start = (bf16[2,128,4,128]{3,2,1,0:T(4,128)(2,1)S(1)}, bf16[2,128,4,128]{3,2,1,0:T(4,128)(2,1)S(1)}, u32[]{:S(2)}, u32[]{:S(2)}) collective-permute-start(bf16[2,128,4,128]{3,2,1,0:T(4,128)(2,1)S(1)} %get-tuple-element.19), channel_id=1, source_target_pairs={{0,1},{1,0},{2,3},{3,2},{4,5},{5,4},{6,7},{7,6},{8,9},{9,8},{10,11... | collective-permute-start | bytes 786440 | tf_op jit(solution)/shard_map/ppermute | solution.py:431
  6.5 1.2 %collective-permute-done.refs_1_ = bf16[2,128,4,128]{3,2,1,0:T(4,128)(2,1)S(1)} collective-permute-done((bf16[2,128,4,128]{3,2,1,0:T(4,128)(2,1)S(1)}, bf16[2,128,4,128]{3,2,1,0:T(4,128)(2,1)S(1)}, u32[]{:S(2)}, u32[]{:S(2)}) %collective-permute-start) | collective-permute-done | bytes 262176 | tf_op jit(solution)/shard_map/ppermute | solution.py:431
  7.7 0.1 add_convert_fusion
  7.8 3.0 %collective-permute-start.1 = (bf16[1,128,4,128]{3,2,1,0:T(4,128)(2,1)S(1)}, bf16[1,128,4,128]{3,2,1,0:T(4,128)(2,1)S(1)}, u32[]{:S(2)}, u32[]{:S(2)}) collective-permute-start(bf16[1,128,4,128]{3,2,1,0:T(4,128)(2,1)S(1)} %add_convert_fusion), channel_id=1, source_target_pairs={{0,2},{1,3},{2,0},{3,1},{4,6},{5,7},{6,4},{7,5},{8,10},{9,11},{10,... | collective-permute-start | bytes 393224 | tf_op jit(solution)/shard_map/ppermute | solution.py:431
  10.7 0.0 copy-start.1
  10.8 0.7 %copy-done.1 = s32[1024,1]{0,1:T(1,128)S(1)} copy-done((s32[1024,1]{0,1:T(1,128)S(1)}, s32[1024,1]{0,1:T(1,128)}, u32[]{:S(2)}) %copy-start.1) | copy-done | bytes 4120
  11.4 0.0 copy-start.3
  11.4 0.7 %copy-done.3 = bf16[4,2,1024]{2,1,0:T(2,128)(2,1)S(1)} copy-done((bf16[4,2,1024]{2,1,0:T(2,128)(2,1)S(1)}, bf16[4,2,1024]{2,1,0:T(2,128)(2,1)}, u32[]{:S(2)}) %copy-start.3) | copy-done | bytes 16408
  12.2 0.0 copy-start.4
  12.2 0.7 %copy-done.4 = s32[128,2]{0,1:T(2,128)S(1)} copy-done((s32[128,2]{0,1:T(2,128)S(1)}, s32[128,2]{0,1:T(2,128)}, u32[]{:S(2)}) %copy-start.4) | copy-done | bytes 1048
  12.8 0.5 %index.1 = (bf16[256,128]{1,0:T(8,128)(2,1)S(1)}, bf16[8,8,512]{2,1,0:T(8,128)(2,1)S(1)}) custom-call(s32[8,128]{1,0:T(8,128)S(1)} %bitcast.19, s32[2,128]{1,0:T(2,128)S(1)} %bitcast.20, bf16[4,2,1024]{2,1,0:T(2,128)(2,1)S(1)} %copy-done.3), custom_call_target="tpu_custom_call" | custom-call | flops 10000000 | bytes 1000000 | tf_op jit(solution)/shard_map/index/pallas_call | solution.py:238
  13.3 1.2 %collective-permute-done.1.refs_2_ = bf16[1,128,4,128]{3,2,1,0:T(4,128)(2,1)S(1)} collective-permute-done((bf16[1,128,4,128]{3,2,1,0:T(4,128)(2,1)S(1)}, bf16[1,128,4,128]{3,2,1,0:T(4,128)(2,1)S(1)}, u32[]{:S(2)}, u32[]{:S(2)}) %collective-permute-start.1) | collective-permute-done | bytes 131104 | tf_op jit(solution)/shard_map/ppermute | solution.py:431
  14.5 0.0 copy-start
  14.5 1.0 %send.1 = bf16[8,32,512]{2,1,0:T(8,128)(2,1)} custom-call(bf16[2,128,4,128]{3,2,1,0:T(4,128)(2,1)S(1)} %get-tuple-element.18.refs_0_, bf16[2,128,4,128]{3,2,1,0:T(4,128)(2,1)S(1)} %collective-permute-done.refs_1_, bf16[1,128,4,128]{3,2,1,0:T(4,128)(2,1)S(1)} %collective-permute-done.1.refs_2_, bf16[256,128]{1,0:T(8,128)(2,1)S(1)} %get-tuple-element.24.refs_3_, ...), custom_call_target="tpu_custom_call" | custom-call | tf_op jit(solution)/shard_map/send/pallas_call | solution.py:271
  15.5 0.0 copy-done.5
  15.5 6.0 %all-to-all-start = ((bf16[8,32,512]{2,1,0:T(8,128)(2,1)}), bf16[8,32,512]{2,1,0:T(8,128)(2,1)S(1)}, u32[]{:S(2)}, u32[]{:S(2)}) async-start(bf16[8,32,512]{2,1,0:T(8,128)(2,1)} %send.1), calls=%async_computation | async-start | bytes 524288 | tf_op jit(solution)/shard_map/all_to_all | solution.py:472
  21.6 0.0 copy-done.2
  21.6 0.2 convert_reduce_fusion
  21.8 0.3 select_reduce_fusion
  22.2 0.1 tile.7
  22.3 0.1 broadcast_in_dim_tile.3.row_off
  22.4 0.1 broadcast_in_dim_squeeze.4.col_off
  22.5 0.6 %rows.1 = bf16[2,256,1536]{2,1,0:T(8,128)(2,1)S(1)} custom-call(s32[1,1536]{1,0:T(1,128)S(1)} %broadcast_in_dim_tile.3.row_off), custom_call_target="tpu_custom_call" | custom-call | flops 10000000 | bytes 1000000 | tf_op jit(solution)/shard_map/rows/pallas_call | solution.py:302
  23.1 7.0 %all-to-all-done.blocks = bf16[8,32,512]{2,1,0:T(8,128)(2,1)S(1)} async-done(((bf16[8,32,512]{2,1,0:T(8,128)(2,1)}), bf16[8,32,512]{2,1,0:T(8,128)(2,1)S(1)}, u32[]{:S(2)}, u32[]{:S(2)}) %all-to-all-start) | async-done | bytes 262176 | tf_op jit(solution)/shard_map/all_to_all | solution.py:472
  30.1 0.0 copy-done
  30.1 1.7 %place.1 = (bf16[1536,512]{1,0:T(8,128)(2,1)S(1)}, bf16[2,64,512]{2,1,0:T(8,128)(2,1)S(1)}) custom-call(bf16[8,32,512]{2,1,0:T(8,128)(2,1)S(1)} %all-to-all-done.blocks, s32[192,1]{1,0:T(8,128)S(1)} %broadcast_in_dim_squeeze.4.col_off, bf16[2,256,1536]{2,1,0:T(8,128)(2,1)S(1)} %rows.1, bf16[256,512]{1,0:T(8,128)(2,1)S(1)} %copy-done), custom_call_target="tpu_custom_call" | custom-call | tf_op jit(solution)/shard_map/place/pallas_call | solution.py:381
  31.8 0.1 collective-permute-start.2
  31.9 0.6 %keep.1 = f32[2,64,512]{2,1,0:T(8,128)S(1)} custom-call(bf16[2,256,1536]{2,1,0:T(8,128)(2,1)S(1)} %rows.1, bf16[1536,512]{1,0:T(8,128)(2,1)S(1)} %get-tuple-element.29.spread), custom_call_target="tpu_custom_call" | custom-call | flops 100000000 | bytes 1000000 | tf_op jit(solution)/shard_map/keep/pallas_call | solution.py:405
  32.4 0.8 %collective-permute-done.2 = bf16[2,64,512]{2,1,0:T(8,128)(2,1)S(1)} collective-permute-done((bf16[2,64,512]{2,1,0:T(8,128)(2,1)S(1)}, bf16[2,64,512]{2,1,0:T(8,128)(2,1)S(1)}, u32[]{:S(2)}, u32[]{:S(2)}) %collective-permute-start.2) | collective-permute-done | bytes 131104 | tf_op jit(solution)/shard_map/ppermute | solution.py:431
  33.2 1.6 %collective-permute-start.3 = (bf16[1,64,512]{2,1,0:T(8,128)(2,1)S(1)}, bf16[1,64,512]{2,1,0:T(8,128)(2,1)S(1)}, u32[]{:S(2)}, u32[]{:S(2)}) collective-permute-start(bf16[1,64,512]{2,1,0:T(8,128)(2,1)S(1)} %fusion), channel_id=1, source_target_pairs={{0,2},{1,3},{2,0},{3,1},{4,6},{5,7},{6,4},{7,5},{8,10},{9,11},{10,... | collective-permute-start | bytes 196616 | tf_op jit(solution)/shard_map/ppermute | solution.py:431
  34.8 2.7 %collective-permute-done.3 = bf16[1,64,512]{2,1,0:T(8,128)(2,1)S(1)} collective-permute-done((bf16[1,64,512]{2,1,0:T(8,128)(2,1)S(1)}, bf16[1,64,512]{2,1,0:T(8,128)(2,1)S(1)}, u32[]{:S(2)}, u32[]{:S(2)}) %collective-permute-start.3) | collective-permute-done | bytes 65568 | tf_op jit(solution)/shard_map/ppermute | solution.py:431
  37.6 0.7 %add.34 = f32[1,64,2,256]{3,2,1,0:T(2,128)} reshape(f32[1,64,512]{2,1,0:T(8,128)S(1)} %fusion.1) | data formatting | bytes 262144 | tf_op jit(solution)/shard_map/add | solution.py:476
  (8 shorter events, 0.1 us)
Async XLA Ops:
  0.0 15.5 %copy-start.5 = (s32[1024,2]{0,1:T(2,128)S(1)}, s32[1024,2]{0,1:T(2,128)}, u32[]{:S(2)}) copy-start(s32[1024,2]{0,1:T(2,128)} %param.13) | copy-start | bytes 24580
  0.0 21.6 %copy-start.2 = (s32[1024,1]{0,1:T(1,128)S(1)}, s32[1024,1]{0,1:T(1,128)}, u32[]{:S(2)}) copy-start(s32[1024,1]{0,1:T(1,128)} %param.12) | copy-start | bytes 12292
  6.0 1.7 %collective-permute-start = (bf16[2,128,4,128]{3,2,1,0:T(4,128)(2,1)S(1)}, bf16[2,128,4,128]{3,2,1,0:T(4,128)(2,1)S(1)}, u32[]{:S(2)}, u32[]{:S(2)}) collective-permute-start(bf16[2,128,4,128]{3,2,1,0:T(4,128)(2,1)S(1)} %get-tuple-element.19), channel_id=1, source_target_pairs={{0,1},{1,0},{2,3},{3,2},{4,5},{5,4},{6,7},{7,6},{8,9},{9,8},{10,11... | collective-permute-start | bytes 786440 | tf_op jit(solution)/shard_map/ppermute | solution.py:431
  7.8 6.8 %collective-permute-start.1 = (bf16[1,128,4,128]{3,2,1,0:T(4,128)(2,1)S(1)}, bf16[1,128,4,128]{3,2,1,0:T(4,128)(2,1)S(1)}, u32[]{:S(2)}, u32[]{:S(2)}) collective-permute-start(bf16[1,128,4,128]{3,2,1,0:T(4,128)(2,1)S(1)} %add_convert_fusion), channel_id=1, source_target_pairs={{0,2},{1,3},{2,0},{3,1},{4,6},{5,7},{6,4},{7,5},{8,10},{9,11},{10,... | collective-permute-start | bytes 393224 | tf_op jit(solution)/shard_map/ppermute | solution.py:431
  10.7 0.7 %copy-start.1 = (s32[1024,1]{0,1:T(1,128)S(1)}, s32[1024,1]{0,1:T(1,128)}, u32[]{:S(2)}) copy-start(s32[1024,1]{0,1:T(1,128)} %param.12) | copy-start | bytes 12292
  11.4 0.7 %copy-start.3 = (bf16[4,2,1024]{2,1,0:T(2,128)(2,1)S(1)}, bf16[4,2,1024]{2,1,0:T(2,128)(2,1)}, u32[]{:S(2)}) copy-start(bf16[4,2,1024]{2,1,0:T(2,128)(2,1)} %screens) | copy-start | bytes 49156
  12.2 0.7 %copy-start.4 = (s32[128,2]{0,1:T(2,128)S(1)}, s32[128,2]{0,1:T(2,128)}, u32[]{:S(2)}) copy-start(s32[128,2]{0,1:T(2,128)} %param.11) | copy-start | bytes 3076
  14.5 15.6 %copy-start = (bf16[256,512]{1,0:T(8,128)(2,1)S(1)}, bf16[256,512]{1,0:T(8,128)(2,1)}, u32[]{:S(2)}) copy-start(bf16[256,512]{1,0:T(8,128)(2,1)} %constant.15.weights) | copy-start | bytes 786436
  15.5 14.5 %all-to-all-start = ((bf16[8,32,512]{2,1,0:T(8,128)(2,1)}), bf16[8,32,512]{2,1,0:T(8,128)(2,1)S(1)}, u32[]{:S(2)}, u32[]{:S(2)}) async-start(bf16[8,32,512]{2,1,0:T(8,128)(2,1)} %send.1), calls=%async_computation | async-start | bytes 524288 | tf_op jit(solution)/shard_map/all_to_all | solution.py:472
  31.8 1.4 %collective-permute-start.2 = (bf16[2,64,512]{2,1,0:T(8,128)(2,1)S(1)}, bf16[2,64,512]{2,1,0:T(8,128)(2,1)S(1)}, u32[]{:S(2)}, u32[]{:S(2)}) collective-permute-start(bf16[2,64,512]{2,1,0:T(8,128)(2,1)S(1)} %get-tuple-element.30), channel_id=1, source_target_pairs={{0,1},{1,0},{2,3},{3,2},{4,5},{5,4},{6,7},{7,6},{8,9},{9,8},{10,11... | collective-permute-start | bytes 393224 | tf_op jit(solution)/shard_map/ppermute | solution.py:431
  33.2 4.3 %collective-permute-start.3 = (bf16[1,64,512]{2,1,0:T(8,128)(2,1)S(1)}, bf16[1,64,512]{2,1,0:T(8,128)(2,1)S(1)}, u32[]{:S(2)}, u32[]{:S(2)}) collective-permute-start(bf16[1,64,512]{2,1,0:T(8,128)(2,1)S(1)} %fusion), channel_id=1, source_target_pairs={{0,2},{1,3},{2,0},{3,1},{4,6},{5,7},{6,4},{7,5},{8,10},{9,11},{10,... | collective-permute-start | bytes 196616 | tf_op jit(solution)/shard_map/ppermute | solution.py:431

commit v5 on v4

--- a/solution.py
+++ b/solution.py
@@ -12,7 +12,7 @@
 SUB = 32
 TILE = 256
 LANES = 128
-GROUP = 32
+GROUP = 64
 SINE = (4.442883014678955, -7.308245658874512, 3.6063544750213623, -0.8461129069328308, 0.10982698202133179)
 COSINE = (1.4142135381698608, -6.978850841522217, 5.7394609451293945, -1.8835626224777222, 0.31069815158843994)
 PARAMS = dict(compiler_params=pltpu.CompilerParams(vmem_limit_bytes=48 * 1024 * 1024))
@@ -199,7 +199,7 @@
     )(*[pltpu.with_memory_space_constraint(x, pltpu.HBM) for x in (counts, offsets, coords, vis)])
 
 
-def index_kernel(T, L, B, cap, capx, held, owners, stations, screens, hot, extras):
+def index_kernel(T, L, B, cap, capx, held, owners, stations, screens, first, second, hot, partial, rows):
     Q2 = SUB // T // 2
     F = Q2 * LANES
     a, base = lax.axis_index("tm"), lax.axis_index("base")
@@ -208,6 +208,12 @@
     rank = jnp.sum(same.astype(jnp.float32), axis=0, keepdims=True).astype(jnp.int32)
     slots = mine[0:1] * capx + rank
     hot[...] = (iota((B * capx, L), 0) == slots).astype(jnp.float32).astype(jnp.bfloat16)
+    for k, term in enumerate((first, second)):
+        rows[k] = term[0].astype(jnp.float32).reshape(L * Q2, LANES)
+    for q in range(Q2):
+        parts = [rows[k, pl.ds(q, L, stride=Q2), :].astype(jnp.bfloat16) for k in range(2)]
+        parts = [jnp.dot(hot[...], x, preferred_element_type=jnp.float32) for x in parts]
+        partial[:, LANES * q : LANES * (q + 1)] = parts[0] + parts[1]
 
     lane = iota((1, F), 1)
     m = T * (((lane // (2 * SUB)) % 2) * Q2 + lane // LANES) + a
@@ -226,45 +232,51 @@
         own = (iota((LANES, L), 0) + o * capx == slots).astype(jnp.float32).astype(jnp.bfloat16)
         listed = lax.dot_general(names, own, (((1,), (1,)), ((), ())), preferred_element_type=jnp.float32)
         listed = jnp.concatenate([listed] + [jnp.zeros((8, F - LANES), jnp.float32)], 1)
-        extras[o] = jnp.where(iota((8, F), 0) < 4, mine_x, listed).astype(jnp.bfloat16)
+        at = pl.ds(pl.multiple_of(o * capx + cap, 8), 8)
+        partial[at, :] = jnp.where(iota((8, F), 0) < 4, mine_x, listed)
         return carry
 
     lax.fori_loop(0, B, one, 0, unroll=min(B, 8))
 
 
-def index_tables(T, L, B, cap, capx, held, owners, stations, screens):
+def index_tables(T, L, B, cap, capx, held, owners, stations, screens, first, second):
     F = SUB // T // 2 * LANES
     vmem = pl.BlockSpec(memory_space=pltpu.VMEM)
     return pl.pallas_call(
         functools.partial(index_kernel, T, L, B, cap, capx, held),
         out_shape=(
             jax.ShapeDtypeStruct((B * capx, L), jnp.bfloat16),
-            jax.ShapeDtypeStruct((B, 8, F), jnp.bfloat16),
+            jax.ShapeDtypeStruct((B * capx, F), jnp.float32),
         ),
-        in_specs=[vmem] * 3,
+        in_specs=[vmem] * 5,
         out_specs=(vmem, vmem),
+        scratch_shapes=[pltpu.VMEM((2, L * SUB // T // 2, LANES), jnp.float32)],
         name="index",
         cost_estimate=pl.CostEstimate(flops=10**7, bytes_accessed=10**6, transcendentals=0),
         **PARAMS,
-    )(owners, stations, screens)
+    )(owners, stations, screens, first, second)
 
 
 def send_kernel(T, L, B, cap, capx, *refs):
-    terms, (hot, extras, out, rows) = refs[:-4], refs[-4:]
+    terms, (hot, partial, out, rows, block, sems) = refs[:-6], refs[-6:]
     Q2 = SUB // T // 2
-    F = Q2 * LANES
     total = terms[0][0].astype(jnp.float32)
     for t in terms[1:]:
         total = total + t[0].astype(jnp.float32)
     rows[...] = total.reshape(L * Q2, LANES)
+    copies = []
     for q in range(Q2):
+        at = slice(LANES * q, LANES * (q + 1))
         x = rows[pl.ds(q, L, stride=Q2), :].astype(jnp.bfloat16)
-        moved = jnp.dot(hot[...], x, preferred_element_type=jnp.float32).astype(jnp.bfloat16)
-        out[:, :, LANES * q : LANES * (q + 1)] = moved.reshape(B, capx, LANES)
-    out[:, cap : cap + 8, :] = extras[...]
-
-
-def send_blocks(T, L, B, cap, capx, terms, hot, extras):
+        moved = partial[:, at] + jnp.dot(hot[...], x, preferred_element_type=jnp.float32)
+        block[:, :, at] = moved.astype(jnp.bfloat16).reshape(B, capx, LANES)
+        copies.append(pltpu.make_async_copy(block.at[:, :, at], out.at[:, :, at], sems.at[q]))
+        copies[-1].start()
+    for copy in copies:
+        copy.wait()
+
+
+def send_blocks(T, L, B, cap, capx, terms, hot, partial):
     Q2 = SUB // T // 2
     F = Q2 * LANES
     vmem = pl.BlockSpec(memory_space=pltpu.VMEM)
@@ -272,11 +284,15 @@
         functools.partial(send_kernel, T, L, B, cap, capx),
         out_shape=jax.ShapeDtypeStruct((B, capx, F), jnp.bfloat16),
         in_specs=[vmem] * (len(terms) + 2),
-        out_specs=vmem,
-        scratch_shapes=[pltpu.VMEM((L * Q2, LANES), jnp.float32)],
+        out_specs=pl.BlockSpec(memory_space=pltpu.HBM),
+        scratch_shapes=[
+            pltpu.VMEM((L * Q2, LANES), jnp.float32),
+            pltpu.VMEM((B, capx, F), jnp.bfloat16),
+            pltpu.SemaphoreType.DMA((Q2,)),
+        ],
         name="send",
         **PARAMS,
-    )(*terms, hot, extras)
+    )(*terms, hot, partial)
 
 
 def rows_kernel(T, S, row_off, rows):
@@ -455,8 +471,8 @@
     keep, send = images(T, L, counts, offsets.T, flat(coords[0]), flat(visibilities[0]))
     terms, late = halve(T, keep, send, (owners, stations, screens))
     owner = late[0][:, 0].reshape(B, L)
-    hot, extras = index_tables(T, L, B, cap, capx, held, owner, late[1].T, late[2])
-    outgoing = send_blocks(T, L, B, cap, capx, terms, hot, extras)
+    hot, partial = index_tables(T, L, B, cap, capx, held, owner, late[1].T, late[2], *terms[:2])
+    outgoing = send_blocks(T, L, B, cap, capx, terms[2:], hot, partial)
     outgoing, owners, offsets = lax.optimization_barrier((outgoing, owners, offsets))
 
     to_me = owners[:, 0].reshape(B, L) == base

time: 38.6 us -> 38.4 us (level)
  transfers between devices with their start and end apart: 5 -> 5, of which waited for: 5 -> 5; matrix products, arithmetic and copies ran while one was open for 2% -> 2% of each run, Pallas kernels for 4% -> 5%
where the time goes in v5:
time: 38.4 us; the launch traced here: 38.1 us
  waiting for transfers between devices  12.6 us (33%)
  starting transfers between devices  11.2 us (29%)
  Pallas kernels  10.3 us (27%)
  local copies, waits for them, and re-layouts  3.09 us (8%)
  other arithmetic  0.73 us (2%)
    all_to_all x1, waiting for transfers between devices, per_device(): lax.all_to_all(outgoing, 'base', split_axis=0, concat_axis=0, tiled=True)  6.96 us
    all_to_all x1, starting transfers between devices, per_device(): lax.all_to_all(outgoing, 'base', split_axis=0, concat_axis=0, tiled=True)  6.04 us
    pallas_call x1, Pallas kernels, images(): pl.pallas_call(functools.partial(images_kernel, T, L, G), out_shape=(half...  5.79 us
    ppermute x4, waiting for transfers between devices, halve(): swap = lambda x, d: lax.ppermute(x, 'tm', [(i, i ^ d) for i in range(T)])  5.67 us
    ppermute x4, starting transfers between devices, halve(): swap = lambda x, d: lax.ppermute(x, 'tm', [(i, i ^ d) for i in range(T)])  5.13 us
    unnamed x13, local copies, waits for them, and re-layouts  2.09 us
    pallas_call x1, Pallas kernels, place_blocks(): pl.pallas_call(functools.partial(place_kernel, T, B, cap, capx, held), ou...  1.67 us
    pallas_call x1, Pallas kernels, send_blocks(): pl.pallas_call(functools.partial(send_kernel, T, L, B, cap, capx), out_sh...  0.95 us
  transfers between devices with their start and end apart: 5, of which 5 were waited for; matrix products, arithmetic and copies ran while one was open for 2% of the time, Pallas kernels for 5%

profile of v5, /device:TPU:0, one launch (start us, length us, event | category | flops | bytes accessed | tf_op | source)
XLA Modules:
  0.0 38.1 jit_solution(10166489642385794555)
XLA Ops:
  0.0 0.0 copy-start.5
  0.0 0.0 copy-start.2
  0.0 5.8 %images.1 = (bf16[2,128,4,128]{3,2,1,0:T(4,128)(2,1)S(1)}, bf16[2,128,4,128]{3,2,1,0:T(4,128)(2,1)S(1)}) custom-call(s32[1,128]{1,0:T(1,128)} %in_counts.1, s32[2,1024]{1,0:T(2,128)} %bitcast.23, f32[512,128]{1,0:T(8,128)} %bitcast.21, bf16[512,128]{1,0:T(8,128)(2,1)} %bitcast.22), custom_call_target="tpu_custom_call" | custom-call | tf_op jit(solution)/shard_map/images/pallas_call | solution.py:184
  5.8 0.5 %collective-permute-start = (bf16[2,128,4,128]{3,2,1,0:T(4,128)(2,1)S(1)}, bf16[2,128,4,128]{3,2,1,0:T(4,128)(2,1)S(1)}, u32[]{:S(2)}, u32[]{:S(2)}) collective-permute-start(bf16[2,128,4,128]{3,2,1,0:T(4,128)(2,1)S(1)} %get-tuple-element.19), channel_id=1, source_target_pairs={{0,1},{1,0},{2,3},{3,2},{4,5},{5,4},{6,7},{7,6},{8,9},{9,8},{10,11... | collective-permute-start | bytes 786440 | tf_op jit(solution)/shard_map/ppermute | solution.py:447
  6.3 1.2 %collective-permute-done.second = bf16[2,128,4,128]{3,2,1,0:T(4,128)(2,1)S(1)} collective-permute-done((bf16[2,128,4,128]{3,2,1,0:T(4,128)(2,1)S(1)}, bf16[2,128,4,128]{3,2,1,0:T(4,128)(2,1)S(1)}, u32[]{:S(2)}, u32[]{:S(2)}) %collective-permute-start) | collective-permute-done | bytes 262176 | tf_op jit(solution)/shard_map/ppermute | solution.py:447
  7.5 0.1 add_convert_fusion
  7.6 3.0 %collective-permute-start.1 = (bf16[1,128,4,128]{3,2,1,0:T(4,128)(2,1)S(1)}, bf16[1,128,4,128]{3,2,1,0:T(4,128)(2,1)S(1)}, u32[]{:S(2)}, u32[]{:S(2)}) collective-permute-start(bf16[1,128,4,128]{3,2,1,0:T(4,128)(2,1)S(1)} %add_convert_fusion), channel_id=1, source_target_pairs={{0,2},{1,3},{2,0},{3,1},{4,6},{5,7},{6,4},{7,5},{8,10},{9,11},{10,... | collective-permute-start | bytes 393224 | tf_op jit(solution)/shard_map/ppermute | solution.py:447
  10.5 0.0 copy-start.1
  10.5 0.7 %copy-done.1 = s32[1024,1]{0,1:T(1,128)S(1)} copy-done((s32[1024,1]{0,1:T(1,128)S(1)}, s32[1024,1]{0,1:T(1,128)}, u32[]{:S(2)}) %copy-start.1) | copy-done | bytes 4120
  11.2 0.0 copy-start.3
  11.2 0.7 %copy-done.3 = bf16[4,2,1024]{2,1,0:T(2,128)(2,1)S(1)} copy-done((bf16[4,2,1024]{2,1,0:T(2,128)(2,1)S(1)}, bf16[4,2,1024]{2,1,0:T(2,128)(2,1)}, u32[]{:S(2)}) %copy-start.3) | copy-done | bytes 16408
  11.9 0.0 copy-start.4
  11.9 0.7 %copy-done.4 = s32[128,2]{0,1:T(2,128)S(1)} copy-done((s32[128,2]{0,1:T(2,128)S(1)}, s32[128,2]{0,1:T(2,128)}, u32[]{:S(2)}) %copy-start.4) | copy-done | bytes 1048
  12.6 0.7 %index.1 = (bf16[256,128]{1,0:T(8,128)(2,1)S(1)}, f32[256,512]{1,0:T(8,128)S(1)}) custom-call(s32[8,128]{1,0:T(8,128)S(1)} %bitcast.19, s32[2,128]{1,0:T(2,128)S(1)} %bitcast.20, bf16[4,2,1024]{2,1,0:T(2,128)(2,1)S(1)} %copy-done.3, bf16[2,128,4,128]{3,2,1,0:T(4,128)(2,1)S(1)} %get-tuple-element.18.first, ...), custom_call_target="tpu_custom_call" | custom-call | flops 10000000 | bytes 1000000 | tf_op jit(solution)/shard_map/index/pallas_call | solution.py:245
  13.3 1.0 %collective-permute-done.1.refs_0_ = bf16[1,128,4,128]{3,2,1,0:T(4,128)(2,1)S(1)} collective-permute-done((bf16[1,128,4,128]{3,2,1,0:T(4,128)(2,1)S(1)}, bf16[1,128,4,128]{3,2,1,0:T(4,128)(2,1)S(1)}, u32[]{:S(2)}, u32[]{:S(2)}) %collective-permute-start.1) | collective-permute-done | bytes 131104 | tf_op jit(solution)/shard_map/ppermute | solution.py:447
  14.3 0.0 copy-start
  14.3 1.0 %send.1 = bf16[8,32,512]{2,1,0:T(8,128)(2,1)} custom-call(bf16[1,128,4,128]{3,2,1,0:T(4,128)(2,1)S(1)} %collective-permute-done.1.refs_0_, bf16[256,128]{1,0:T(8,128)(2,1)S(1)} %get-tuple-element.24.refs_1_, f32[256,512]{1,0:T(8,128)S(1)} %get-tuple-element.25.refs_2_), custom_call_target="tpu_custom_call" | custom-call | tf_op jit(solution)/shard_map/send/pallas_call | solution.py:283
  15.3 0.0 copy-done.5
  15.3 6.0 %all-to-all-start = ((bf16[8,32,512]{2,1,0:T(8,128)(2,1)}), bf16[8,32,512]{2,1,0:T(8,128)(2,1)S(1)}, u32[]{:S(2)}, u32[]{:S(2)}) async-start(bf16[8,32,512]{2,1,0:T(8,128)(2,1)} %send.1), calls=%async_computation | async-start | bytes 524288 | tf_op jit(solution)/shard_map/all_to_all | solution.py:488
  21.3 0.0 copy-done.2
  21.4 0.2 convert_reduce_fusion
  21.6 0.3 select_reduce_fusion
  22.0 0.1 tile.7
  22.1 0.1 broadcast_in_dim_tile.3.row_off
  22.1 0.1 broadcast_in_dim_squeeze.4.col_off
  22.2 0.6 %rows.1 = bf16[2,256,1536]{2,1,0:T(8,128)(2,1)S(1)} custom-call(s32[1,1536]{1,0:T(1,128)S(1)} %broadcast_in_dim_tile.3.row_off), custom_call_target="tpu_custom_call" | custom-call | flops 10000000 | bytes 1000000 | tf_op jit(solution)/shard_map/rows/pallas_call | solution.py:318
  22.9 7.0 %all-to-all-done.blocks = bf16[8,32,512]{2,1,0:T(8,128)(2,1)S(1)} async-done(((bf16[8,32,512]{2,1,0:T(8,128)(2,1)}), bf16[8,32,512]{2,1,0:T(8,128)(2,1)S(1)}, u32[]{:S(2)}, u32[]{:S(2)}) %all-to-all-start) | async-done | bytes 262176 | tf_op jit(solution)/shard_map/all_to_all | solution.py:488
  29.9 0.0 copy-done
  29.9 1.7 %place.1 = (bf16[1536,512]{1,0:T(8,128)(2,1)S(1)}, bf16[2,64,512]{2,1,0:T(8,128)(2,1)S(1)}) custom-call(bf16[8,32,512]{2,1,0:T(8,128)(2,1)S(1)} %all-to-all-done.blocks, s32[192,1]{1,0:T(8,128)S(1)} %broadcast_in_dim_squeeze.4.col_off, bf16[2,256,1536]{2,1,0:T(8,128)(2,1)S(1)} %rows.1, bf16[256,512]{1,0:T(8,128)(2,1)S(1)} %copy-done), custom_call_target="tpu_custom_call" | custom-call | tf_op jit(solution)/shard_map/place/pallas_call | solution.py:397
  31.5 0.1 collective-permute-start.2
  31.6 0.6 %keep.1 = f32[2,64,512]{2,1,0:T(8,128)S(1)} custom-call(bf16[2,256,1536]{2,1,0:T(8,128)(2,1)S(1)} %rows.1, bf16[1536,512]{1,0:T(8,128)(2,1)S(1)} %get-tuple-element.29.spread), custom_call_target="tpu_custom_call" | custom-call | flops 100000000 | bytes 1000000 | tf_op jit(solution)/shard_map/keep/pallas_call | solution.py:421
  32.2 0.8 %collective-permute-done.2 = bf16[2,64,512]{2,1,0:T(8,128)(2,1)S(1)} collective-permute-done((bf16[2,64,512]{2,1,0:T(8,128)(2,1)S(1)}, bf16[2,64,512]{2,1,0:T(8,128)(2,1)S(1)}, u32[]{:S(2)}, u32[]{:S(2)}) %collective-permute-start.2) | collective-permute-done | bytes 131104 | tf_op jit(solution)/shard_map/ppermute | solution.py:447
  33.0 1.6 %collective-permute-start.3 = (bf16[1,64,512]{2,1,0:T(8,128)(2,1)S(1)}, bf16[1,64,512]{2,1,0:T(8,128)(2,1)S(1)}, u32[]{:S(2)}, u32[]{:S(2)}) collective-permute-start(bf16[1,64,512]{2,1,0:T(8,128)(2,1)S(1)} %fusion), channel_id=1, source_target_pairs={{0,2},{1,3},{2,0},{3,1},{4,6},{5,7},{6,4},{7,5},{8,10},{9,11},{10,... | collective-permute-start | bytes 196616 | tf_op jit(solution)/shard_map/ppermute | solution.py:447
  34.6 2.7 %collective-permute-done.3 = bf16[1,64,512]{2,1,0:T(8,128)(2,1)S(1)} collective-permute-done((bf16[1,64,512]{2,1,0:T(8,128)(2,1)S(1)}, bf16[1,64,512]{2,1,0:T(8,128)(2,1)S(1)}, u32[]{:S(2)}, u32[]{:S(2)}) %collective-permute-start.3) | collective-permute-done | bytes 65568 | tf_op jit(solution)/shard_map/ppermute | solution.py:447
  37.3 0.7 %add.34 = f32[1,64,2,256]{3,2,1,0:T(2,128)} reshape(f32[1,64,512]{2,1,0:T(8,128)S(1)} %fusion.1) | data formatting | bytes 262144 | tf_op jit(solution)/shard_map/add | solution.py:492
  (8 shorter events, 0.1 us)
Async XLA Ops:
  0.0 15.3 %copy-start.5 = (s32[1024,2]{0,1:T(2,128)S(1)}, s32[1024,2]{0,1:T(2,128)}, u32[]{:S(2)}) copy-start(s32[1024,2]{0,1:T(2,128)} %param.13) | copy-start | bytes 24580
  0.0 21.3 %copy-start.2 = (s32[1024,1]{0,1:T(1,128)S(1)}, s32[1024,1]{0,1:T(1,128)}, u32[]{:S(2)}) copy-start(s32[1024,1]{0,1:T(1,128)} %param.12) | copy-start | bytes 12292
  5.8 1.7 %collective-permute-start = (bf16[2,128,4,128]{3,2,1,0:T(4,128)(2,1)S(1)}, bf16[2,128,4,128]{3,2,1,0:T(4,128)(2,1)S(1)}, u32[]{:S(2)}, u32[]{:S(2)}) collective-permute-start(bf16[2,128,4,128]{3,2,1,0:T(4,128)(2,1)S(1)} %get-tuple-element.19), channel_id=1, source_target_pairs={{0,1},{1,0},{2,3},{3,2},{4,5},{5,4},{6,7},{7,6},{8,9},{9,8},{10,11... | collective-permute-start | bytes 786440 | tf_op jit(solution)/shard_map/ppermute | solution.py:447
  7.6 6.8 %collective-permute-start.1 = (bf16[1,128,4,128]{3,2,1,0:T(4,128)(2,1)S(1)}, bf16[1,128,4,128]{3,2,1,0:T(4,128)(2,1)S(1)}, u32[]{:S(2)}, u32[]{:S(2)}) collective-permute-start(bf16[1,128,4,128]{3,2,1,0:T(4,128)(2,1)S(1)} %add_convert_fusion), channel_id=1, source_target_pairs={{0,2},{1,3},{2,0},{3,1},{4,6},{5,7},{6,4},{7,5},{8,10},{9,11},{10,... | collective-permute-start | bytes 393224 | tf_op jit(solution)/shard_map/ppermute | solution.py:447
  10.5 0.7 %copy-start.1 = (s32[1024,1]{0,1:T(1,128)S(1)}, s32[1024,1]{0,1:T(1,128)}, u32[]{:S(2)}) copy-start(s32[1024,1]{0,1:T(1,128)} %param.12) | copy-start | bytes 12292
  11.2 0.7 %copy-start.3 = (bf16[4,2,1024]{2,1,0:T(2,128)(2,1)S(1)}, bf16[4,2,1024]{2,1,0:T(2,128)(2,1)}, u32[]{:S(2)}) copy-start(bf16[4,2,1024]{2,1,0:T(2,128)(2,1)} %screens) | copy-start | bytes 49156
  11.9 0.7 %copy-start.4 = (s32[128,2]{0,1:T(2,128)S(1)}, s32[128,2]{0,1:T(2,128)}, u32[]{:S(2)}) copy-start(s32[128,2]{0,1:T(2,128)} %param.11) | copy-start | bytes 3076
  14.3 15.6 %copy-start = (bf16[256,512]{1,0:T(8,128)(2,1)S(1)}, bf16[256,512]{1,0:T(8,128)(2,1)}, u32[]{:S(2)}) copy-start(bf16[256,512]{1,0:T(8,128)(2,1)} %constant.15.weights) | copy-start | bytes 786436
  15.3 14.6 %all-to-all-start = ((bf16[8,32,512]{2,1,0:T(8,128)(2,1)}), bf16[8,32,512]{2,1,0:T(8,128)(2,1)S(1)}, u32[]{:S(2)}, u32[]{:S(2)}) async-start(bf16[8,32,512]{2,1,0:T(8,128)(2,1)} %send.1), calls=%async_computation | async-start | bytes 524288 | tf_op jit(solution)/shard_map/all_to_all | solution.py:488
  31.5 1.4 %collective-permute-start.2 = (bf16[2,64,512]{2,1,0:T(8,128)(2,1)S(1)}, bf16[2,64,512]{2,1,0:T(8,128)(2,1)S(1)}, u32[]{:S(2)}, u32[]{:S(2)}) collective-permute-start(bf16[2,64,512]{2,1,0:T(8,128)(2,1)S(1)} %get-tuple-element.30), channel_id=1, source_target_pairs={{0,1},{1,0},{2,3},{3,2},{4,5},{5,4},{6,7},{7,6},{8,9},{9,8},{10,11... | collective-permute-start | bytes 393224 | tf_op jit(solution)/shard_map/ppermute | solution.py:447
  33.0 4.3 %collective-permute-start.3 = (bf16[1,64,512]{2,1,0:T(8,128)(2,1)S(1)}, bf16[1,64,512]{2,1,0:T(8,128)(2,1)S(1)}, u32[]{:S(2)}, u32[]{:S(2)}) collective-permute-start(bf16[1,64,512]{2,1,0:T(8,128)(2,1)S(1)} %fusion), channel_id=1, source_target_pairs={{0,2},{1,3},{2,0},{3,1},{4,6},{5,7},{6,4},{7,5},{8,10},{9,11},{10,... | collective-permute-start | bytes 196616 | tf_op jit(solution)/shard_map/ppermute | solution.py:447

commit v6 on v5

--- a/solution.py
+++ b/solution.py
@@ -368,6 +368,7 @@
         scaled = (n.astype(jnp.float32) + 0.5 - SUB / 2.0) / (SUB / 2.0)
         return 1.0 - scaled * scaled
 
+    mixed = []
     for q in range(Q2):
         at = slice(LANES * q, LANES * (q + 1))
         at_i = slice(F + LANES * q, F + LANES * (q + 1))
@@ -378,7 +379,10 @@
         qr, qi = [jnp.dot(hot_q, t, preferred_element_type=jnp.float32) for t in tables]
         d = data[:, at] * window
         x = jnp.concatenate([d * (pr * qr + pi * qi), d * (pr * qi - pi * qr)], 1).astype(jnp.bfloat16)
-        y = jnp.dot(x, weights[...], preferred_element_type=jnp.float32)
+        mixed.append(x)
+
+    for q in range(Q2):
+        y = jnp.dot(mixed[q], weights[...], preferred_element_type=jnp.float32)
         for h in range(2):
             for c in range(2):
                 v = y[:, (h * 2 + c) * LANES : (h * 2 + c + 1) * LANES]

time: 38.4 us -> 38 us (0.990)
  no operation moved by 1% of the time
where the time goes in v6:
time: 38 us; the launch traced here: 37.7 us
  waiting for transfers between devices  12.6 us (33%)
  starting transfers between devices  11.2 us (29%)
  Pallas kernels  9.96 us (26%)
  local copies, waits for them, and re-layouts  3.09 us (8%)
  other arithmetic  0.73 us (2%)
    all_to_all x1, waiting for transfers between devices, per_device(): lax.all_to_all(outgoing, 'base', split_axis=0, concat_axis=0, tiled=True)  6.96 us
    all_to_all x1, starting transfers between devices, per_device(): lax.all_to_all(outgoing, 'base', split_axis=0, concat_axis=0, tiled=True)  6.04 us
    pallas_call x1, Pallas kernels, images(): pl.pallas_call(functools.partial(images_kernel, T, L, G), out_shape=(half...  5.79 us
    ppermute x4, waiting for transfers between devices, halve(): swap = lambda x, d: lax.ppermute(x, 'tm', [(i, i ^ d) for i in range(T)])  5.67 us
    ppermute x4, starting transfers between devices, halve(): swap = lambda x, d: lax.ppermute(x, 'tm', [(i, i ^ d) for i in range(T)])  5.13 us
    unnamed x13, local copies, waits for them, and re-layouts  2.09 us
    pallas_call x1, Pallas kernels, place_blocks(): pl.pallas_call(functools.partial(place_kernel, T, B, cap, capx, held), ou...  1.32 us
    pallas_call x1, Pallas kernels, send_blocks(): pl.pallas_call(functools.partial(send_kernel, T, L, B, cap, capx), out_sh...  0.95 us
  transfers between devices with their start and end apart: 5, of which 5 were waited for; matrix products, arithmetic and copies ran while one was open for 2% of the time, Pallas kernels for 5%

profile of v6, /device:TPU:0, one launch (start us, length us, event | category | flops | bytes accessed | tf_op | source)
XLA Modules:
  0.0 37.7 jit_solution(11011674810059519676)
XLA Ops:
  0.0 0.0 copy-start.5
  0.0 0.0 copy-start.2
  0.0 5.8 %images.1 = (bf16[2,128,4,128]{3,2,1,0:T(4,128)(2,1)S(1)}, bf16[2,128,4,128]{3,2,1,0:T(4,128)(2,1)S(1)}) custom-call(s32[1,128]{1,0:T(1,128)} %in_counts.1, s32[2,1024]{1,0:T(2,128)} %bitcast.23, f32[512,128]{1,0:T(8,128)} %bitcast.21, bf16[512,128]{1,0:T(8,128)(2,1)} %bitcast.22), custom_call_target="tpu_custom_call" | custom-call | tf_op jit(solution)/shard_map/images/pallas_call | solution.py:184
  5.8 0.5 %collective-permute-start = (bf16[2,128,4,128]{3,2,1,0:T(4,128)(2,1)S(1)}, bf16[2,128,4,128]{3,2,1,0:T(4,128)(2,1)S(1)}, u32[]{:S(2)}, u32[]{:S(2)}) collective-permute-start(bf16[2,128,4,128]{3,2,1,0:T(4,128)(2,1)S(1)} %get-tuple-element.19), channel_id=1, source_target_pairs={{0,1},{1,0},{2,3},{3,2},{4,5},{5,4},{6,7},{7,6},{8,9},{9,8},{10,11... | collective-permute-start | bytes 786440 | tf_op jit(solution)/shard_map/ppermute | solution.py:451
  6.3 1.2 %collective-permute-done.second = bf16[2,128,4,128]{3,2,1,0:T(4,128)(2,1)S(1)} collective-permute-done((bf16[2,128,4,128]{3,2,1,0:T(4,128)(2,1)S(1)}, bf16[2,128,4,128]{3,2,1,0:T(4,128)(2,1)S(1)}, u32[]{:S(2)}, u32[]{:S(2)}) %collective-permute-start) | collective-permute-done | bytes 262176 | tf_op jit(solution)/shard_map/ppermute | solution.py:451
  7.5 0.1 add_convert_fusion
  7.6 3.0 %collective-permute-start.1 = (bf16[1,128,4,128]{3,2,1,0:T(4,128)(2,1)S(1)}, bf16[1,128,4,128]{3,2,1,0:T(4,128)(2,1)S(1)}, u32[]{:S(2)}, u32[]{:S(2)}) collective-permute-start(bf16[1,128,4,128]{3,2,1,0:T(4,128)(2,1)S(1)} %add_convert_fusion), channel_id=1, source_target_pairs={{0,2},{1,3},{2,0},{3,1},{4,6},{5,7},{6,4},{7,5},{8,10},{9,11},{10,... | collective-permute-start | bytes 393224 | tf_op jit(solution)/shard_map/ppermute | solution.py:451
  10.5 0.0 copy-start.1
  10.5 0.7 %copy-done.1 = s32[1024,1]{0,1:T(1,128)S(1)} copy-done((s32[1024,1]{0,1:T(1,128)S(1)}, s32[1024,1]{0,1:T(1,128)}, u32[]{:S(2)}) %copy-start.1) | copy-done | bytes 4120
  11.2 0.0 copy-start.3
  11.2 0.7 %copy-done.3 = bf16[4,2,1024]{2,1,0:T(2,128)(2,1)S(1)} copy-done((bf16[4,2,1024]{2,1,0:T(2,128)(2,1)S(1)}, bf16[4,2,1024]{2,1,0:T(2,128)(2,1)}, u32[]{:S(2)}) %copy-start.3) | copy-done | bytes 16408
  11.9 0.0 copy-start.4
  11.9 0.7 %copy-done.4 = s32[128,2]{0,1:T(2,128)S(1)} copy-done((s32[128,2]{0,1:T(2,128)S(1)}, s32[128,2]{0,1:T(2,128)}, u32[]{:S(2)}) %copy-start.4) | copy-done | bytes 1048
  12.6 0.7 %index.1 = (bf16[256,128]{1,0:T(8,128)(2,1)S(1)}, f32[256,512]{1,0:T(8,128)S(1)}) custom-call(s32[8,128]{1,0:T(8,128)S(1)} %bitcast.19, s32[2,128]{1,0:T(2,128)S(1)} %bitcast.20, bf16[4,2,1024]{2,1,0:T(2,128)(2,1)S(1)} %copy-done.3, bf16[2,128,4,128]{3,2,1,0:T(4,128)(2,1)S(1)} %get-tuple-element.18.first, ...), custom_call_target="tpu_custom_call" | custom-call | flops 10000000 | bytes 1000000 | tf_op jit(solution)/shard_map/index/pallas_call | solution.py:245
  13.3 1.0 %collective-permute-done.1.refs_0_ = bf16[1,128,4,128]{3,2,1,0:T(4,128)(2,1)S(1)} collective-permute-done((bf16[1,128,4,128]{3,2,1,0:T(4,128)(2,1)S(1)}, bf16[1,128,4,128]{3,2,1,0:T(4,128)(2,1)S(1)}, u32[]{:S(2)}, u32[]{:S(2)}) %collective-permute-start.1) | collective-permute-done | bytes 131104 | tf_op jit(solution)/shard_map/ppermute | solution.py:451
  14.3 0.0 copy-start
  14.3 1.0 %send.1 = bf16[8,32,512]{2,1,0:T(8,128)(2,1)} custom-call(bf16[1,128,4,128]{3,2,1,0:T(4,128)(2,1)S(1)} %collective-permute-done.1.refs_0_, bf16[256,128]{1,0:T(8,128)(2,1)S(1)} %get-tuple-element.24.refs_1_, f32[256,512]{1,0:T(8,128)S(1)} %get-tuple-element.25.refs_2_), custom_call_target="tpu_custom_call" | custom-call | tf_op jit(solution)/shard_map/send/pallas_call | solution.py:283
  15.3 0.0 copy-done.5
  15.3 6.0 %all-to-all-start = ((bf16[8,32,512]{2,1,0:T(8,128)(2,1)}), bf16[8,32,512]{2,1,0:T(8,128)(2,1)S(1)}, u32[]{:S(2)}, u32[]{:S(2)}) async-start(bf16[8,32,512]{2,1,0:T(8,128)(2,1)} %send.1), calls=%async_computation | async-start | bytes 524288 | tf_op jit(solution)/shard_map/all_to_all | solution.py:492
  21.3 0.0 copy-done.2
  21.4 0.2 convert_reduce_fusion
  21.6 0.3 select_reduce_fusion
  22.0 0.1 tile.7
  22.1 0.1 broadcast_in_dim_tile.3.row_off
  22.1 0.1 broadcast_in_dim_squeeze.4.col_off
  22.2 0.6 %rows.1 = bf16[2,256,1536]{2,1,0:T(8,128)(2,1)S(1)} custom-call(s32[1,1536]{1,0:T(1,128)S(1)} %broadcast_in_dim_tile.3.row_off), custom_call_target="tpu_custom_call" | custom-call | flops 10000000 | bytes 1000000 | tf_op jit(solution)/shard_map/rows/pallas_call | solution.py:318
  22.9 7.0 %all-to-all-done.blocks = bf16[8,32,512]{2,1,0:T(8,128)(2,1)S(1)} async-done(((bf16[8,32,512]{2,1,0:T(8,128)(2,1)}), bf16[8,32,512]{2,1,0:T(8,128)(2,1)S(1)}, u32[]{:S(2)}, u32[]{:S(2)}) %all-to-all-start) | async-done | bytes 262176 | tf_op jit(solution)/shard_map/all_to_all | solution.py:492
  29.9 0.0 copy-done
  29.9 1.3 %place.1 = (bf16[1536,512]{1,0:T(8,128)(2,1)S(1)}, bf16[2,64,512]{2,1,0:T(8,128)(2,1)S(1)}) custom-call(bf16[8,32,512]{2,1,0:T(8,128)(2,1)S(1)} %all-to-all-done.blocks, s32[192,1]{1,0:T(8,128)S(1)} %broadcast_in_dim_squeeze.4.col_off, bf16[2,256,1536]{2,1,0:T(8,128)(2,1)S(1)} %rows.1, bf16[256,512]{1,0:T(8,128)(2,1)S(1)} %copy-done), custom_call_target="tpu_custom_call" | custom-call | tf_op jit(solution)/shard_map/place/pallas_call | solution.py:401
  31.2 0.1 collective-permute-start.2
  31.3 0.6 %keep.1 = f32[2,64,512]{2,1,0:T(8,128)S(1)} custom-call(bf16[2,256,1536]{2,1,0:T(8,128)(2,1)S(1)} %rows.1, bf16[1536,512]{1,0:T(8,128)(2,1)S(1)} %get-tuple-element.29.spread), custom_call_target="tpu_custom_call" | custom-call | flops 100000000 | bytes 1000000 | tf_op jit(solution)/shard_map/keep/pallas_call | solution.py:425
  31.8 0.8 %collective-permute-done.2 = bf16[2,64,512]{2,1,0:T(8,128)(2,1)S(1)} collective-permute-done((bf16[2,64,512]{2,1,0:T(8,128)(2,1)S(1)}, bf16[2,64,512]{2,1,0:T(8,128)(2,1)S(1)}, u32[]{:S(2)}, u32[]{:S(2)}) %collective-permute-start.2) | collective-permute-done | bytes 131104 | tf_op jit(solution)/shard_map/ppermute | solution.py:451
  32.6 1.6 %collective-permute-start.3 = (bf16[1,64,512]{2,1,0:T(8,128)(2,1)S(1)}, bf16[1,64,512]{2,1,0:T(8,128)(2,1)S(1)}, u32[]{:S(2)}, u32[]{:S(2)}) collective-permute-start(bf16[1,64,512]{2,1,0:T(8,128)(2,1)S(1)} %fusion), channel_id=1, source_target_pairs={{0,2},{1,3},{2,0},{3,1},{4,6},{5,7},{6,4},{7,5},{8,10},{9,11},{10,... | collective-permute-start | bytes 196616 | tf_op jit(solution)/shard_map/ppermute | solution.py:451
  34.2 2.7 %collective-permute-done.3 = bf16[1,64,512]{2,1,0:T(8,128)(2,1)S(1)} collective-permute-done((bf16[1,64,512]{2,1,0:T(8,128)(2,1)S(1)}, bf16[1,64,512]{2,1,0:T(8,128)(2,1)S(1)}, u32[]{:S(2)}, u32[]{:S(2)}) %collective-permute-start.3) | collective-permute-done | bytes 65568 | tf_op jit(solution)/shard_map/ppermute | solution.py:451
  37.0 0.7 %add.34 = f32[1,64,2,256]{3,2,1,0:T(2,128)} reshape(f32[1,64,512]{2,1,0:T(8,128)S(1)} %fusion.1) | data formatting | bytes 262144 | tf_op jit(solution)/shard_map/add | solution.py:496
  (8 shorter events, 0.1 us)
Async XLA Ops:
  0.0 15.3 %copy-start.5 = (s32[1024,2]{0,1:T(2,128)S(1)}, s32[1024,2]{0,1:T(2,128)}, u32[]{:S(2)}) copy-start(s32[1024,2]{0,1:T(2,128)} %param.13) | copy-start | bytes 24580
  0.0 21.3 %copy-start.2 = (s32[1024,1]{0,1:T(1,128)S(1)}, s32[1024,1]{0,1:T(1,128)}, u32[]{:S(2)}) copy-start(s32[1024,1]{0,1:T(1,128)} %param.12) | copy-start | bytes 12292
  5.8 1.7 %collective-permute-start = (bf16[2,128,4,128]{3,2,1,0:T(4,128)(2,1)S(1)}, bf16[2,128,4,128]{3,2,1,0:T(4,128)(2,1)S(1)}, u32[]{:S(2)}, u32[]{:S(2)}) collective-permute-start(bf16[2,128,4,128]{3,2,1,0:T(4,128)(2,1)S(1)} %get-tuple-element.19), channel_id=1, source_target_pairs={{0,1},{1,0},{2,3},{3,2},{4,5},{5,4},{6,7},{7,6},{8,9},{9,8},{10,11... | collective-permute-start | bytes 786440 | tf_op jit(solution)/shard_map/ppermute | solution.py:451
  7.6 6.8 %collective-permute-start.1 = (bf16[1,128,4,128]{3,2,1,0:T(4,128)(2,1)S(1)}, bf16[1,128,4,128]{3,2,1,0:T(4,128)(2,1)S(1)}, u32[]{:S(2)}, u32[]{:S(2)}) collective-permute-start(bf16[1,128,4,128]{3,2,1,0:T(4,128)(2,1)S(1)} %add_convert_fusion), channel_id=1, source_target_pairs={{0,2},{1,3},{2,0},{3,1},{4,6},{5,7},{6,4},{7,5},{8,10},{9,11},{10,... | collective-permute-start | bytes 393224 | tf_op jit(solution)/shard_map/ppermute | solution.py:451
  10.5 0.7 %copy-start.1 = (s32[1024,1]{0,1:T(1,128)S(1)}, s32[1024,1]{0,1:T(1,128)}, u32[]{:S(2)}) copy-start(s32[1024,1]{0,1:T(1,128)} %param.12) | copy-start | bytes 12292
  11.2 0.7 %copy-start.3 = (bf16[4,2,1024]{2,1,0:T(2,128)(2,1)S(1)}, bf16[4,2,1024]{2,1,0:T(2,128)(2,1)}, u32[]{:S(2)}) copy-start(bf16[4,2,1024]{2,1,0:T(2,128)(2,1)} %screens) | copy-start | bytes 49156
  11.9 0.7 %copy-start.4 = (s32[128,2]{0,1:T(2,128)S(1)}, s32[128,2]{0,1:T(2,128)}, u32[]{:S(2)}) copy-start(s32[128,2]{0,1:T(2,128)} %param.11) | copy-start | bytes 3076
  14.3 15.6 %copy-start = (bf16[256,512]{1,0:T(8,128)(2,1)S(1)}, bf16[256,512]{1,0:T(8,128)(2,1)}, u32[]{:S(2)}) copy-start(bf16[256,512]{1,0:T(8,128)(2,1)} %constant.15.weights) | copy-start | bytes 786436
  15.3 14.6 %all-to-all-start = ((bf16[8,32,512]{2,1,0:T(8,128)(2,1)}), bf16[8,32,512]{2,1,0:T(8,128)(2,1)S(1)}, u32[]{:S(2)}, u32[]{:S(2)}) async-start(bf16[8,32,512]{2,1,0:T(8,128)(2,1)} %send.1), calls=%async_computation | async-start | bytes 524288 | tf_op jit(solution)/shard_map/all_to_all | solution.py:492
  31.2 1.4 %collective-permute-start.2 = (bf16[2,64,512]{2,1,0:T(8,128)(2,1)S(1)}, bf16[2,64,512]{2,1,0:T(8,128)(2,1)S(1)}, u32[]{:S(2)}, u32[]{:S(2)}) collective-permute-start(bf16[2,64,512]{2,1,0:T(8,128)(2,1)S(1)} %get-tuple-element.30), channel_id=1, source_target_pairs={{0,1},{1,0},{2,3},{3,2},{4,5},{5,4},{6,7},{7,6},{8,9},{9,8},{10,11... | collective-permute-start | bytes 393224 | tf_op jit(solution)/shard_map/ppermute | solution.py:451
  32.6 4.3 %collective-permute-start.3 = (bf16[1,64,512]{2,1,0:T(8,128)(2,1)S(1)}, bf16[1,64,512]{2,1,0:T(8,128)(2,1)S(1)}, u32[]{:S(2)}, u32[]{:S(2)}) collective-permute-start(bf16[1,64,512]{2,1,0:T(8,128)(2,1)S(1)} %fusion), channel_id=1, source_target_pairs={{0,2},{1,3},{2,0},{3,1},{4,6},{5,7},{6,4},{7,5},{8,10},{9,11},{10,... | collective-permute-start | bytes 196616 | tf_op jit(solution)/shard_map/ppermute | solution.py:451

commit v7 on v6

--- a/solution.py
+++ b/solution.py
@@ -119,25 +119,28 @@
         return jnp.concatenate(lhs, 1), [jnp.concatenate(r, 1) for r in rhs]
 
     def products(keep, send, n, *refs):
-        s = 2 * n
-        (l0, r0), (l1, r1) = sides(2 * n, *refs), sides(2 * n + 1, *refs)
+        made = [sides(4 * n + j, *refs) for j in range(4)]
         out = lax.dot_general(
-            jnp.concatenate([l0, l1], 0),
-            jnp.concatenate(r0 + r1, 0),
+            jnp.concatenate([m[0] for m in made], 0),
+            jnp.concatenate(sum([m[1] for m in made], []), 0),
             (((1,), (1,)), ((), ())),
             preferred_element_type=jnp.float32,
         )
         group = max(1, 8 // Q)
-        for g in range(4):
-            x, y = out[8 * g : 8 * g + 8], out[SUB + 8 * g : SUB + 8 * g + 8]
-            x = jnp.where(low, x, pltpu.roll(pltpu.roll(x, 8 - Q2, 0), LANES // 2, 1)).astype(jnp.bfloat16)
-            y = jnp.where(low, pltpu.roll(y, LANES // 2, 1), pltpu.roll(y, 8 - Q2, 0)).astype(jnp.bfloat16)
-            for k in range(group):
-                d = g * group + k
-                place = bit_reverse(d // 2, T // 2)
-                ref = send if d % 2 else keep
-                ref[place, s] = x[k * Q : k * Q + Q2]
-                ref[place, s + 1] = y[k * Q : k * Q + Q2]
+        for j in range(4):
+            mine = out[SUB * j : SUB * (j + 1), LANES * (j // 2) : LANES * (j // 2 + 1)]
+            for g in range(4):
+                x = mine[8 * g : 8 * g + 8]
+                if j % 2:
+                    x = jnp.where(low, pltpu.roll(x, LANES // 2, 1), pltpu.roll(x, 8 - Q2, 0))
+                else:
+                    x = jnp.where(low, x, pltpu.roll(pltpu.roll(x, 8 - Q2, 0), LANES // 2, 1))
+                x = x.astype(jnp.bfloat16)
+                for k in range(group):
+                    d = g * group + k
+                    place = bit_reverse(d // 2, T // 2)
+                    ref = send if d % 2 else keep
+                    ref[place, 4 * n + j] = x[k * Q : k * Q + Q2]
 
     for copy in numbers:
         copy.wait()
@@ -156,7 +159,7 @@
 
     def use(i, side):
         at = pl.ds(i * G, G)
-        for n in range(G // 2):
+        for n in range(G // 4):
             products(keep.at[:, at], send.at[:, at], n, *sides_of[side])
 
     def step(j, carry):

time: 38 us -> 38 us (level)
  no operation moved by 1% of the time
where the time goes in v7:
time: 38 us; the launch traced here: 37.7 us
  waiting for transfers between devices  12.6 us (33%)
  starting transfers between devices  11.2 us (29%)
  Pallas kernels  9.92 us (26%)
  local copies, waits for them, and re-layouts  3.09 us (8%)
  other arithmetic  0.73 us (2%)
    all_to_all x1, waiting for transfers between devices, per_device(): lax.all_to_all(outgoing, 'base', split_axis=0, concat_axis=0, tiled=True)  6.96 us
    all_to_all x1, starting transfers between devices, per_device(): lax.all_to_all(outgoing, 'base', split_axis=0, concat_axis=0, tiled=True)  6.04 us
    pallas_call x1, Pallas kernels, images(): pl.pallas_call(functools.partial(images_kernel, T, L, G), out_shape=(half...  5.75 us
    ppermute x4, waiting for transfers between devices, halve(): swap = lambda x, d: lax.ppermute(x, 'tm', [(i, i ^ d) for i in range(T)])  5.68 us
    ppermute x4, starting transfers between devices, halve(): swap = lambda x, d: lax.ppermute(x, 'tm', [(i, i ^ d) for i in range(T)])  5.13 us
    unnamed x13, local copies, waits for them, and re-layouts  2.09 us
    pallas_call x1, Pallas kernels, place_blocks(): pl.pallas_call(functools.partial(place_kernel, T, B, cap, capx, held), ou...  1.32 us
    pallas_call x1, Pallas kernels, send_blocks(): pl.pallas_call(functools.partial(send_kernel, T, L, B, cap, capx), out_sh...  0.95 us
  transfers between devices with their start and end apart: 5, of which 5 were waited for; matrix products, arithmetic and copies ran while one was open for 2% of the time, Pallas kernels for 5%

profile of v7, /device:TPU:0, one launch (start us, length us, event | category | flops | bytes accessed | tf_op | source)
XLA Modules:
  0.0 37.7 jit_solution(9981362213092555120)
XLA Ops:
  0.0 0.0 copy-start.5
  0.0 0.0 copy-start.2
  0.0 5.8 %images.1 = (bf16[2,128,4,128]{3,2,1,0:T(4,128)(2,1)S(1)}, bf16[2,128,4,128]{3,2,1,0:T(4,128)(2,1)S(1)}) custom-call(s32[1,128]{1,0:T(1,128)} %in_counts.1, s32[2,1024]{1,0:T(2,128)} %bitcast.23, f32[512,128]{1,0:T(8,128)} %bitcast.21, bf16[512,128]{1,0:T(8,128)(2,1)} %bitcast.22), custom_call_target="tpu_custom_call" | custom-call | tf_op jit(solution)/shard_map/images/pallas_call | solution.py:187
  5.8 0.5 %collective-permute-start = (bf16[2,128,4,128]{3,2,1,0:T(4,128)(2,1)S(1)}, bf16[2,128,4,128]{3,2,1,0:T(4,128)(2,1)S(1)}, u32[]{:S(2)}, u32[]{:S(2)}) collective-permute-start(bf16[2,128,4,128]{3,2,1,0:T(4,128)(2,1)S(1)} %get-tuple-element.19), channel_id=1, source_target_pairs={{0,1},{1,0},{2,3},{3,2},{4,5},{5,4},{6,7},{7,6},{8,9},{9,8},{10,11... | collective-permute-start | bytes 786440 | tf_op jit(solution)/shard_map/ppermute | solution.py:454
  6.3 1.2 %collective-permute-done.second = bf16[2,128,4,128]{3,2,1,0:T(4,128)(2,1)S(1)} collective-permute-done((bf16[2,128,4,128]{3,2,1,0:T(4,128)(2,1)S(1)}, bf16[2,128,4,128]{3,2,1,0:T(4,128)(2,1)S(1)}, u32[]{:S(2)}, u32[]{:S(2)}) %collective-permute-start) | collective-permute-done | bytes 262176 | tf_op jit(solution)/shard_map/ppermute | solution.py:454
  7.4 0.1 add_convert_fusion
  7.5 3.0 %collective-permute-start.1 = (bf16[1,128,4,128]{3,2,1,0:T(4,128)(2,1)S(1)}, bf16[1,128,4,128]{3,2,1,0:T(4,128)(2,1)S(1)}, u32[]{:S(2)}, u32[]{:S(2)}) collective-permute-start(bf16[1,128,4,128]{3,2,1,0:T(4,128)(2,1)S(1)} %add_convert_fusion), channel_id=1, source_target_pairs={{0,2},{1,3},{2,0},{3,1},{4,6},{5,7},{6,4},{7,5},{8,10},{9,11},{10,... | collective-permute-start | bytes 393224 | tf_op jit(solution)/shard_map/ppermute | solution.py:454
  10.5 0.0 copy-start.1
  10.5 0.7 %copy-done.1 = s32[1024,1]{0,1:T(1,128)S(1)} copy-done((s32[1024,1]{0,1:T(1,128)S(1)}, s32[1024,1]{0,1:T(1,128)}, u32[]{:S(2)}) %copy-start.1) | copy-done | bytes 4120
  11.2 0.0 copy-start.3
  11.2 0.7 %copy-done.3 = bf16[4,2,1024]{2,1,0:T(2,128)(2,1)S(1)} copy-done((bf16[4,2,1024]{2,1,0:T(2,128)(2,1)S(1)}, bf16[4,2,1024]{2,1,0:T(2,128)(2,1)}, u32[]{:S(2)}) %copy-start.3) | copy-done | bytes 16408
  11.9 0.0 copy-start.4
  11.9 0.7 %copy-done.4 = s32[128,2]{0,1:T(2,128)S(1)} copy-done((s32[128,2]{0,1:T(2,128)S(1)}, s32[128,2]{0,1:T(2,128)}, u32[]{:S(2)}) %copy-start.4) | copy-done | bytes 1048
  12.6 0.7 %index.1 = (bf16[256,128]{1,0:T(8,128)(2,1)S(1)}, f32[256,512]{1,0:T(8,128)S(1)}) custom-call(s32[8,128]{1,0:T(8,128)S(1)} %bitcast.19, s32[2,128]{1,0:T(2,128)S(1)} %bitcast.20, bf16[4,2,1024]{2,1,0:T(2,128)(2,1)S(1)} %copy-done.3, bf16[2,128,4,128]{3,2,1,0:T(4,128)(2,1)S(1)} %get-tuple-element.18.first, ...), custom_call_target="tpu_custom_call" | custom-call | flops 10000000 | bytes 1000000 | tf_op jit(solution)/shard_map/index/pallas_call | solution.py:248
  13.3 1.0 %collective-permute-done.1.refs_0_ = bf16[1,128,4,128]{3,2,1,0:T(4,128)(2,1)S(1)} collective-permute-done((bf16[1,128,4,128]{3,2,1,0:T(4,128)(2,1)S(1)}, bf16[1,128,4,128]{3,2,1,0:T(4,128)(2,1)S(1)}, u32[]{:S(2)}, u32[]{:S(2)}) %collective-permute-start.1) | collective-permute-done | bytes 131104 | tf_op jit(solution)/shard_map/ppermute | solution.py:454
  14.3 0.0 copy-start
  14.3 1.0 %send.1 = bf16[8,32,512]{2,1,0:T(8,128)(2,1)} custom-call(bf16[1,128,4,128]{3,2,1,0:T(4,128)(2,1)S(1)} %collective-permute-done.1.refs_0_, bf16[256,128]{1,0:T(8,128)(2,1)S(1)} %get-tuple-element.24.refs_1_, f32[256,512]{1,0:T(8,128)S(1)} %get-tuple-element.25.refs_2_), custom_call_target="tpu_custom_call" | custom-call | tf_op jit(solution)/shard_map/send/pallas_call | solution.py:286
  15.2 0.0 copy-done.5
  15.3 6.0 %all-to-all-start = ((bf16[8,32,512]{2,1,0:T(8,128)(2,1)}), bf16[8,32,512]{2,1,0:T(8,128)(2,1)S(1)}, u32[]{:S(2)}, u32[]{:S(2)}) async-start(bf16[8,32,512]{2,1,0:T(8,128)(2,1)} %send.1), calls=%async_computation | async-start | bytes 524288 | tf_op jit(solution)/shard_map/all_to_all | solution.py:495
  21.3 0.0 copy-done.2
  21.3 0.2 convert_reduce_fusion
  21.6 0.3 select_reduce_fusion
  21.9 0.1 tile.7
  22.0 0.1 broadcast_in_dim_tile.3.row_off
  22.1 0.1 broadcast_in_dim_squeeze.4.col_off
  22.2 0.6 %rows.1 = bf16[2,256,1536]{2,1,0:T(8,128)(2,1)S(1)} custom-call(s32[1,1536]{1,0:T(1,128)S(1)} %broadcast_in_dim_tile.3.row_off), custom_call_target="tpu_custom_call" | custom-call | flops 10000000 | bytes 1000000 | tf_op jit(solution)/shard_map/rows/pallas_call | solution.py:321
  22.9 7.0 %all-to-all-done.blocks = bf16[8,32,512]{2,1,0:T(8,128)(2,1)S(1)} async-done(((bf16[8,32,512]{2,1,0:T(8,128)(2,1)}), bf16[8,32,512]{2,1,0:T(8,128)(2,1)S(1)}, u32[]{:S(2)}, u32[]{:S(2)}) %all-to-all-start) | async-done | bytes 262176 | tf_op jit(solution)/shard_map/all_to_all | solution.py:495
  29.8 0.0 copy-done
  29.8 1.3 %place.1 = (bf16[1536,512]{1,0:T(8,128)(2,1)S(1)}, bf16[2,64,512]{2,1,0:T(8,128)(2,1)S(1)}) custom-call(bf16[8,32,512]{2,1,0:T(8,128)(2,1)S(1)} %all-to-all-done.blocks, s32[192,1]{1,0:T(8,128)S(1)} %broadcast_in_dim_squeeze.4.col_off, bf16[2,256,1536]{2,1,0:T(8,128)(2,1)S(1)} %rows.1, bf16[256,512]{1,0:T(8,128)(2,1)S(1)} %copy-done), custom_call_target="tpu_custom_call" | custom-call | tf_op jit(solution)/shard_map/place/pallas_call | solution.py:404
  31.2 0.1 collective-permute-start.2
  31.2 0.6 %keep.1 = f32[2,64,512]{2,1,0:T(8,128)S(1)} custom-call(bf16[2,256,1536]{2,1,0:T(8,128)(2,1)S(1)} %rows.1, bf16[1536,512]{1,0:T(8,128)(2,1)S(1)} %get-tuple-element.29.spread), custom_call_target="tpu_custom_call" | custom-call | flops 100000000 | bytes 1000000 | tf_op jit(solution)/shard_map/keep/pallas_call | solution.py:428
  31.8 0.8 %collective-permute-done.2 = bf16[2,64,512]{2,1,0:T(8,128)(2,1)S(1)} collective-permute-done((bf16[2,64,512]{2,1,0:T(8,128)(2,1)S(1)}, bf16[2,64,512]{2,1,0:T(8,128)(2,1)S(1)}, u32[]{:S(2)}, u32[]{:S(2)}) %collective-permute-start.2) | collective-permute-done | bytes 131104 | tf_op jit(solution)/shard_map/ppermute | solution.py:454
  32.6 1.6 %collective-permute-start.3 = (bf16[1,64,512]{2,1,0:T(8,128)(2,1)S(1)}, bf16[1,64,512]{2,1,0:T(8,128)(2,1)S(1)}, u32[]{:S(2)}, u32[]{:S(2)}) collective-permute-start(bf16[1,64,512]{2,1,0:T(8,128)(2,1)S(1)} %fusion), channel_id=1, source_target_pairs={{0,2},{1,3},{2,0},{3,1},{4,6},{5,7},{6,4},{7,5},{8,10},{9,11},{10,... | collective-permute-start | bytes 196616 | tf_op jit(solution)/shard_map/ppermute | solution.py:454
  34.2 2.7 %collective-permute-done.3 = bf16[1,64,512]{2,1,0:T(8,128)(2,1)S(1)} collective-permute-done((bf16[1,64,512]{2,1,0:T(8,128)(2,1)S(1)}, bf16[1,64,512]{2,1,0:T(8,128)(2,1)S(1)}, u32[]{:S(2)}, u32[]{:S(2)}) %collective-permute-start.3) | collective-permute-done | bytes 65568 | tf_op jit(solution)/shard_map/ppermute | solution.py:454
  36.9 0.7 %add.34 = f32[1,64,2,256]{3,2,1,0:T(2,128)} reshape(f32[1,64,512]{2,1,0:T(8,128)S(1)} %fusion.1) | data formatting | bytes 262144 | tf_op jit(solution)/shard_map/add | solution.py:499
  (8 shorter events, 0.1 us)
Async XLA Ops:
  0.0 15.2 %copy-start.5 = (s32[1024,2]{0,1:T(2,128)S(1)}, s32[1024,2]{0,1:T(2,128)}, u32[]{:S(2)}) copy-start(s32[1024,2]{0,1:T(2,128)} %param.13) | copy-start | bytes 24580
  0.0 21.3 %copy-start.2 = (s32[1024,1]{0,1:T(1,128)S(1)}, s32[1024,1]{0,1:T(1,128)}, u32[]{:S(2)}) copy-start(s32[1024,1]{0,1:T(1,128)} %param.12) | copy-start | bytes 12292
  5.8 1.7 %collective-permute-start = (bf16[2,128,4,128]{3,2,1,0:T(4,128)(2,1)S(1)}, bf16[2,128,4,128]{3,2,1,0:T(4,128)(2,1)S(1)}, u32[]{:S(2)}, u32[]{:S(2)}) collective-permute-start(bf16[2,128,4,128]{3,2,1,0:T(4,128)(2,1)S(1)} %get-tuple-element.19), channel_id=1, source_target_pairs={{0,1},{1,0},{2,3},{3,2},{4,5},{5,4},{6,7},{7,6},{8,9},{9,8},{10,11... | collective-permute-start | bytes 786440 | tf_op jit(solution)/shard_map/ppermute | solution.py:454
  7.5 6.8 %collective-permute-start.1 = (bf16[1,128,4,128]{3,2,1,0:T(4,128)(2,1)S(1)}, bf16[1,128,4,128]{3,2,1,0:T(4,128)(2,1)S(1)}, u32[]{:S(2)}, u32[]{:S(2)}) collective-permute-start(bf16[1,128,4,128]{3,2,1,0:T(4,128)(2,1)S(1)} %add_convert_fusion), channel_id=1, source_target_pairs={{0,2},{1,3},{2,0},{3,1},{4,6},{5,7},{6,4},{7,5},{8,10},{9,11},{10,... | collective-permute-start | bytes 393224 | tf_op jit(solution)/shard_map/ppermute | solution.py:454
  10.5 0.7 %copy-start.1 = (s32[1024,1]{0,1:T(1,128)S(1)}, s32[1024,1]{0,1:T(1,128)}, u32[]{:S(2)}) copy-start(s32[1024,1]{0,1:T(1,128)} %param.12) | copy-start | bytes 12292
  11.2 0.7 %copy-start.3 = (bf16[4,2,1024]{2,1,0:T(2,128)(2,1)S(1)}, bf16[4,2,1024]{2,1,0:T(2,128)(2,1)}, u32[]{:S(2)}) copy-start(bf16[4,2,1024]{2,1,0:T(2,128)(2,1)} %screens) | copy-start | bytes 49156
  11.9 0.7 %copy-start.4 = (s32[128,2]{0,1:T(2,128)S(1)}, s32[128,2]{0,1:T(2,128)}, u32[]{:S(2)}) copy-start(s32[128,2]{0,1:T(2,128)} %param.11) | copy-start | bytes 3076
  14.3 15.6 %copy-start = (bf16[256,512]{1,0:T(8,128)(2,1)S(1)}, bf16[256,512]{1,0:T(8,128)(2,1)}, u32[]{:S(2)}) copy-start(bf16[256,512]{1,0:T(8,128)(2,1)} %constant.15.weights) | copy-start | bytes 786436
  15.3 14.6 %all-to-all-start = ((bf16[8,32,512]{2,1,0:T(8,128)(2,1)}), bf16[8,32,512]{2,1,0:T(8,128)(2,1)S(1)}, u32[]{:S(2)}, u32[]{:S(2)}) async-start(bf16[8,32,512]{2,1,0:T(8,128)(2,1)} %send.1), calls=%async_computation | async-start | bytes 524288 | tf_op jit(solution)/shard_map/all_to_all | solution.py:495
  31.2 1.4 %collective-permute-start.2 = (bf16[2,64,512]{2,1,0:T(8,128)(2,1)S(1)}, bf16[2,64,512]{2,1,0:T(8,128)(2,1)S(1)}, u32[]{:S(2)}, u32[]{:S(2)}) collective-permute-start(bf16[2,64,512]{2,1,0:T(8,128)(2,1)S(1)} %get-tuple-element.30), channel_id=1, source_target_pairs={{0,1},{1,0},{2,3},{3,2},{4,5},{5,4},{6,7},{7,6},{8,9},{9,8},{10,11... | collective-permute-start | bytes 393224 | tf_op jit(solution)/shard_map/ppermute | solution.py:454
  32.6 4.3 %collective-permute-start.3 = (bf16[1,64,512]{2,1,0:T(8,128)(2,1)S(1)}, bf16[1,64,512]{2,1,0:T(8,128)(2,1)S(1)}, u32[]{:S(2)}, u32[]{:S(2)}) collective-permute-start(bf16[1,64,512]{2,1,0:T(8,128)(2,1)S(1)} %fusion), channel_id=1, source_target_pairs={{0,2},{1,3},{2,0},{3,1},{4,6},{5,7},{6,4},{7,5},{8,10},{9,11},{10,... | collective-permute-start | bytes 196616 | tf_op jit(solution)/shard_map/ppermute | solution.py:454
